TPU v7x, 32 devices: a whole 2x2x4 slice. The times are simulated.
32 devices in a mesh: dp: 16 (over z, x, core), seq: 2 (over y).
Axes of the slice: x: 2, y: 2, z: 4, core: 2. Of those that a mesh axis runs over, the one named last changes fastest.
Arguments:
- queries: bfloat16 [16, 256, 1024], P('dp', 'seq'), may hold values from -6 to 6
- keys: bfloat16 [16, 256, 1024], P('dp', 'seq'), may hold values from -6 to 6
- values: bfloat16 [16, 256, 1024], P('dp', 'seq'), may hold values from -6 to 6
- stream: bfloat16 [16, 256, 1024], P('dp', 'seq'), may hold values from -6 to 6
- cotangent: bfloat16 [16, 256, 1024], P('dp', 'seq'), may hold values from -6 to 6
- attn_out: bfloat16 [1024, 1024], replicated, may hold values from -0.1875 to 0.1875
- point_in: bfloat16 [1024, 2048], replicated, may hold values from -0.1875 to 0.1875
- kernel: bfloat16 [31, 1024], replicated, may hold values from -1 to 1
- point_out: bfloat16 [1024, 1024], replicated, may hold values from -0.1875 to 0.1875
- norm_gain: float32 [1024], replicated, may hold values from 0.1 to 1.9
- conv_gain: float32 [1024], replicated, may hold values from 0.1 to 1.9
- segments: int32 [16, 256], replicated, may hold values from 0 to 127, as said below
- plan: int32 [16], replicated, may hold values from 0 to 15, as said below
Outputs:
- query_grad: bfloat16 [16, 256, 1024], P('dp', 'seq')
- key_grad: bfloat16 [16, 256, 1024], P('dp', 'seq')
- value_grad: bfloat16 [16, 256, 1024], P('dp', 'seq')
- stream_grad: bfloat16 [16, 256, 1024], P('dp', 'seq')
- kernel_grad: float32 [31, 1024], replicated
- proj_grads: float32 [1024, 2048], P(('dp', 'seq'))
Inputs may be any that keep to these rules, and one draw needn't show every extreme that they name: `segments`: along each pack the numbers never fall and change only at even frames; one number marks one utterance. `plan`: A permutation of 0 to 15.
All inputs are finite; a program needn't handle non-finite values.
Results may differ from a plain program's by a relative error of at most 0.024.
Values may be sent and summed in bfloat16 or wider, within the bound.
A program may use at most 128 MiB of HBM per device.

v0:
```python
import math

import jax
import jax.numpy as jnp
from jax import lax
from jax.sharding import PartitionSpec as P

HEAD_DIM = 64


EPSILON = 1e-05
MASKED = -1e30


def extended(cells, sides, width):
    for axis, dim in sides:
        count = lax.axis_size(axis)
        ends = count - 1
        head = lax.slice_in_dim(cells, 0, width, axis=dim)
        tail = lax.slice_in_dim(cells, cells.shape[dim] - width, cells.shape[dim], axis=dim)
        cells = jnp.concatenate(
            [
                lax.ppermute(tail, axis, [(i, (i + 1) % count) for i in range(ends)]),
                cells,
                lax.ppermute(head, axis, [((i + 1) % count, i) for i in range(ends)]),
            ],
            axis=dim,
        )
    return cells


def layer_norm(stream, gain):
    center = jnp.mean(stream, -1, keepdims=True)
    shifted = stream - center
    inverse = lax.rsqrt(jnp.mean(shifted * shifted, -1, keepdims=True) + EPSILON)
    normed = shifted * inverse
    return (normed * gain, normed, inverse)


def norm_backward(upstream, normed, inverse, gain):
    scaled = upstream * gain
    return inverse * (
        scaled
        - jnp.mean(scaled, -1, keepdims=True)
        - normed * jnp.mean(scaled * normed, -1, keepdims=True)
    )


def swish_slope(values):
    logistic = jax.nn.sigmoid(values)
    return logistic * (1.0 + values * (1.0 - logistic))


def tap_table(padded_ids, own_ids, taps):
    length = own_ids.shape[0]
    return (
        jnp.stack([padded_ids[tap : tap + length] for tap in range(taps)], 1) == own_ids[:, None]
    ).astype(jnp.float32)


def depthwise(padded, weights, table):
    length = table.shape[0]
    total = jnp.zeros((length, padded.shape[1]), jnp.float32)
    for tap in range(weights.shape[0]):
        total = (
            total
            + weights[tap].astype(jnp.float32)
            * padded[tap : tap + length].astype(jnp.float32)
            * table[:, tap : tap + 1]
        )
    return total


def tap_sums(upstream, padded, table):
    length = table.shape[0]
    return jnp.stack(
        [
            jnp.sum(
                upstream * padded[tap : tap + length].astype(jnp.float32) * table[:, tap : tap + 1],
                0,
            )
            for tap in range(table.shape[1])
        ]
    )


def times_transposed(left, right):
    return lax.dot_general(
        left, right, (((1,), (1,)), ((), ())), preferred_element_type=jnp.float32
    )


def transposed_times(left, right):
    return lax.dot_general(
        left, right, (((0,), (0,)), ((), ())), preferred_element_type=jnp.float32
    )


def split_heads(matrix):
    return matrix.reshape(matrix.shape[0], -1, HEAD_DIM).transpose(1, 0, 2)


def merge_heads(tensor):
    return tensor.transpose(1, 0, 2).reshape(tensor.shape[1], -1)


def tiling(length, heads):
    block_rows = min(length, 512)
    per_group = max(1, min(heads, 1024 // block_rows))
    return (block_rows, per_group)


def to_blocks(tensor, per_group, block_rows):
    heads, length, depth = tensor.shape
    groups, blocks = (heads // per_group, length // block_rows)
    return (
        tensor.reshape(groups, per_group, blocks, block_rows, depth)
        .transpose(0, 2, 1, 3, 4)
        .reshape(groups * blocks, per_group, block_rows, depth)
    )


def from_blocks(tensor, groups):
    total, per_group, block_rows, depth = tensor.shape
    blocks = total // groups
    return (
        tensor.reshape(groups, blocks, per_group, block_rows, depth)
        .transpose(0, 2, 1, 3, 4)
        .reshape(groups * per_group, blocks * block_rows, depth)
    )


def masked_scores(query_block, key_group, query_ids, key_ids):
    scores = jnp.einsum(
        "hqe,hke->hqk", query_block, key_group, preferred_element_type=jnp.float32
    ) * HEAD_DIM ** (-0.5)
    return jnp.where((query_ids[:, None] == key_ids[None, :])[None], scores, MASKED)


def attend(queries, keys, values, query_ids, key_ids):
    query_heads = split_heads(queries)
    heads, length = (query_heads.shape[0], query_heads.shape[1])
    block_rows, per_group = tiling(length, heads)
    groups, blocks = (heads // per_group, length // block_rows)
    query_blocks = to_blocks(query_heads, per_group, block_rows)
    key_groups = split_heads(keys).reshape(groups, per_group, keys.shape[0], HEAD_DIM)
    value_groups = split_heads(values).reshape(groups, per_group, values.shape[0], HEAD_DIM)
    id_blocks = query_ids.reshape(blocks, block_rows)

    def one_block(position):
        which = position // blocks
        scores = masked_scores(
            query_blocks[position], key_groups[which], id_blocks[position % blocks], key_ids
        )
        highest = jnp.max(scores, -1, keepdims=True)
        log_total = highest + jnp.log(jnp.sum(jnp.exp(scores - highest), -1, keepdims=True))
        weights = jnp.exp(scores - log_total)
        mixed = jnp.einsum(
            "hqk,hke->hqe",
            weights.astype(jnp.bfloat16),
            value_groups[which],
            preferred_element_type=jnp.float32,
        )
        return (mixed.astype(jnp.bfloat16), weights, log_total)

    mixed, weights, log_total = lax.map(one_block, jnp.arange(groups * blocks))
    return (
        merge_heads(from_blocks(mixed, groups)),
        weights,
        from_blocks(log_total, groups)[:, :, 0].T,
    )


def attend_backward(queries, upstream, keys, values, weights):
    query_heads = split_heads(queries)
    heads, length = (query_heads.shape[0], query_heads.shape[1])
    block_rows, per_group = tiling(length, heads)
    groups, blocks = (heads // per_group, length // block_rows)
    grad_blocks = to_blocks(split_heads(upstream), per_group, block_rows)
    key_count = keys.shape[0]
    key_groups = split_heads(keys).reshape(groups, per_group, key_count, HEAD_DIM)
    value_groups = split_heads(values).reshape(groups, per_group, key_count, HEAD_DIM)
    scale = HEAD_DIM ** (-0.5)

    def one_block(totals, position):
        which = position // blocks
        weight_block = weights[position]
        slope = jnp.einsum(
            "hqe,hke->hqk",
            grad_blocks[position],
            value_groups[which],
            preferred_element_type=jnp.float32,
        )
        delta = jnp.sum(weight_block * slope, -1, keepdims=True)
        score_grad = (weight_block * (slope - delta)).astype(jnp.bfloat16)
        query_part = (
            jnp.einsum(
                "hqk,hke->hqe", score_grad, key_groups[which], preferred_element_type=jnp.float32
            )
            * scale
        ).astype(jnp.bfloat16)
        return (totals, (query_part, delta))

    start_totals = ()
    totals, outputs = lax.scan(one_block, start_totals, jnp.arange(groups * blocks))
    query_grad = merge_heads(from_blocks(outputs[0], groups))
    delta = from_blocks(outputs[1], groups)[:, :, 0].T
    return (query_grad, delta, query_grad, query_grad)


def per_device(
    queries,
    keys,
    values,
    stream,
    cotangent,
    attn_out,
    point_in,
    kernel,
    point_out,
    norm_gain,
    conv_gain,
    segments,
    plan,
):
    frames, width = (queries.shape[1], queries.shape[2])
    seq_place = lax.axis_index("seq")
    spread = (
        lax.all_to_all(queries[0], "dp", split_axis=0, concat_axis=0, tiled=True),
        lax.all_to_all(keys[0], "dp", split_axis=0, concat_axis=0, tiled=True),
        lax.all_to_all(values[0], "dp", split_axis=0, concat_axis=0, tiled=True),
        lax.all_to_all(stream[0], "dp", split_axis=0, concat_axis=0, tiled=True),
        lax.all_to_all(cotangent[0], "dp", split_axis=0, concat_axis=0, tiled=True),
    )

    def reorder(matrix):
        return jnp.take(matrix.reshape(plan.shape[0], -1, width), plan, axis=0).reshape(
            frames, width
        )

    arranged = [reorder(matrix) for matrix in spread]
    query_rows, key_rows, value_rows, stream_rows, grad_rows = (
        lax.all_to_all(arranged[0], "dp", split_axis=0, concat_axis=0, tiled=True),
        lax.all_to_all(arranged[1], "dp", split_axis=0, concat_axis=0, tiled=True),
        lax.all_to_all(arranged[2], "dp", split_axis=0, concat_axis=0, tiled=True),
        lax.all_to_all(arranged[3], "dp", split_axis=0, concat_axis=0, tiled=True),
        lax.all_to_all(arranged[4], "dp", split_axis=0, concat_axis=0, tiled=True),
    )
    source = plan[lax.axis_index("dp")]
    pack_ids = lax.dynamic_index_in_dim(segments, source, 0, keepdims=False)
    own_ids = lax.dynamic_slice_in_dim(pack_ids, seq_place * frames, frames)
    key_all, value_all = (
        lax.all_gather(key_rows, "seq", axis=0, tiled=True),
        lax.all_gather(value_rows, "seq", axis=0, tiled=True),
    )
    mixed, weights, log_totals = attend(query_rows, key_all, value_all, own_ids, pack_ids)
    hidden = stream_rows.astype(jnp.float32) + jnp.dot(
        mixed, attn_out, preferred_element_type=jnp.float32
    )
    normed_in, hat_in, inv_in = layer_norm(hidden, norm_gain)
    both = jnp.dot(normed_in.astype(jnp.bfloat16), point_in, preferred_element_type=jnp.float32)
    linear = both[:, :width]
    logistic = jax.nn.sigmoid(both[:, width:])
    conv_in = (linear * logistic).astype(jnp.bfloat16)
    taps = kernel.shape[0]
    reach = taps // 2
    padded = extended(conv_in, (("seq", 0),), reach)
    padded_ids = lax.dynamic_slice_in_dim(
        jnp.pad(pack_ids, reach, constant_values=-1), seq_place * frames, frames + 2 * reach
    )
    table = tap_table(padded_ids, own_ids, taps)
    conv_out = depthwise(padded, kernel, table)
    normed_out, hat_out, inv_out = layer_norm(conv_out, conv_gain)
    activated = (normed_out * jax.nn.sigmoid(normed_out)).astype(jnp.bfloat16)
    act_grad = times_transposed(grad_rows, point_out)
    conv_grad = norm_backward(act_grad * swish_slope(normed_out), hat_out, inv_out, conv_gain)
    grad_padded = extended(conv_grad.astype(jnp.bfloat16), (("seq", 0),), reach).astype(
        conv_grad.dtype
    )
    kernel_grad = lax.psum(tap_sums(conv_grad, padded, table), ("dp", "seq"))
    in_grad = depthwise(grad_padded, kernel[::-1], table)
    both_grad = jnp.concatenate(
        [in_grad * logistic, in_grad * linear * logistic * (1.0 - logistic)], 1
    ).astype(jnp.bfloat16)
    back_in = times_transposed(both_grad, point_in)
    stream_out = (
        grad_rows.astype(jnp.float32) + norm_backward(back_in, hat_in, inv_in, norm_gain)
    ).astype(jnp.bfloat16)
    mixed_grad = times_transposed(stream_out, attn_out).astype(jnp.bfloat16)
    proj_grads = lax.psum_scatter(
        jnp.concatenate(
            [transposed_times(mixed, stream_out), transposed_times(activated, grad_rows)], 1
        ),
        ("dp", "seq"),
        scatter_dimension=0,
        tiled=True,
    )
    query_grad, deltas, unused_keys, unused_values = attend_backward(
        query_rows, mixed_grad, key_all, value_all, weights
    )
    totals_all, deltas_all = (
        lax.all_gather(log_totals, "seq", axis=0, tiled=True),
        lax.all_gather(deltas, "seq", axis=0, tiled=True),
    )
    own_key_heads = split_heads(key_rows)
    own_value_heads = split_heads(value_rows)
    scale = HEAD_DIM ** (-0.5)
    empty = jnp.zeros((width // HEAD_DIM, frames, HEAD_DIM), jnp.float32)
    query_piece = lax.all_gather(query_rows, "seq", axis=0, tiled=True)
    grad_piece = lax.all_gather(mixed_grad, "seq", axis=0, tiled=True)
    amount = query_piece.shape[0]
    stride = math.gcd(amount, 512)
    piece_queries = split_heads(query_piece)
    piece_grads = split_heads(grad_piece)

    def inner(position, accum):
        first = position * stride
        query_block = lax.dynamic_slice_in_dim(piece_queries, first, stride, 1)
        grad_block = lax.dynamic_slice_in_dim(piece_grads, first, stride, 1)
        total_block = lax.dynamic_slice_in_dim(totals_all, first, stride, 0).T
        delta_block = lax.dynamic_slice_in_dim(deltas_all, first, stride, 0).T
        block_ids = lax.dynamic_slice_in_dim(pack_ids, first, stride)
        scores = masked_scores(query_block, own_key_heads, block_ids, own_ids)
        weight_block = jnp.exp(scores - total_block[..., None])
        slope = jnp.einsum(
            "hqe,hke->hqk", grad_block, own_value_heads, preferred_element_type=jnp.float32
        )
        score_grad = (weight_block * (slope - delta_block[..., None])).astype(jnp.bfloat16)
        key_add = (
            jnp.einsum("hqk,hqe->hke", score_grad, query_block, preferred_element_type=jnp.float32)
            * scale
        )
        value_add = jnp.einsum(
            "hqk,hqe->hke",
            weight_block.astype(jnp.bfloat16),
            grad_block,
            preferred_element_type=jnp.float32,
        )
        return (accum[0] + key_add, accum[1] + value_add)

    key_total, value_total = lax.fori_loop(0, amount // stride, inner, (empty, empty))
    key_grad = merge_heads(key_total).astype(jnp.bfloat16)
    value_grad = merge_heads(value_total).astype(jnp.bfloat16)
    return (
        query_grad[None],
        key_grad[None],
        value_grad[None],
        stream_out[None],
        kernel_grad,
        proj_grads,
    )


def solution(mesh):
    placed = (
        P("dp", "seq", None),
        P("dp", "seq", None),
        P("dp", "seq", None),
        P("dp", "seq", None),
        P("dp", "seq", None),
        P(),
        P(),
        P(),
        P(),
        P(),
        P(),
        P(),
        P(),
    )
    return jax.shard_map(
        per_device,
        mesh=mesh,
        in_specs=placed,
        out_specs=(
            P("dp", "seq", None),
            P("dp", "seq", None),
            P("dp", "seq", None),
            P("dp", "seq", None),
            P(),
            P(("dp", "seq"), None),
        ),
        check_vma=False,
    )
```

profile of v0, /device:TPU:0, one launch (start us, length us, event | category | flops | bytes accessed | tf_op | source)
XLA Modules:
  0.0 518.7 jit_solution(8317517646542661471)
XLA Ops:
  7.2 17.5 %all_to_all.87 = bf16[16,8,1024]{2,1,0:T(8,128)(2,1)S(1)} all-to-all(bf16[16,8,1024]{2,1,0:T(8,128)(2,1)} %bitcast.379), channel_id=1, replica_groups=mesh['dp'=16,'seq'=2] {'dp'}, dimensions={0} | all-to-all | bytes 524288 | tf_op jit(solution)/shard_map/all_to_all | solution.py:229
  24.7 13.5 %all_to_all.88 = bf16[16,8,1024]{2,1,0:T(8,128)(2,1)S(1)} all-to-all(bf16[16,8,1024]{2,1,0:T(8,128)(2,1)} %bitcast.380), channel_id=1, replica_groups=mesh['dp'=16,'seq'=2] {'dp'}, dimensions={0} | all-to-all | bytes 524288 | tf_op jit(solution)/shard_map/all_to_all | solution.py:230
  38.2 13.5 %all_to_all.89 = bf16[16,8,1024]{2,1,0:T(8,128)(2,1)S(1)} all-to-all(bf16[16,8,1024]{2,1,0:T(8,128)(2,1)} %bitcast.381), channel_id=1, replica_groups=mesh['dp'=16,'seq'=2] {'dp'}, dimensions={0} | all-to-all | bytes 524288 | tf_op jit(solution)/shard_map/all_to_all | solution.py:231
  51.7 13.5 %all_to_all.90 = bf16[16,8,1024]{2,1,0:T(8,128)(2,1)S(1)} all-to-all(bf16[16,8,1024]{2,1,0:T(8,128)(2,1)} %bitcast.382), channel_id=1, replica_groups=mesh['dp'=16,'seq'=2] {'dp'}, dimensions={0} | all-to-all | bytes 524288 | tf_op jit(solution)/shard_map/all_to_all | solution.py:232
  85.3 9.7 %all-to-all-done.5 = bf16[16,8,1024]{2,1,0:T(8,128)(2,1)S(1)} async-done(((bf16[16,8,1024]{2,1,0:T(8,128)(2,1)}), bf16[16,8,1024]{2,1,0:T(8,128)(2,1)S(1)}, u32[]{:S(2)}, u32[]{:S(2)}) %all-to-all-start.5) | async-done | bytes 262176 | tf_op jit(solution)/shard_map/all_to_all | solution.py:245
  100.8 7.7 %all-to-all-done.1 = bf16[16,8,1024]{2,1,0:T(8,128)(2,1)S(1)} async-done(((bf16[16,8,1024]{2,1,0:T(8,128)(2,1)}), bf16[16,8,1024]{2,1,0:T(8,128)(2,1)S(1)}, u32[]{:S(2)}, u32[]{:S(2)}) %all-to-all-start.1) | async-done | bytes 262176 | tf_op jit(solution)/shard_map/all_to_all | solution.py:243
  116.1 9.3 %all_gather.19 = bf16[256,1024]{1,0:T(8,128)(2,1)} all-gather(bf16[128,1024]{1,0:T(8,128)(2,1)S(1)} %bitcast.367), channel_id=1, replica_groups=mesh['dp'=16,'seq'=2] {'seq'}, dimensions={0}, use_global_device_ids=true | all-gather | bytes 786432 | tf_op jit(solution)/shard_map/all_gather | solution.py:254
  126.6 5.9 %all-to-all-start.9 = ((bf16[16,8,1024]{2,1,0:T(8,128)(2,1)}), bf16[16,8,1024]{2,1,0:T(8,128)(2,1)}, u32[]{:S(2)}, u32[]{:S(2)}) async-start(bf16[16,8,1024]{2,1,0:T(8,128)(2,1)} %get-tuple-element.518), calls=%async_computation.9 | async-start | bytes 524288 | tf_op jit(solution)/shard_map/all_to_all | solution.py:246
  132.5 9.3 %all_gather.18 = bf16[256,1024]{1,0:T(8,128)(2,1)} all-gather(bf16[128,1024]{1,0:T(8,128)(2,1)S(1)} %bitcast.369), channel_id=1, replica_groups=mesh['dp'=16,'seq'=2] {'seq'}, dimensions={0}, use_global_device_ids=true | all-gather | bytes 786432 | tf_op jit(solution)/shard_map/all_gather | solution.py:253
  143.9 12.5 %while.36 = (s32[]{:T(128)}, bf16[2,8,128,64]{2,3,1,0:T(8,128)(2,1)}, f32[2,8,128,256]{3,2,1,0:T(8,128)}, f32[2,8,128,1]{2,1,3,0:T(8,128)S(1)}, s32[1,128]{1,0:T...) while((s32[]{:T(128)}, ...), condition=%wide.region_3.5_spmd, body=%wide.region_0.4_spmd.sunk | while | flops 69303296 | bytes 25008948 | solution.py:166
  168.2 5.8 %all-to-all-start.7 = ((bf16[16,8,1024]{2,1,0:T(8,128)(2,1)}), bf16[16,8,1024]{2,1,0:T(8,128)(2,1)}, u32[]{:S(2)}, u32[]{:S(2)}) async-start(bf16[16,8,1024]{2,1,0:T(8,128)(2,1)} %get-tuple-element.515), calls=%async_computation.7 | async-start | bytes 524288 | tf_op jit(solution)/shard_map/all_to_all | solution.py:247
  174.2 4.1 fusion.273
  179.3 4.7 all-to-all-done.7
  195.4 5.5 %stack.255 = f32[31,1024]{1,0:T(8,128)} concatenate(f32[1,1024]{1,0:T(1,128)} %bitcast.460, f32[1,1024]{1,0:T(1,128)} %bitcast.459, f32[1,1024]{1,0:T(1,128)} %bitcast.458, f32[1,1024]{1,0:T(1,128)} %bitcast.476, f32[1,1024]{1,0:T(1,128)} %bitcast.475, f32[1,1024]{1,0:T(1,128)} %bitcast.474, f32[1,1024]{1,0:T(1,128)} %bitcast.473, f32[1,1024]{1,0:T(1,128)} %bitcast.472, ...), dimensions={0} | concatenate | bytes 253952 | tf_op jit(solution)/shard_map/stack | solution.py:76
  201.7 4.5 collective-permute-start.2
  222.3 4.1 pad_maximum_fusion
  226.4 9.2 %copy.63 = f32[1024,2048]{1,0:T(8,128)} copy(f32[1024,2048]{0,1:T(8,128)} %pad_maximum_fusion) | data formatting | bytes 16777216
  236.3 8.9 %all_gather.20 = bf16[256,1024]{1,0:T(8,128)(2,1)} all-gather(bf16[128,1024]{1,0:T(8,128)(2,1)} %bitcast.368), channel_id=1, replica_groups=mesh['dp'=16,'seq'=2] {'seq'}, dimensions={0}, use_global_device_ids=true | all-gather | bytes 786432 | tf_op jit(solution)/shard_map/all_gather | solution.py:309
  255.0 4.3 all_gather.21
  266.3 11.4 %while.37 = (s32[]{:T(128)}, bf16[2,8,128,64]{2,3,1,0:T(8,128)(2,1)}, f32[2,8,128,1]{2,1,3,0:T(8,128)S(1)}, s32[2]{0:T(128)S(1)}, f32[2,8,128,256]{3,2,1,0:T(8,1...) while((s32[]{:T(128)}, ...), condition=%wide.region_14.16_spmd, body=%wide.region_12.15_spmd.sunk | while | flops 68549632 | bytes 15486203 | solution.py:205
  279.4 7.7 %all_gather.22 = bf16[256,1024]{1,0:T(8,128)(2,1)} all-gather(bf16[128,1024]{1,0:T(8,128)(2,1)} %convolution_convert_fusion.2), channel_id=1, replica_groups=mesh['dp'=16,'seq'=2] {'seq'}, dimensions={0}, use_global_device_ids=true | all-gather | bytes 786432 | tf_op jit(solution)/shard_map/all_gather | solution.py:310
  292.8 4.3 all_gather.23
  302.4 22.5 %all-reduce.3.cloned.1.call-done = f32[31,1024]{1,0:T(8,128)} async-done(((f32[31,1024]{1,0:T(8,128)}), f32[31,1024]{1,0:T(8,128)}) %all-reduce.3.cloned.1.call-update) | async-done | bytes 126992 | tf_op jit(solution)/shard_map/psum | solution.py:280
  324.9 185.4 %reduce-scatter.4.cloned.1.call-done = f32[32,2048]{1,0:T(8,128)} async-done(((f32[1024,2048]{1,0:T(8,128)}), f32[32,2048]{1,0:T(8,128)}) %reduce-scatter.4.cloned.1.call-update) | async-done | bytes 262160
  (347 shorter events, 122.0 us)
Async XLA Ops:
  7.2 149.2 %copy-start = (bf16[1024,1024]{1,0:T(8,128)(2,1)S(1)}, bf16[1024,1024]{1,0:T(8,128)(2,1)}, u32[]{:S(2)}) copy-start(bf16[1024,1024]{1,0:T(8,128)(2,1)} %param.24) | copy-start | bytes 6291460
  7.2 61.6 %copy-start.107 = (s32[16]{0:T(128)S(1)}, s32[16]{0:T(128)}, u32[]{:S(2)}) copy-start(s32[16]{0:T(128)} %param.31) | copy-start | bytes 196
  65.2 13.5 %all-to-all-start.6 = ((bf16[16,8,1024]{2,1,0:T(8,128)(2,1)}), bf16[16,8,1024]{2,1,0:T(8,128)(2,1)S(1)}, u32[]{:S(2)}, u32[]{:S(2)}) async-start(bf16[16,8,1024]{2,1,0:T(8,128)(2,1)} %bitcast.383), calls=%async_computation.6 | async-start | bytes 524288 | tf_op jit(solution)/shard_map/all_to_all | solution.py:233
  75.7 25.0 %copy-start.26 = (bf16[31,1024]{1,0:T(8,128)(2,1)S(1)}, bf16[31,1024]{1,0:T(8,128)(2,1)}, u32[]{:S(2)}) copy-start(bf16[31,1024]{1,0:T(8,128)(2,1)} %param.26) | copy-start | bytes 190468
  81.5 13.5 %all-to-all-start.5 = ((bf16[16,8,1024]{2,1,0:T(8,128)(2,1)}), bf16[16,8,1024]{2,1,0:T(8,128)(2,1)S(1)}, u32[]{:S(2)}, u32[]{:S(2)}) async-start(bf16[16,8,1024]{2,1,0:T(8,128)(2,1)} %get-tuple-element.517), calls=%async_computation.5 | async-start | bytes 524288 | tf_op jit(solution)/shard_map/all_to_all | solution.py:245
  95.0 21.0 %copy-start.11 = (bf16[16,8,1024]{2,1,0:T(8,128)(2,1)}, bf16[16,8,1024]{2,1,0:T(8,128)(2,1)S(1)}, u32[]{:S(2)}) copy-start(bf16[16,8,1024]{2,1,0:T(8,128)(2,1)S(1)} %all-to-all-done.5) | copy-start | bytes 786436
  95.0 13.5 %all-to-all-start.1 = ((bf16[16,8,1024]{2,1,0:T(8,128)(2,1)}), bf16[16,8,1024]{2,1,0:T(8,128)(2,1)S(1)}, u32[]{:S(2)}, u32[]{:S(2)}) async-start(bf16[16,8,1024]{2,1,0:T(8,128)(2,1)} %get-tuple-element.519), calls=%async_computation.1 | async-start | bytes 524288 | tf_op jit(solution)/shard_map/all_to_all | solution.py:243
  99.4 9.2 %copy-start.103 = (s32[128]{0:T(128)}, s32[128]{0:T(128)S(1)}, u32[]{:S(2)}) copy-start(s32[128]{0:T(128)S(1)} %dynamic-slice_bitcast_fusion) | copy-start | bytes 1540
  108.6 18.0 %all-to-all-start.3 = ((bf16[16,8,1024]{2,1,0:T(8,128)(2,1)}), bf16[16,8,1024]{2,1,0:T(8,128)(2,1)S(1)}, u32[]{:S(2)}, u32[]{:S(2)}) async-start(bf16[16,8,1024]{2,1,0:T(8,128)(2,1)} %get-tuple-element.516), calls=%async_computation.3 | async-start | bytes 524288 | tf_op jit(solution)/shard_map/all_to_all | solution.py:244
  116.1 27.8 %copy-start.45 = (s32[1,128]{1,0:T(1,128)S(1)}, s32[1,128]{1,0:T(1,128)}, u32[]{:S(2)}) copy-start(s32[1,128]{1,0:T(1,128)} %dynamic_slice.84) | copy-start | bytes 1540
  126.6 29.7 %all-to-all-start.9 = ((bf16[16,8,1024]{2,1,0:T(8,128)(2,1)}), bf16[16,8,1024]{2,1,0:T(8,128)(2,1)}, u32[]{:S(2)}, u32[]{:S(2)}) async-start(bf16[16,8,1024]{2,1,0:T(8,128)(2,1)} %get-tuple-element.518), calls=%async_computation.9 | async-start | bytes 524288 | tf_op jit(solution)/shard_map/all_to_all | solution.py:246
  162.9 11.4 %collective-permute-start = (bf16[15,1024]{1,0:T(8,128)(2,1)}, bf16[15,1024]{1,0:T(8,128)(2,1)S(1)}, u32[]{:S(2)}, u32[]{:S(2)}) collective-permute-start(bf16[15,1024]{1,0:T(8,128)(2,1)} %get-tuple-element.420), channel_id=1, source_target_pairs={{0,1},{2,3},{4,5},{6,7},{8,9},{10,11},{12,13},{14,15},{16,17},{18,... | collective-permute-start | bytes 92168 | tf_op jit(solution)/shard_map/ppermute | solution.py:23
  166.3 8.0 %collective-permute-start.1 = (bf16[15,1024]{1,0:T(8,128)(2,1)}, bf16[15,1024]{1,0:T(8,128)(2,1)S(1)}, u32[]{:S(2)}, u32[]{:S(2)}) collective-permute-start(bf16[15,1024]{1,0:T(8,128)(2,1)} %get-tuple-element.421), channel_id=1, source_target_pairs={{1,0},{3,2},{5,4},{7,6},{9,8},{11,10},{13,12},{15,14},{17,16},{19,... | collective-permute-start | bytes 92168 | tf_op jit(solution)/shard_map/ppermute | solution.py:25
  168.2 15.8 %all-to-all-start.7 = ((bf16[16,8,1024]{2,1,0:T(8,128)(2,1)}), bf16[16,8,1024]{2,1,0:T(8,128)(2,1)}, u32[]{:S(2)}, u32[]{:S(2)}) async-start(bf16[16,8,1024]{2,1,0:T(8,128)(2,1)} %get-tuple-element.515), calls=%async_computation.7 | async-start | bytes 524288 | tf_op jit(solution)/shard_map/all_to_all | solution.py:247
  174.0 150.9 %all-reduce.3.cloned.1.call-start = ((), (), s32[]{:S(2)}) async-start(), calls=%async_computation.11 | async-start | bytes 262144 | tf_op jit(solution)/shard_map/psum | solution.py:280
  178.3 8.6 %copy-start.105 = (f32[128]{0:T(128)}, f32[128]{0:T(128)S(1)}, u32[]{:S(2)}) copy-start(f32[128]{0:T(128)S(1)} %broadcast_multiply_fusion.4) | copy-start | bytes 1540
  200.9 309.4 %reduce-scatter.4.cloned.1.call-start = ((), (), s32[]{:S(2)}) async-start(), calls=%async_computation.12 | async-start | bytes 8650752
  201.7 8.6 %collective-permute-start.2 = (bf16[15,1024]{1,0:T(8,128)(2,1)S(1)}, bf16[15,1024]{1,0:T(8,128)(2,1)S(1)}, u32[]{:S(2)}, u32[]{:S(2)}) collective-permute-start(bf16[15,1024]{1,0:T(8,128)(2,1)S(1)} %get-tuple-element.418), channel_id=1, source_target_pairs={{0,1},{2,3},{4,5},{6,7},{8,9},{10,11},{12,13},{14,15},{16,17},{18,... | collective-permute-start | bytes 92168 | tf_op jit(solution)/shard_map/ppermute | solution.py:23
  206.7 5.9 %collective-permute-start.3 = (bf16[15,1024]{1,0:T(8,128)(2,1)S(1)}, bf16[15,1024]{1,0:T(8,128)(2,1)S(1)}, u32[]{:S(2)}, u32[]{:S(2)}) collective-permute-start(bf16[15,1024]{1,0:T(8,128)(2,1)S(1)} %get-tuple-element.419), channel_id=1, source_target_pairs={{1,0},{3,2},{5,4},{7,6},{9,8},{11,10},{13,12},{15,14},{17,16},{19,... | collective-permute-start | bytes 92168 | tf_op jit(solution)/shard_map/ppermute | solution.py:25
  235.6 11.7 %copy-start.12 = (bf16[16,8,1024]{2,1,0:T(8,128)(2,1)S(1)}, bf16[16,8,1024]{2,1,0:T(8,128)(2,1)}, u32[]{:S(2)}) copy-start(bf16[16,8,1024]{2,1,0:T(8,128)(2,1)} %copy-done.11) | copy-start | bytes 786436
  245.2 9.8 %copy-start.44 = (f32[2,8,128,1]{2,1,3,0:T(8,128)S(1)}, f32[2,8,128,1]{2,1,3,0:T(8,128)}, u32[]{:S(2)}) copy-start(f32[2,8,128,1]{2,1,3,0:T(8,128)} %copy-done.43) | copy-start | bytes 24580
  252.9 10.0 %copy-start.16 = (bf16[128,1024]{1,0:T(8,128)(2,1)S(1)}, bf16[128,1024]{1,0:T(8,128)(2,1)}, u32[]{:S(2)}) copy-start(bf16[128,1024]{1,0:T(8,128)(2,1)} %copy-done.15) | copy-start | bytes 786436
  287.1 10.1 %copy-start.20 = (bf16[256,1024]{0,1:T(8,128)(2,1)S(1)}, bf16[256,1024]{0,1:T(8,128)(2,1)}, u32[]{:S(2)}) copy-start(bf16[256,1024]{0,1:T(8,128)(2,1)} %copy.55) | copy-start | bytes 1572868
  287.1 10.1 %copy-start.22 = (bf16[128,16,64]{0,2,1:T(8,128)(2,1)S(1)}, bf16[128,16,64]{0,2,1:T(8,128)(2,1)}, u32[]{:S(2)}) copy-start(bf16[128,16,64]{0,2,1:T(8,128)(2,1)} %copy.58) | copy-start | bytes 786436
  (103 other events, 462.4 us)
Sparse Core Ops, SparseCore 0:
  201.0 123.8 all-reduce.2
  327.8 182.4 reduce-scatter.3
where the time goes:
time: 521 us; the launch traced here: 519 us
  waiting for transfers between devices  235 us (45%)
  blocking collectives  102 us (20%)
  local copies, waits for them, and re-layouts  63 us (12%)
  starting transfers between devices  36.9 us (7%)
  matrix products  29.4 us (6%)
  other arithmetic  26.4 us (5%)
  between operations  17.6 us (3%)
  loops' own time  8.02 us (2%)
    unnamed x3, waiting for transfers between devices  185 us
    psum x1, waiting for transfers between devices, per_device(): kernel_grad = lax.psum(tap_sums(conv_grad, padded, table), ('dp', 'seq'))  22.5 us
    unnamed x207, local copies, waits for them, and re-layouts  19.6 us
    all_to_all x1, blocking collectives, per_device(): lax.all_to_all(queries[0], 'dp', split_axis=0, concat_axis=0, tiled=True)  17.5 us
    all_to_all x1, blocking collectives, per_device(): lax.all_to_all(keys[0], 'dp', split_axis=0, concat_axis=0, tiled=True)  13.5 us
    all_to_all x1, blocking collectives, per_device(): lax.all_to_all(values[0], 'dp', split_axis=0, concat_axis=0, tiled=True)  13.5 us
    all_to_all x1, blocking collectives, per_device(): lax.all_to_all(stream[0], 'dp', split_axis=0, concat_axis=0, tiled=True)  13.5 us
  transfers between devices with their start and end apart: 12, of which 7 were waited for; matrix products, arithmetic and copies ran while one was open for 16% of the time, Pallas kernels for 0%

commit v1 on v0

v1 whole, which is shorter than its diff:
```python
import jax
import jax.numpy as jnp
from jax import lax
from jax.sharding import PartitionSpec as P

HEAD_DIM = 64


EPSILON = 1e-05
MASKED = -1e30


def extended(cells, sides, width):
    for axis, dim in sides:
        count = lax.axis_size(axis)
        ends = count - 1
        head = lax.slice_in_dim(cells, 0, width, axis=dim)
        tail = lax.slice_in_dim(cells, cells.shape[dim] - width, cells.shape[dim], axis=dim)
        cells = jnp.concatenate(
            [
                lax.ppermute(tail, axis, [(i, (i + 1) % count) for i in range(ends)]),
                cells,
                lax.ppermute(head, axis, [((i + 1) % count, i) for i in range(ends)]),
            ],
            axis=dim,
        )
    return cells


def layer_norm(stream, gain):
    center = jnp.mean(stream, -1, keepdims=True)
    shifted = stream - center
    inverse = lax.rsqrt(jnp.mean(shifted * shifted, -1, keepdims=True) + EPSILON)
    normed = shifted * inverse
    return (normed * gain, normed, inverse)


def norm_backward(upstream, normed, inverse, gain):
    scaled = upstream * gain
    return inverse * (
        scaled
        - jnp.mean(scaled, -1, keepdims=True)
        - normed * jnp.mean(scaled * normed, -1, keepdims=True)
    )


def swish_slope(values):
    logistic = jax.nn.sigmoid(values)
    return logistic * (1.0 + values * (1.0 - logistic))


def tap_table(padded_ids, own_ids, taps):
    length = own_ids.shape[0]
    return (
        jnp.stack([padded_ids[tap : tap + length] for tap in range(taps)], 1) == own_ids[:, None]
    ).astype(jnp.float32)


def depthwise(padded, weights, table):
    length = table.shape[0]
    total = jnp.zeros((length, padded.shape[1]), jnp.float32)
    for tap in range(weights.shape[0]):
        total = (
            total
            + weights[tap].astype(jnp.float32)
            * padded[tap : tap + length].astype(jnp.float32)
            * table[:, tap : tap + 1]
        )
    return total


def tap_sums(upstream, padded, table):
    length = table.shape[0]
    return jnp.stack(
        [
            jnp.sum(
                upstream * padded[tap : tap + length].astype(jnp.float32) * table[:, tap : tap + 1],
                0,
            )
            for tap in range(table.shape[1])
        ]
    )


def times_transposed(left, right):
    return lax.dot_general(
        left, right, (((1,), (1,)), ((), ())), preferred_element_type=jnp.float32
    )


def transposed_times(left, right):
    return lax.dot_general(
        left, right, (((0,), (0,)), ((), ())), preferred_element_type=jnp.float32
    )


def split_heads(matrix):
    return matrix.reshape(matrix.shape[0], -1, HEAD_DIM).transpose(1, 0, 2)


def merge_heads(tensor):
    return tensor.transpose(1, 0, 2).reshape(tensor.shape[1], -1)


def shifted_copies(cells, axis):
    count = lax.axis_size(axis)
    return [cells] + [
        lax.ppermute(cells, axis, [((i + step) % count, i) for i in range(count)])
        for step in range(1, count)
    ]


def returned(parts, axis):
    count = lax.axis_size(axis)
    total = parts[0]
    for step in range(1, count):
        back = lax.ppermute(
            parts[step].astype(jnp.bfloat16),
            axis,
            [(i, (i + step) % count) for i in range(count)],
        )
        total = total + back.astype(jnp.float32)
    return total


def route(matrix, plan):
    rows, width = matrix.shape
    slots = plan.shape[0]
    spread = lax.all_to_all(matrix, "dp", split_axis=0, concat_axis=0, tiled=True)
    arranged = jnp.take(spread.reshape(slots, -1, width), plan, axis=0, mode="clip")
    return lax.all_to_all(
        arranged.reshape(rows, width), "dp", split_axis=0, concat_axis=0, tiled=True
    )


def per_device(
    queries,
    keys,
    values,
    stream,
    cotangent,
    attn_out,
    point_in,
    kernel,
    point_out,
    norm_gain,
    conv_gain,
    segments,
    plan,
):
    frames, width = (queries.shape[1], queries.shape[2])
    seq_place = lax.axis_index("seq")
    seq_count = lax.axis_size("seq")
    scale = HEAD_DIM ** (-0.5)
    query_rows, key_rows, value_rows = (queries[0], keys[0], values[0])
    stream_rows, grad_rows = (stream[0], cotangent[0])
    pack_ids = lax.dynamic_index_in_dim(segments, lax.axis_index("dp"), 0, keepdims=False)
    own_ids = lax.dynamic_slice_in_dim(pack_ids, seq_place * frames, frames)
    key_ids = jnp.roll(pack_ids, -seq_place * frames)

    pairs = shifted_copies(jnp.concatenate([key_rows, value_rows], 1), "seq")
    all_pairs = jnp.concatenate(pairs, 0)
    query_heads = split_heads(query_rows)
    key_heads = split_heads(all_pairs[:, :width])
    value_heads = split_heads(all_pairs[:, width:])
    scores = (
        jnp.einsum("hqe,hke->hqk", query_heads, key_heads, preferred_element_type=jnp.float32)
        * scale
    )
    scores = jnp.where((own_ids[:, None] == key_ids[None, :])[None], scores, MASKED)
    highest = jnp.max(scores, -1, keepdims=True)
    raised = jnp.exp(scores - highest)
    weights = raised * (1.0 / jnp.sum(raised, -1, keepdims=True))
    weights_low = weights.astype(jnp.bfloat16)
    mixed = merge_heads(
        jnp.einsum(
            "hqk,hke->hqe", weights_low, value_heads, preferred_element_type=jnp.float32
        ).astype(jnp.bfloat16)
    )
    hidden = stream_rows.astype(jnp.float32) + jnp.dot(
        mixed, attn_out, preferred_element_type=jnp.float32
    )
    normed_in, hat_in, inv_in = layer_norm(hidden, norm_gain)
    both = jnp.dot(normed_in.astype(jnp.bfloat16), point_in, preferred_element_type=jnp.float32)
    linear = both[:, :width]
    logistic = jax.nn.sigmoid(both[:, width:])
    conv_in = (linear * logistic).astype(jnp.bfloat16)
    taps = kernel.shape[0]
    reach = taps // 2
    padded = extended(conv_in, (("seq", 0),), reach)
    padded_ids = lax.dynamic_slice_in_dim(
        jnp.pad(pack_ids, reach, constant_values=-1), seq_place * frames, frames + 2 * reach
    )
    table = tap_table(padded_ids, own_ids, taps)
    conv_out = depthwise(padded, kernel, table)
    normed_out, hat_out, inv_out = layer_norm(conv_out, conv_gain)
    activated = (normed_out * jax.nn.sigmoid(normed_out)).astype(jnp.bfloat16)
    out_part = lax.psum_scatter(
        transposed_times(activated, grad_rows).astype(jnp.bfloat16),
        ("dp", "seq"),
        scatter_dimension=0,
        tiled=True,
    )
    act_grad = times_transposed(grad_rows, point_out)
    conv_grad = norm_backward(act_grad * swish_slope(normed_out), hat_out, inv_out, conv_gain)
    grad_padded = extended(conv_grad.astype(jnp.bfloat16), (("seq", 0),), reach).astype(
        conv_grad.dtype
    )
    kernel_grad = lax.psum(tap_sums(conv_grad, padded, table), ("dp", "seq"))
    in_grad = depthwise(grad_padded, kernel[::-1], table)
    both_grad = jnp.concatenate(
        [in_grad * logistic, in_grad * linear * logistic * (1.0 - logistic)], 1
    ).astype(jnp.bfloat16)
    back_in = times_transposed(both_grad, point_in)
    stream_out = (
        grad_rows.astype(jnp.float32) + norm_backward(back_in, hat_in, inv_in, norm_gain)
    ).astype(jnp.bfloat16)
    in_part = lax.psum_scatter(
        transposed_times(mixed, stream_out).astype(jnp.bfloat16),
        ("dp", "seq"),
        scatter_dimension=0,
        tiled=True,
    )
    mixed_grad = times_transposed(stream_out, attn_out).astype(jnp.bfloat16)
    grad_heads = split_heads(mixed_grad)
    slope = jnp.einsum(
        "hqe,hke->hqk", grad_heads, value_heads, preferred_element_type=jnp.float32
    )
    delta = jnp.sum(weights * slope, -1, keepdims=True)
    score_grad = (weights * (slope - delta)).astype(jnp.bfloat16)
    query_grad = merge_heads(
        (
            jnp.einsum("hqk,hke->hqe", score_grad, key_heads, preferred_element_type=jnp.float32)
            * scale
        ).astype(jnp.bfloat16)
    )
    key_part = merge_heads(
        jnp.einsum("hqk,hqe->hke", score_grad, query_heads, preferred_element_type=jnp.float32)
        * scale
    )
    value_part = merge_heads(
        jnp.einsum("hqk,hqe->hke", weights_low, grad_heads, preferred_element_type=jnp.float32)
    )
    pair_part = jnp.concatenate([key_part, value_part], 1)
    pair_grad = returned(
        [pair_part[step * frames : (step + 1) * frames] for step in range(seq_count)], "seq"
    ).astype(jnp.bfloat16)
    stream_routed = route(stream_out, plan)
    routed = route(jnp.concatenate([query_grad, pair_grad], 1), plan)
    return (
        routed[None, :, :width],
        routed[None, :, width : 2 * width],
        routed[None, :, 2 * width :],
        stream_routed[None],
        kernel_grad,
        jnp.concatenate([in_part, out_part], 1).astype(jnp.float32),
    )


def solution(mesh):
    placed = (
        P("dp", "seq", None),
        P("dp", "seq", None),
        P("dp", "seq", None),
        P("dp", "seq", None),
        P("dp", "seq", None),
        P(),
        P(),
        P(),
        P(),
        P(),
        P(),
        P(),
        P(),
    )
    return jax.shard_map(
        per_device,
        mesh=mesh,
        in_specs=placed,
        out_specs=(
            P("dp", "seq", None),
            P("dp", "seq", None),
            P("dp", "seq", None),
            P("dp", "seq", None),
            P(),
            P(("dp", "seq"), None),
        ),
        check_vma=False,
    )
```

time: 521 us -> 483 us (0.927)
  waiting for transfers between devices: 235 us -> 343 us
  blocking collectives: 102 us -> 0 us
  local copies, waits for them, and re-layouts: 63 us -> 30.1 us
  loops' own time: 8.02 us -> 0 us
    unnamed x3, waiting for transfers between devices: 185 us -> 0.05 us
    reduce_scatter x0 -> x2, waiting for transfers between devices: none -> 156 us  [the longest x1 137 us: per_device(): lax.psum_scatter(transposed_times(mixed, stream_out).astype(jnp.bfloat16)...]
    psum x1, waiting for transfers between devices: 22.5 us -> 126 us  [per_device(): kernel_grad = lax.psum(tap_sums(conv_grad, padded, table), ('dp', 'seq'))]
    all_to_all x4 -> x0, blocking collectives: 58 us -> none  [the longest x1 17.5 us: per_device(): lax.all_to_all(queries[0], 'dp', split_axis=0, concat_axis=0, tiled=True)]
    all_gather x6 -> x0, blocking collectives: 43.9 us -> none  [the longest x1 9.34 us: per_device(): lax.all_gather(key_rows, 'seq', axis=0, tiled=True)]
    ppermute x0 -> x2, waiting for transfers between devices: none -> 17.8 us  [the longest x1 12.6 us: returned(): lax.ppermute(parts[step].astype(jnp.bfloat16), axis, [(i, (i + step) % co...]
    unnamed x207 -> x229, local copies, waits for them, and re-layouts: 19.6 us -> 6.5 us
    all_to_all x6 -> x4, waiting for transfers between devices: 25.2 us -> 37 us  [the longest x2 20.5 us: route(): lax.all_to_all(arranged.reshape(rows, width), 'dp', split_axis=0, concat_...]
  transfers between devices with their start and end apart: 12 -> 13, of which waited for: 7 -> 11; matrix products, arithmetic and copies ran while one was open for 16% -> 12% of each run, Pallas kernels for 0% -> 0%
where the time goes in v1:
time: 483 us; the launch traced here: 482 us
  waiting for transfers between devices  343 us (71%)
  starting transfers between devices  36.5 us (8%)
  local copies, waits for them, and re-layouts  30.1 us (6%)
  matrix products  28.9 us (6%)
  other arithmetic  27 us (6%)
  between operations  15.6 us (3%)
    reduce_scatter x1, waiting for transfers between devices, per_device(): lax.psum_scatter(transposed_times(mixed, stream_out).astype(jnp.bfloat16)...  137 us
    psum x1, waiting for transfers between devices, per_device(): kernel_grad = lax.psum(tap_sums(conv_grad, padded, table), ('dp', 'seq'))  126 us
    all_to_all x2, waiting for transfers between devices, route(): lax.all_to_all(arranged.reshape(rows, width), 'dp', split_axis=0, concat_...  20.5 us
    reduce_scatter x1, waiting for transfers between devices, per_device(): lax.psum_scatter(transposed_times(activated, grad_rows).astype(jnp.bfloat...  19.2 us
    all_to_all x2, waiting for transfers between devices, route(): lax.all_to_all(matrix, 'dp', split_axis=0, concat_axis=0, tiled=True)  16.5 us
    all_to_all x2, starting transfers between devices, route(): lax.all_to_all(matrix, 'dp', split_axis=0, concat_axis=0, tiled=True)  12.6 us
    ppermute x1, waiting for transfers between devices, returned(): lax.ppermute(parts[step].astype(jnp.bfloat16), axis, [(i, (i + step) % co...  12.6 us
    all_to_all x2, starting transfers between devices, route(): lax.all_to_all(arranged.reshape(rows, width), 'dp', split_axis=0, concat_...  11.1 us
  transfers between devices with their start and end apart: 13, of which 11 were waited for; matrix products, arithmetic and copies ran while one was open for 12% of the time, Pallas kernels for 0%

profile of v1, /device:TPU:0, one launch (start us, length us, event | category | flops | bytes accessed | tf_op | source)
XLA Modules:
  0.0 481.6 jit_solution(6743566292965435913)
XLA Ops:
  8.5 3.1 collective-permute-start
  18.3 5.2 %collective-permute-done = bf16[128,2048]{1,0:T(8,128)(2,1)} collective-permute-done((bf16[128,2048]{1,0:T(8,128)(2,1)S(1)}, bf16[128,2048]{1,0:T(8,128)(2,1)}, u32[]{:S(2)}, u32[]{:S(2)}) %collective-permute-start) | collective-permute-done | bytes 524320 | tf_op jit(solution)/shard_map/ppermute | solution.py:108
  35.9 3.0 fusion.204
  40.1 3.8 collective-permute-start.1
  45.4 4.2 collective-permute-done.2
  50.0 3.2 fusion.261
  68.1 4.4 multiply_convert_fusion.4
  75.3 6.0 %all-to-all-start.2 = ((bf16[16,8,1024]{2,1,0:T(8,128)(2,1)}), bf16[16,8,1024]{2,1,0:T(8,128)(2,1)}, u32[]{:S(2)}, u32[]{:S(2)}) async-start(bf16[16,8,1024]{2,1,0:T(8,128)(2,1)} %bitcast.275), calls=%async_computation.2 | async-start | bytes 524288 | tf_op jit(solution)/shard_map/all_to_all | solution.py:129
  84.0 3.4 fusion.203
  87.4 2.5 copy.41
  95.2 2.6 copy.40
  104.1 3.0 convolution_convert_fusion.1
  107.2 12.6 %collective-permute-done.5 = bf16[128,2048]{1,0:T(8,128)(2,1)} collective-permute-done((bf16[128,2048]{1,0:T(8,128)(2,1)}, bf16[128,2048]{1,0:T(8,128)(2,1)}, u32[]{:S(2)}, u32[]{:S(2)}) %collective-permute-start.5) | collective-permute-done | bytes 524320 | tf_op jit(solution)/shard_map/ppermute | solution.py:117
  122.2 6.7 %all-to-all-start = ((bf16[16,8,3072]{2,1,0:T(8,128)(2,1)}), bf16[16,8,3072]{2,1,0:T(8,128)(2,1)}, u32[]{:S(2)}, u32[]{:S(2)}) async-start(bf16[16,8,3072]{2,1,0:T(8,128)(2,1)} %pad_maximum_fusion.2), calls=%async_computation | async-start | bytes 1572864 | tf_op jit(solution)/shard_map/all_to_all | solution.py:129
  131.2 16.5 %all-to-all-done = bf16[16,8,3072]{2,1,0:T(8,128)(2,1)} async-done(((bf16[16,8,3072]{2,1,0:T(8,128)(2,1)}), bf16[16,8,3072]{2,1,0:T(8,128)(2,1)}, u32[]{:S(2)}, u32[]{:S(2)}) %all-to-all-start) | async-done | bytes 786464 | tf_op jit(solution)/shard_map/all_to_all | solution.py:129
  147.7 6.8 %all-to-all-start.3 = ((bf16[16,8,1024]{2,1,0:T(8,128)(2,1)}), bf16[16,8,1024]{2,1,0:T(8,128)(2,1)S(1)}, u32[]{:S(2)}, u32[]{:S(2)}) async-start(bf16[16,8,1024]{2,1,0:T(8,128)(2,1)} %gather_fusion.1), calls=%async_computation.3 | async-start | bytes 524288 | tf_op jit(solution)/shard_map/all_to_all | solution.py:131
  154.5 2.6 gather_fusion
  157.2 7.3 %all-to-all-done.3 = bf16[16,8,1024]{2,1,0:T(8,128)(2,1)S(1)} async-done(((bf16[16,8,1024]{2,1,0:T(8,128)(2,1)}), bf16[16,8,1024]{2,1,0:T(8,128)(2,1)S(1)}, u32[]{:S(2)}, u32[]{:S(2)}) %all-to-all-start.3) | async-done | bytes 262176 | tf_op jit(solution)/shard_map/all_to_all | solution.py:131
  164.5 4.3 all-to-all-start.1
  171.5 2.7 stack.255
  174.2 13.3 %all-to-all-done.1 = bf16[16,8,3072]{2,1,0:T(8,128)(2,1)} async-done(((bf16[16,8,3072]{2,1,0:T(8,128)(2,1)}), bf16[16,8,3072]{2,1,0:T(8,128)(2,1)}, u32[]{:S(2)}, u32[]{:S(2)}) %all-to-all-start.1) | async-done | bytes 786464 | tf_op jit(solution)/shard_map/all_to_all | solution.py:131
  189.4 19.2 %reduce-scatter.5.cloned.1.call-done = bf16[32,1024]{1,0:T(8,128)(2,1)} async-done(((bf16[1024,1024]{1,0:T(8,128)(2,1)}), bf16[32,1024]{1,0:T(8,128)(2,1)}) %reduce-scatter.5.cloned.1.call-update) | async-done | bytes 65552 | tf_op jit(solution)/shard_map/reduce_scatter | solution.py:198
  208.6 137.0 %reduce-scatter.3.cloned.1.call-done = bf16[32,1024]{1,0:T(8,128)(2,1)} async-done(((bf16[1024,1024]{1,0:T(8,128)(2,1)}), bf16[32,1024]{1,0:T(8,128)(2,1)}) %reduce-scatter.3.cloned.1.call-update) | async-done | bytes 65552 | tf_op jit(solution)/shard_map/reduce_scatter | solution.py:218
  347.1 125.7 %all-reduce.3.cloned.1.call-done = f32[31,1024]{1,0:T(8,128)} async-done(((f32[31,1024]{1,0:T(8,128)}), f32[31,1024]{1,0:T(8,128)}) %all-reduce.3.cloned.1.call-update) | async-done | bytes 126992 | tf_op jit(solution)/shard_map/psum | solution.py:209
  (306 shorter events, 67.3 us)
Async XLA Ops:
  7.2 26.6 %copy-start = (bf16[1024,1024]{1,0:T(8,128)(2,1)S(1)}, bf16[1024,1024]{1,0:T(8,128)(2,1)}, u32[]{:S(2)}) copy-start(bf16[1024,1024]{1,0:T(8,128)(2,1)} %param.18) | copy-start | bytes 6291460
  7.2 16.4 %copy-start.16 = (bf16[1,128,1024]{2,1,0:T(8,128)(2,1)S(1)}, bf16[1,128,1024]{2,1,0:T(8,128)(2,1)}, u32[]{:S(2)}) copy-start(bf16[1,128,1024]{2,1,0:T(8,128)(2,1)} %param.15) | copy-start | bytes 786436
  7.2 16.4 %copy-start.17 = (bf16[1,128,1024]{2,1,0:T(8,128)(2,1)S(1)}, bf16[1,128,1024]{2,1,0:T(8,128)(2,1)}, u32[]{:S(2)}) copy-start(bf16[1,128,1024]{2,1,0:T(8,128)(2,1)} %param.14) | copy-start | bytes 786436
  7.2 201.4 %reduce-scatter.5.cloned.1.call-start = ((), (), s32[]{:S(2)}) async-start(), calls=%async_computation.8 | async-start | bytes 2162688 | tf_op jit(solution)/shard_map/reduce_scatter | solution.py:198
  8.5 15.1 %collective-permute-start = (bf16[128,2048]{1,0:T(8,128)(2,1)S(1)}, bf16[128,2048]{1,0:T(8,128)(2,1)}, u32[]{:S(2)}, u32[]{:S(2)}) collective-permute-start(bf16[128,2048]{1,0:T(8,128)(2,1)S(1)} %pad_maximum_fusion.3), channel_id=1, source_target_pairs={{1,0},{0,1},{3,2},{2,3},{5,4},{4,5},{7,6},{6,7},{9,8},{8,9},{11,10... | collective-permute-start | bytes 1572872 | tf_op jit(solution)/shard_map/ppermute | solution.py:108
  13.6 17.7 %copy-start.41 = (pred[128,256]{0,1:T(8,128)(4,1)}, pred[128,256]{0,1:T(8,128)(4,1)S(1)}, u32[]{:S(2)}) copy-start(pred[128,256]{0,1:T(8,128)(4,1)S(1)} %broadcast_compare_fusion) | copy-start | bytes 98308
  40.1 5.4 %collective-permute-start.1 = (bf16[15,1024]{1,0:T(8,128)(2,1)S(1)}, bf16[15,1024]{1,0:T(8,128)(2,1)S(1)}, u32[]{:S(2)}, u32[]{:S(2)}) collective-permute-start(bf16[15,1024]{1,0:T(8,128)(2,1)S(1)} %get-tuple-element.54), channel_id=1, source_target_pairs={{0,1},{2,3},{4,5},{6,7},{8,9},{10,11},{12,13},{14,15},{16,17},{18,... | collective-permute-start | bytes 92168 | tf_op jit(solution)/shard_map/ppermute | solution.py:21
  43.9 5.8 %collective-permute-start.2 = (bf16[15,1024]{1,0:T(8,128)(2,1)S(1)}, bf16[15,1024]{1,0:T(8,128)(2,1)S(1)}, u32[]{:S(2)}, u32[]{:S(2)}) collective-permute-start(bf16[15,1024]{1,0:T(8,128)(2,1)S(1)} %get-tuple-element.55), channel_id=1, source_target_pairs={{1,0},{3,2},{5,4},{7,6},{9,8},{11,10},{13,12},{15,14},{17,16},{19,... | collective-permute-start | bytes 92168 | tf_op jit(solution)/shard_map/ppermute | solution.py:23
  58.6 5.9 %collective-permute-start.3 = (bf16[15,1024]{1,0:T(8,128)(2,1)}, bf16[15,1024]{1,0:T(8,128)(2,1)}, u32[]{:S(2)}, u32[]{:S(2)}) collective-permute-start(bf16[15,1024]{1,0:T(8,128)(2,1)} %get-tuple-element.52), channel_id=1, source_target_pairs={{0,1},{2,3},{4,5},{6,7},{8,9},{10,11},{12,13},{14,15},{16,17},{18,... | collective-permute-start | bytes 92168 | tf_op jit(solution)/shard_map/ppermute | solution.py:21
  60.8 6.1 %collective-permute-start.4 = (bf16[15,1024]{1,0:T(8,128)(2,1)}, bf16[15,1024]{1,0:T(8,128)(2,1)}, u32[]{:S(2)}, u32[]{:S(2)}) collective-permute-start(bf16[15,1024]{1,0:T(8,128)(2,1)} %get-tuple-element.53), channel_id=1, source_target_pairs={{1,0},{3,2},{5,4},{7,6},{9,8},{11,10},{13,12},{15,14},{17,16},{19,... | collective-permute-start | bytes 92168 | tf_op jit(solution)/shard_map/ppermute | solution.py:23
  75.3 46.9 %all-to-all-start.2 = ((bf16[16,8,1024]{2,1,0:T(8,128)(2,1)}), bf16[16,8,1024]{2,1,0:T(8,128)(2,1)}, u32[]{:S(2)}, u32[]{:S(2)}) async-start(bf16[16,8,1024]{2,1,0:T(8,128)(2,1)} %bitcast.275), calls=%async_computation.2 | async-start | bytes 524288 | tf_op jit(solution)/shard_map/all_to_all | solution.py:129
  81.3 264.2 %reduce-scatter.3.cloned.1.call-start = ((), (), s32[]{:S(2)}) async-start(), calls=%async_computation.7 | async-start | bytes 2162688 | tf_op jit(solution)/shard_map/reduce_scatter | solution.py:218
  100.0 19.8 %collective-permute-start.5 = (bf16[128,2048]{1,0:T(8,128)(2,1)}, bf16[128,2048]{1,0:T(8,128)(2,1)}, u32[]{:S(2)}, u32[]{:S(2)}) collective-permute-start(bf16[128,2048]{1,0:T(8,128)(2,1)} %fusion.8), channel_id=1, source_target_pairs={{0,1},{1,0},{2,3},{3,2},{4,5},{5,4},{6,7},{7,6},{8,9},{9,8},{10,11... | collective-permute-start | bytes 1572872 | tf_op jit(solution)/shard_map/ppermute | solution.py:117
  122.2 25.4 %all-to-all-start = ((bf16[16,8,3072]{2,1,0:T(8,128)(2,1)}), bf16[16,8,3072]{2,1,0:T(8,128)(2,1)}, u32[]{:S(2)}, u32[]{:S(2)}) async-start(bf16[16,8,3072]{2,1,0:T(8,128)(2,1)} %pad_maximum_fusion.2), calls=%async_computation | async-start | bytes 1572864 | tf_op jit(solution)/shard_map/all_to_all | solution.py:129
  128.9 40.2 %copy-start.103 = (f32[128]{0:T(128)S(1)}, f32[128]{0:T(128)}, u32[]{:S(2)}) copy-start(f32[128]{0:T(128)} %get-tuple-element.87) | copy-start | bytes 1540
  128.9 40.2 %copy-start.105 = (f32[128]{0:T(128)S(1)}, f32[128]{0:T(128)}, u32[]{:S(2)}) copy-start(f32[128]{0:T(128)} %copy-done.104) | copy-start | bytes 1540
  129.0 40.2 %copy-start.107 = (f32[128]{0:T(128)S(1)}, f32[128]{0:T(128)}, u32[]{:S(2)}) copy-start(f32[128]{0:T(128)} %copy-done.106) | copy-start | bytes 1540
  147.7 16.8 %all-to-all-start.3 = ((bf16[16,8,1024]{2,1,0:T(8,128)(2,1)}), bf16[16,8,1024]{2,1,0:T(8,128)(2,1)S(1)}, u32[]{:S(2)}, u32[]{:S(2)}) async-start(bf16[16,8,1024]{2,1,0:T(8,128)(2,1)} %gather_fusion.1), calls=%async_computation.3 | async-start | bytes 524288 | tf_op jit(solution)/shard_map/all_to_all | solution.py:131
  154.5 15.4 %copy-start.63 = (f32[128]{0:T(128)S(1)}, f32[128]{0:T(128)}, u32[]{:S(2)}) copy-start(f32[128]{0:T(128)} %get-tuple-element.104) | copy-start | bytes 1540
  154.5 15.4 %copy-start.65 = (f32[128]{0:T(128)S(1)}, f32[128]{0:T(128)}, u32[]{:S(2)}) copy-start(f32[128]{0:T(128)} %get-tuple-element.105) | copy-start | bytes 1540
  154.5 15.4 %copy-start.87 = (f32[128]{0:T(128)S(1)}, f32[128]{0:T(128)}, u32[]{:S(2)}) copy-start(f32[128]{0:T(128)} %copy-done.86) | copy-start | bytes 1540
  154.5 15.4 %copy-start.89 = (f32[128]{0:T(128)S(1)}, f32[128]{0:T(128)}, u32[]{:S(2)}) copy-start(f32[128]{0:T(128)} %copy-done.88) | copy-start | bytes 1540
  164.5 23.0 %all-to-all-start.1 = ((bf16[16,8,3072]{2,1,0:T(8,128)(2,1)}), bf16[16,8,3072]{2,1,0:T(8,128)(2,1)}, u32[]{:S(2)}, u32[]{:S(2)}) async-start(bf16[16,8,3072]{2,1,0:T(8,128)(2,1)} %gather_fusion), calls=%async_computation.1 | async-start | bytes 1572864 | tf_op jit(solution)/shard_map/all_to_all | solution.py:131
  168.9 303.9 %all-reduce.3.cloned.1.call-start = ((), (), s32[]{:S(2)}) async-start(), calls=%async_computation.6 | async-start | bytes 262144 | tf_op jit(solution)/shard_map/psum | solution.py:209
  (102 other events, 976.4 us)
Sparse Core Ops, SparseCore 0:
  64.7 143.8 reduce-scatter.4
  210.8 134.6 reduce-scatter.2
  351.7 121.0 all-reduce.2

commit v2 on v1

--- a/solution.py
+++ b/solution.py
@@ -131,6 +131,57 @@
     return lax.all_to_all(
         arranged.reshape(rows, width), "dp", split_axis=0, concat_axis=0, tiled=True
     )
+
+
+def exchange_order():
+    slots = (lax.axis_size("dp") - 1).bit_length()
+    seqs = (lax.axis_size("seq") - 1).bit_length()
+    return (
+        [("dp", bit, seqs + bit) for bit in range(min(2, slots))]
+        + [("seq", bit, bit) for bit in range(seqs)]
+        + [("dp", bit, seqs + bit) for bit in range(2, slots)]
+    )
+
+
+def swapped(cells, axis, bit):
+    return lax.ppermute(
+        cells, axis, [(i, i ^ (1 << bit)) for i in range(lax.axis_size(axis))]
+    )
+
+
+def reduced_product(left, right):
+    order = exchange_order()
+    blocks = 1 << len(order)
+    rows = left.shape[1] // blocks
+    positions = sorted(position for _, _, position in order)
+    total = None
+    for axis, bit, position in order:
+        low = rows << positions.index(position)
+        positions.remove(position)
+        mine = (lax.axis_index(axis) >> bit) & 1
+        if total is None:
+            split = left.reshape(left.shape[0], -1, 2, low)
+
+            def piece(which):
+                chosen = lax.dynamic_index_in_dim(split, which, 2, keepdims=False)
+                return transposed_times(chosen.reshape(left.shape[0], -1), right)
+
+        else:
+            split = total.reshape(-1, 2, low, right.shape[1])
+
+            def piece(which):
+                chosen = lax.dynamic_index_in_dim(split, which, 1, keepdims=False)
+                return chosen.reshape(-1, right.shape[1])
+
+        arrived = swapped(piece(1 - mine).astype(jnp.bfloat16), axis, bit)
+        total = piece(mine) + arrived.astype(jnp.float32)
+    return total
+
+
+def reduced_everywhere(cells):
+    for axis, bit, _ in exchange_order():
+        cells = cells + swapped(cells, axis, bit)
+    return cells
 
 
 def per_device(
@@ -195,18 +246,13 @@
     conv_out = depthwise(padded, kernel, table)
     normed_out, hat_out, inv_out = layer_norm(conv_out, conv_gain)
     activated = (normed_out * jax.nn.sigmoid(normed_out)).astype(jnp.bfloat16)
-    out_part = lax.psum_scatter(
-        transposed_times(activated, grad_rows).astype(jnp.bfloat16),
-        ("dp", "seq"),
-        scatter_dimension=0,
-        tiled=True,
-    )
+    out_part = reduced_product(activated, grad_rows)
     act_grad = times_transposed(grad_rows, point_out)
     conv_grad = norm_backward(act_grad * swish_slope(normed_out), hat_out, inv_out, conv_gain)
     grad_padded = extended(conv_grad.astype(jnp.bfloat16), (("seq", 0),), reach).astype(
         conv_grad.dtype
     )
-    kernel_grad = lax.psum(tap_sums(conv_grad, padded, table), ("dp", "seq"))
+    kernel_grad = reduced_everywhere(tap_sums(conv_grad, padded, table))
     in_grad = depthwise(grad_padded, kernel[::-1], table)
     both_grad = jnp.concatenate(
         [in_grad * logistic, in_grad * linear * logistic * (1.0 - logistic)], 1
@@ -215,12 +261,7 @@
     stream_out = (
         grad_rows.astype(jnp.float32) + norm_backward(back_in, hat_in, inv_in, norm_gain)
     ).astype(jnp.bfloat16)
-    in_part = lax.psum_scatter(
-        transposed_times(mixed, stream_out).astype(jnp.bfloat16),
-        ("dp", "seq"),
-        scatter_dimension=0,
-        tiled=True,
-    )
+    in_part = reduced_product(mixed, stream_out)
     mixed_grad = times_transposed(stream_out, attn_out).astype(jnp.bfloat16)
     grad_heads = split_heads(mixed_grad)
     slope = jnp.einsum(
@@ -253,7 +294,7 @@
         routed[None, :, 2 * width :],
         stream_routed[None],
         kernel_grad,
-        jnp.concatenate([in_part, out_part], 1).astype(jnp.float32),
+        jnp.concatenate([in_part, out_part], 1),
     )
 
 

time: 483 us -> 235 us (0.49)
  waiting for transfers between devices: 343 us -> 71.2 us
  starting transfers between devices: 36.5 us -> 50.1 us
  between operations: 15.6 us -> 2.1 us
  other arithmetic: 27 us -> 37.1 us
  local copies, waits for them, and re-layouts: 30.1 us -> 37.5 us
  matrix products: 28.9 us -> 35 us
    reduce_scatter x2 -> x0, waiting for transfers between devices: 156 us -> none  [the longest x1 137 us: per_device(): lax.psum_scatter(transposed_times(mixed, stream_out).astype(jnp.bfloat16)...]
    psum x1 -> x0, waiting for transfers between devices: 126 us -> none  [per_device(): kernel_grad = lax.psum(tap_sums(conv_grad, padded, table), ('dp', 'seq'))]
    ppermute x0 -> x15, waiting for transfers between devices: none -> 59.2 us  [swapped(): lax.ppermute(cells, axis, [(i, i ^ 1 << bit) for i in range(lax.axis_size...]
    ppermute x0 -> x15, starting transfers between devices: none -> 17.4 us  [swapped(): lax.ppermute(cells, axis, [(i, i ^ 1 << bit) for i in range(lax.axis_size...]
    all_to_all x2, waiting for transfers between devices: 16.5 us -> 0.01 us  [route(): lax.all_to_all(matrix, 'dp', split_axis=0, concat_axis=0, tiled=True)]
    all_to_all x2, waiting for transfers between devices: 20.5 us -> 6.04 us  [route(): lax.all_to_all(arranged.reshape(rows, width), 'dp', split_axis=0, concat_...]
    ppermute x1, waiting for transfers between devices: 12.6 us -> 0.01 us  [returned(): lax.ppermute(parts[step].astype(jnp.bfloat16), axis, [(i, (i + step) % co...]
    add x0 -> x13, other arithmetic: none -> 8.96 us  [the longest x5 6.61 us: reduced_everywhere(): cells = cells + swapped(cells, axis, bit)]
  transfers between devices with their start and end apart: 13 -> 25, of which waited for: 11 -> 9; matrix products, arithmetic and copies ran while one was open for 12% -> 33% of each run, Pallas kernels for 0% -> 0%
where the time goes in v2:
time: 235 us; the launch traced here: 233 us
  waiting for transfers between devices  71.2 us (30%)
  starting transfers between devices  50.1 us (21%)
  local copies, waits for them, and re-layouts  37.5 us (16%)
  other arithmetic  37.1 us (16%)
  matrix products  35 us (15%)
    ppermute x15, waiting for transfers between devices, swapped(): lax.ppermute(cells, axis, [(i, i ^ 1 << bit) for i in range(lax.axis_size...  59.2 us
    ppermute x15, starting transfers between devices, swapped(): lax.ppermute(cells, axis, [(i, i ^ 1 << bit) for i in range(lax.axis_size...  17.4 us
    ppermute x2, starting transfers between devices, extended(): lax.ppermute(tail, axis, [(i, (i + 1) % count) for i in range(ends)])  10.3 us
    all_to_all x2, starting transfers between devices, route(): lax.all_to_all(matrix, 'dp', split_axis=0, concat_axis=0, tiled=True)  8.65 us
    all_to_all x2, starting transfers between devices, route(): lax.all_to_all(arranged.reshape(rows, width), 'dp', split_axis=0, concat_...  8.17 us
    dot_general x4, matrix products, transposed_times(): lax.dot_general(left, right, (((0,), (0,)), ((), ())), preferred_element_...  7.18 us
    another operation x3, other arithmetic  6.64 us
    add x5, other arithmetic, reduced_everywhere(): cells = cells + swapped(cells, axis, bit)  6.61 us
  transfers between devices with their start and end apart: 25, of which 9 were waited for; matrix products, arithmetic and copies ran while one was open for 33% of the time, Pallas kernels for 0%

profile of v2, /device:TPU:0, one launch (start us, length us, event | category | flops | bytes accessed | tf_op | source)
XLA Modules:
  0.0 232.9 jit_solution(13519582075816495410)
XLA Ops:
  2.7 3.0 %collective-permute-start = (bf16[128,2048]{1,0:T(8,128)(2,1)}, bf16[128,2048]{1,0:T(8,128)(2,1)}, u32[]{:S(2)}, u32[]{:S(2)}) collective-permute-start(bf16[128,2048]{1,0:T(8,128)(2,1)} %pad_maximum_fusion.3), channel_id=1, source_target_pairs={{1,0},{0,1},{3,2},{2,3},{5,4},{4,5},{7,6},{6,7},{9,8},{8,9},{11,10... | collective-permute-start | bytes 1572872 | tf_op jit(solution)/shard_map/ppermute | solution.py:108
  13.2 4.7 %collective-permute-done = bf16[128,2048]{1,0:T(8,128)(2,1)} collective-permute-done((bf16[128,2048]{1,0:T(8,128)(2,1)}, bf16[128,2048]{1,0:T(8,128)(2,1)}, u32[]{:S(2)}, u32[]{:S(2)}) %collective-permute-start) | collective-permute-done | bytes 524320 | tf_op jit(solution)/shard_map/ppermute | solution.py:108
  26.2 2.6 %convolution_convert_fusion.2 = bf16[16,128,64]{1,2,0:T(8,128)(2,1)S(1)} fusion(bf16[16,256,64]{1,2,0:T(8,128)(2,1)} %bitcast.337, f32[16,128]{1,0:T(8,128)S(1)} %broadcast_divide_fusion, f32[16,256,128]{2,1,0:T(8,128)} %fusion.269, pred[128,256]{0,1:T(8,128)(4,1)S(1)} %broadcast_compare_fusion), kind=kOutput, calls=%fused_computation.50 | convolution fusion | flops 69863680 | bytes 2924544 | tf_op jit(solution)/shard_map/hqk,hke->hqe/dot_general | solution.py:227
  31.4 3.0 %fusion.204 = f32[128,2048]{1,0:T(8,128)S(1)} fusion(bf16[1024,2048]{1,0:T(8,128)(2,1)} %param.19, f32[128,1024]{1,0:T(8,128)S(1)} %get-tuple-element.157, f32[1024]{0:T(1024)S(1)} %copy-done.36, f32[128]{0:T(128)S(1)} %add_rsqrt_fusion.1, f32[128]{0:T(128)S(1)} %broadcast_multiply_fusion.5), kind=kOutput, calls=%fused_computation.373 | convolution fusion | flops 537395200 | bytes 5772288 | tf_op jit(solution)/shard_map/dot_general | solution.py:235
  37.4 4.5 %collective-permute-start.1 = (bf16[15,1024]{1,0:T(8,128)(2,1)}, bf16[15,1024]{1,0:T(8,128)(2,1)S(1)}, u32[]{:S(2)}, u32[]{:S(2)}) collective-permute-start(bf16[15,1024]{1,0:T(8,128)(2,1)} %get-tuple-element.59), channel_id=1, source_target_pairs={{0,1},{2,3},{4,5},{6,7},{8,9},{10,11},{12,13},{14,15},{16,17},{18,... | collective-permute-start | bytes 92168 | tf_op jit(solution)/shard_map/ppermute | solution.py:21
  44.0 4.1 %fusion.262 = (f32[128]{0:T(128)S(1)}, f32[128,1024]{1,0:T(8,128)S(1)}) fusion(f32[128]{0:T(128)} %get-tuple-element.93, bf16[15,1024]{1,0:T(8,128)(2,1)S(1)} %collective-permute-done.2, bf16[128,1024]{1,0:T(8,128)(2,1)S(1)} %multiply_convert_fusion.5, f32[1024]{0:T(1024)S(1)} %bitcast.383, f32[128]{0:T(128)} %get-tuple-element.94, f32[1024]{0:T(1024)S(1)} %bitcast.385, ...), kind=kLoop, calls=%fused_computation.556 | loop fusion | flops 28049280 | bytes 991232 | tf_op jit(solution)/shard_map/reduce_sum | solution.py:31
  54.5 5.7 %collective-permute-start.3 = (bf16[15,1024]{1,0:T(8,128)(2,1)}, bf16[15,1024]{1,0:T(8,128)(2,1)}, u32[]{:S(2)}, u32[]{:S(2)}) collective-permute-start(bf16[15,1024]{1,0:T(8,128)(2,1)} %get-tuple-element.57), channel_id=1, source_target_pairs={{0,1},{2,3},{4,5},{6,7},{8,9},{10,11},{12,13},{14,15},{16,17},{18,... | collective-permute-start | bytes 92168 | tf_op jit(solution)/shard_map/ppermute | solution.py:21
  63.7 4.1 %stack.255 = f32[31,1024]{1,0:T(8,128)} concatenate(f32[1,1024]{1,0:T(1,128)S(1)} %bitcast.441, f32[1,1024]{1,0:T(1,128)S(1)} %bitcast.440, f32[1,1024]{1,0:T(1,128)S(1)} %bitcast.439, f32[1,1024]{1,0:T(1,128)} %bitcast.447, f32[1,1024]{1,0:T(1,128)} %bitcast.446, f32[1,1024]{1,0:T(1,128)} %bitcast.445, f32[1,1024]{1,0:T(1,128)} %bitcast.444, f32[1,1024]{1,0:T(1,128)} %bitcast.443, ...), dimensions={0} | concatenate | bytes 253952 | tf_op jit(solution)/shard_map/stack | solution.py:74
  74.4 4.5 %multiply_convert_fusion.4 = (bf16[128,1024]{1,0:T(8,128)(2,1)S(1)}, f32[128,1024]{1,0:T(8,128)S(1)}) fusion(f32[128,2048]{1,0:T(8,128)S(1)} %copy-done.3, f32[128]{0:T(128)} %get-tuple-element.93, f32[158,1024]{1,0:T(8,128)S(1)} %maximum_convert_fusion, f32[1024]{0:T(1024)} %bitcast.390, f32[128]{0:T(128)} %get-tuple-element.94, f32[1024]{0:T(1024)S(1)} %bitcast.366, ...), kind=kLoop, calls=%fused_computation.361 | loop fusion | flops 12713984 | bytes 17706496 | tf_op jit(solution)/shard_map/convert.33
  81.8 2.5 %convolution_convert_fusion.3 = bf16[128,1024]{1,0:T(8,128)(2,1)} fusion(bf16[128,1024]{1,0:T(8,128)(2,1)} %add_convert_fusion, bf16[1024,1024]{1,0:T(8,128)(2,1)S(1)} %copy-done.5), kind=kOutput, calls=%fused_computation.51 | convolution fusion | flops 268566528 | bytes 2621440 | tf_op jit(solution)/shard_map/dot_general | solution.py:86
  90.6 3.4 %fusion.203 = f32[16,256,64]{1,2,0:T(8,128)} fusion(bf16[16,128,64]{1,2,0:T(8,128)(2,1)S(1)} %bitcast.344, f32[16,128]{1,0:T(8,128)S(1)} %broadcast_divide_fusion, f32[16,256,128]{2,1,0:T(8,128)} %fusion.269, pred[128,256]{0,1:T(8,128)(4,1)} %copy-done.35), kind=kOutput, calls=%fused_computation.371 | convolution fusion | flops 69732608 | bytes 3448832 | tf_op jit(solution)/shard_map/hqk,hqe->hke/dot_general | solution.py:283
  95.6 2.6 %copy.54 = f32[256,1024]{1,0:T(8,128)} copy(f32[256,1024]{0,1:T(8,128)} %bitcast.328) | data formatting | bytes 2097152 | tf_op jit(solution)/shard_map/reshape | solution.py:102
  103.4 5.0 %all-to-all-start.2 = ((bf16[16,8,1024]{2,1,0:T(8,128)(2,1)}), bf16[16,8,1024]{2,1,0:T(8,128)(2,1)}, u32[]{:S(2)}, u32[]{:S(2)}) async-start(bf16[16,8,1024]{2,1,0:T(8,128)(2,1)} %bitcast.122), calls=%async_computation.2 | async-start | bytes 524288 | tf_op jit(solution)/shard_map/all_to_all | solution.py:129
  114.0 6.0 %collective-permute-done.8 = f32[31,1024]{1,0:T(8,128)S(1)} collective-permute-done((f32[31,1024]{1,0:T(8,128)S(1)}, f32[31,1024]{1,0:T(8,128)S(1)}, u32[]{:S(2)}, u32[]{:S(2)}) %collective-permute-start.8) | collective-permute-done | bytes 127008 | tf_op jit(solution)/shard_map/ppermute | solution.py:147
  130.6 2.6 %collective-permute-start.10 = (f32[31,1024]{1,0:T(8,128)}, f32[31,1024]{1,0:T(8,128)}, u32[]{:S(2)}, u32[]{:S(2)}) collective-permute-start(f32[31,1024]{1,0:T(8,128)} %add.410), channel_id=1, source_target_pairs={{0,16},{2,18},{4,20},{6,22},{8,24},{10,26},{12,28},{14,30},{16,0},... | collective-permute-start | bytes 380936 | tf_op jit(solution)/shard_map/ppermute | solution.py:147
  135.5 4.2 %all-to-all-start.3 = ((bf16[16,8,1024]{2,1,0:T(8,128)(2,1)}), bf16[16,8,1024]{2,1,0:T(8,128)(2,1)}, u32[]{:S(2)}, u32[]{:S(2)}) async-start(bf16[16,8,1024]{2,1,0:T(8,128)(2,1)} %gather_fusion.1), calls=%async_computation.3 | async-start | bytes 524288 | tf_op jit(solution)/shard_map/all_to_all | solution.py:131
  143.7 6.0 %all-to-all-done.3 = bf16[16,8,1024]{2,1,0:T(8,128)(2,1)} async-done(((bf16[16,8,1024]{2,1,0:T(8,128)(2,1)}), bf16[16,8,1024]{2,1,0:T(8,128)(2,1)}, u32[]{:S(2)}, u32[]{:S(2)}) %all-to-all-start.3) | async-done | bytes 262176 | tf_op jit(solution)/shard_map/all_to_all | solution.py:131
  149.7 3.6 %all-to-all-start = ((bf16[16,8,3072]{2,1,0:T(8,128)(2,1)}), bf16[16,8,3072]{2,1,0:T(8,128)(2,1)S(1)}, u32[]{:S(2)}, u32[]{:S(2)}) async-start(bf16[16,8,3072]{2,1,0:T(8,128)(2,1)} %pad_maximum_fusion.2), calls=%async_computation | async-start | bytes 1572864 | tf_op jit(solution)/shard_map/all_to_all | solution.py:129
  159.3 17.2 %collective-permute-done.17 = bf16[256,1024]{1,0:T(8,128)(2,1)S(1)} collective-permute-done((bf16[256,1024]{1,0:T(8,128)(2,1)S(1)}, bf16[256,1024]{1,0:T(8,128)(2,1)S(1)}, u32[]{:S(2)}, u32[]{:S(2)}) %collective-permute-start.17) | collective-permute-done | bytes 524320 | tf_op jit(solution)/shard_map/ppermute | solution.py:147
  177.2 10.1 %collective-permute-done.12 = bf16[256,1024]{1,0:T(8,128)(2,1)S(1)} collective-permute-done((bf16[256,1024]{1,0:T(8,128)(2,1)S(1)}, bf16[256,1024]{1,0:T(8,128)(2,1)S(1)}, u32[]{:S(2)}, u32[]{:S(2)}) %collective-permute-start.12) | collective-permute-done | bytes 524320 | tf_op jit(solution)/shard_map/ppermute | solution.py:147
  190.7 4.5 %collective-permute-done.13 = bf16[128,1024]{1,0:T(8,128)(2,1)S(1)} collective-permute-done((bf16[128,1024]{1,0:T(8,128)(2,1)S(1)}, bf16[128,1024]{1,0:T(8,128)(2,1)S(1)}, u32[]{:S(2)}, u32[]{:S(2)}) %collective-permute-start.13) | collective-permute-done | bytes 262176 | tf_op jit(solution)/shard_map/ppermute | solution.py:147
  199.1 4.0 %all-to-all-start.1 = ((bf16[16,8,3072]{2,1,0:T(8,128)(2,1)}), bf16[16,8,3072]{2,1,0:T(8,128)(2,1)S(1)}, u32[]{:S(2)}, u32[]{:S(2)}) async-start(bf16[16,8,3072]{2,1,0:T(8,128)(2,1)} %gather_fusion), calls=%async_computation.1 | async-start | bytes 1572864 | tf_op jit(solution)/shard_map/all_to_all | solution.py:131
  204.1 2.9 %collective-permute-start.20 = (bf16[32,1024]{1,0:T(8,128)(2,1)S(1)}, bf16[32,1024]{1,0:T(8,128)(2,1)S(1)}, u32[]{:S(2)}, u32[]{:S(2)}) collective-permute-start(bf16[32,1024]{1,0:T(8,128)(2,1)S(1)} %fusion.245), channel_id=1, source_target_pairs={{0,16},{2,18},{4,20},{6,22},{8,24},{10,26},{12,28},{14,30},{16,0},... | collective-permute-start | bytes 196616 | tf_op jit(solution)/shard_map/ppermute | solution.py:147
  208.2 20.6 %collective-permute-done.20 = bf16[32,1024]{1,0:T(8,128)(2,1)S(1)} collective-permute-done((bf16[32,1024]{1,0:T(8,128)(2,1)S(1)}, bf16[32,1024]{1,0:T(8,128)(2,1)S(1)}, u32[]{:S(2)}, u32[]{:S(2)}) %collective-permute-start.20) | collective-permute-done | bytes 65568 | tf_op jit(solution)/shard_map/ppermute | solution.py:147
  (279 shorter events, 99.5 us)
Async XLA Ops:
  2.7 15.2 %collective-permute-start = (bf16[128,2048]{1,0:T(8,128)(2,1)}, bf16[128,2048]{1,0:T(8,128)(2,1)}, u32[]{:S(2)}, u32[]{:S(2)}) collective-permute-start(bf16[128,2048]{1,0:T(8,128)(2,1)} %pad_maximum_fusion.3), channel_id=1, source_target_pairs={{1,0},{0,1},{3,2},{2,3},{5,4},{4,5},{7,6},{6,7},{9,8},{8,9},{11,10... | collective-permute-start | bytes 1572872 | tf_op jit(solution)/shard_map/ppermute | solution.py:108
  36.1 6.4 %collective-permute-start.2 = (bf16[15,1024]{1,0:T(8,128)(2,1)}, bf16[15,1024]{1,0:T(8,128)(2,1)S(1)}, u32[]{:S(2)}, u32[]{:S(2)}) collective-permute-start(bf16[15,1024]{1,0:T(8,128)(2,1)} %get-tuple-element.60), channel_id=1, source_target_pairs={{1,0},{3,2},{5,4},{7,6},{9,8},{11,10},{13,12},{15,14},{17,16},{19,... | collective-permute-start | bytes 92168 | tf_op jit(solution)/shard_map/ppermute | solution.py:23
  53.3 20.2 %collective-permute-start.4 = (bf16[15,1024]{1,0:T(8,128)(2,1)}, bf16[15,1024]{1,0:T(8,128)(2,1)}, u32[]{:S(2)}, u32[]{:S(2)}) collective-permute-start(bf16[15,1024]{1,0:T(8,128)(2,1)} %get-tuple-element.58), channel_id=1, source_target_pairs={{1,0},{3,2},{5,4},{7,6},{9,8},{11,10},{13,12},{15,14},{17,16},{19,... | collective-permute-start | bytes 92168 | tf_op jit(solution)/shard_map/ppermute | solution.py:23
  54.5 18.9 %collective-permute-start.3 = (bf16[15,1024]{1,0:T(8,128)(2,1)}, bf16[15,1024]{1,0:T(8,128)(2,1)}, u32[]{:S(2)}, u32[]{:S(2)}) collective-permute-start(bf16[15,1024]{1,0:T(8,128)(2,1)} %get-tuple-element.57), channel_id=1, source_target_pairs={{0,1},{2,3},{4,5},{6,7},{8,9},{10,11},{12,13},{14,15},{16,17},{18,... | collective-permute-start | bytes 92168 | tf_op jit(solution)/shard_map/ppermute | solution.py:21
  67.8 30.3 %collective-permute-start.6 = (f32[31,1024]{1,0:T(8,128)}, f32[31,1024]{1,0:T(8,128)}, u32[]{:S(2)}, u32[]{:S(2)}) collective-permute-start(f32[31,1024]{1,0:T(8,128)} %stack.255), channel_id=1, source_target_pairs={{0,2},{2,0},{4,6},{6,4},{8,10},{10,8},{12,14},{14,12},{16,18},{18,... | collective-permute-start | bytes 380936 | tf_op jit(solution)/shard_map/ppermute | solution.py:147
  73.0 80.4 %collective-permute-start.16 = (bf16[512,1024]{1,0:T(8,128)(2,1)}, bf16[512,1024]{1,0:T(8,128)(2,1)}, u32[]{:S(2)}, u32[]{:S(2)}) collective-permute-start(bf16[512,1024]{1,0:T(8,128)(2,1)} %convolution_convert_fusion), channel_id=1, source_target_pairs={{0,2},{2,0},{4,6},{6,4},{8,10},{10,8},{12,14},{14,12},{16,18},{18,... | collective-permute-start | bytes 3145736 | tf_op jit(solution)/shard_map/ppermute | solution.py:147
  99.8 8.7 %collective-permute-start.7 = (f32[31,1024]{1,0:T(8,128)}, f32[31,1024]{1,0:T(8,128)}, u32[]{:S(2)}, u32[]{:S(2)}) collective-permute-start(f32[31,1024]{1,0:T(8,128)} %add.407), channel_id=1, source_target_pairs={{0,4},{2,6},{4,0},{6,2},{8,12},{10,14},{12,8},{14,10},{16,20},{18,... | collective-permute-start | bytes 380936 | tf_op jit(solution)/shard_map/ppermute | solution.py:147
  103.4 36.3 %collective-permute-start.5 = (bf16[128,2048]{1,0:T(8,128)(2,1)}, bf16[128,2048]{1,0:T(8,128)(2,1)}, u32[]{:S(2)}, u32[]{:S(2)}) collective-permute-start(bf16[128,2048]{1,0:T(8,128)(2,1)} %fusion.8), channel_id=1, source_target_pairs={{0,1},{1,0},{2,3},{3,2},{4,5},{5,4},{6,7},{7,6},{8,9},{9,8},{10,11... | collective-permute-start | bytes 1572872 | tf_op jit(solution)/shard_map/ppermute | solution.py:117
  103.4 29.7 %all-to-all-start.2 = ((bf16[16,8,1024]{2,1,0:T(8,128)(2,1)}), bf16[16,8,1024]{2,1,0:T(8,128)(2,1)}, u32[]{:S(2)}, u32[]{:S(2)}) async-start(bf16[16,8,1024]{2,1,0:T(8,128)(2,1)} %bitcast.122), calls=%async_computation.2 | async-start | bytes 524288 | tf_op jit(solution)/shard_map/all_to_all | solution.py:129
  109.5 10.5 %collective-permute-start.8 = (f32[31,1024]{1,0:T(8,128)S(1)}, f32[31,1024]{1,0:T(8,128)S(1)}, u32[]{:S(2)}, u32[]{:S(2)}) collective-permute-start(f32[31,1024]{1,0:T(8,128)S(1)} %add.408), channel_id=1, source_target_pairs={{0,1},{1,0},{2,3},{3,2},{4,5},{5,4},{6,7},{7,6},{8,9},{9,8},{10,11... | collective-permute-start | bytes 380936 | tf_op jit(solution)/shard_map/ppermute | solution.py:147
  120.6 8.3 %collective-permute-start.9 = (f32[31,1024]{1,0:T(8,128)}, f32[31,1024]{1,0:T(8,128)}, u32[]{:S(2)}, u32[]{:S(2)}) collective-permute-start(f32[31,1024]{1,0:T(8,128)} %add.409), channel_id=1, source_target_pairs={{0,8},{2,10},{4,12},{6,14},{8,0},{10,2},{12,4},{14,6},{16,24},{18,... | collective-permute-start | bytes 380936 | tf_op jit(solution)/shard_map/ppermute | solution.py:147
  128.9 28.2 %collective-permute-start.11 = (bf16[512,1024]{1,0:T(8,128)(2,1)}, bf16[512,1024]{1,0:T(8,128)(2,1)}, u32[]{:S(2)}, u32[]{:S(2)}) collective-permute-start(bf16[512,1024]{1,0:T(8,128)(2,1)} %convolution_convert_fusion.1), channel_id=1, source_target_pairs={{0,2},{2,0},{4,6},{6,4},{8,10},{10,8},{12,14},{14,12},{16,18},{18,... | collective-permute-start | bytes 3145736 | tf_op jit(solution)/shard_map/ppermute | solution.py:147
  130.6 11.5 %collective-permute-start.10 = (f32[31,1024]{1,0:T(8,128)}, f32[31,1024]{1,0:T(8,128)}, u32[]{:S(2)}, u32[]{:S(2)}) collective-permute-start(f32[31,1024]{1,0:T(8,128)} %add.410), channel_id=1, source_target_pairs={{0,16},{2,18},{4,20},{6,22},{8,24},{10,26},{12,28},{14,30},{16,0},... | collective-permute-start | bytes 380936 | tf_op jit(solution)/shard_map/ppermute | solution.py:147
  135.5 14.2 %all-to-all-start.3 = ((bf16[16,8,1024]{2,1,0:T(8,128)(2,1)}), bf16[16,8,1024]{2,1,0:T(8,128)(2,1)}, u32[]{:S(2)}, u32[]{:S(2)}) async-start(bf16[16,8,1024]{2,1,0:T(8,128)(2,1)} %gather_fusion.1), calls=%async_computation.3 | async-start | bytes 524288 | tf_op jit(solution)/shard_map/all_to_all | solution.py:131
  149.7 47.8 %all-to-all-start = ((bf16[16,8,3072]{2,1,0:T(8,128)(2,1)}), bf16[16,8,3072]{2,1,0:T(8,128)(2,1)S(1)}, u32[]{:S(2)}, u32[]{:S(2)}) async-start(bf16[16,8,3072]{2,1,0:T(8,128)(2,1)} %pad_maximum_fusion.2), calls=%async_computation | async-start | bytes 1572864 | tf_op jit(solution)/shard_map/all_to_all | solution.py:129
  155.1 21.5 %collective-permute-start.17 = (bf16[256,1024]{1,0:T(8,128)(2,1)S(1)}, bf16[256,1024]{1,0:T(8,128)(2,1)S(1)}, u32[]{:S(2)}, u32[]{:S(2)}) collective-permute-start(bf16[256,1024]{1,0:T(8,128)(2,1)S(1)} %bitcast.359), channel_id=1, source_target_pairs={{0,4},{2,6},{4,0},{6,2},{8,12},{10,14},{12,8},{14,10},{16,20},{18,... | collective-permute-start | bytes 1572872 | tf_op jit(solution)/shard_map/ppermute | solution.py:147
  158.9 28.3 %collective-permute-start.12 = (bf16[256,1024]{1,0:T(8,128)(2,1)S(1)}, bf16[256,1024]{1,0:T(8,128)(2,1)S(1)}, u32[]{:S(2)}, u32[]{:S(2)}) collective-permute-start(bf16[256,1024]{1,0:T(8,128)(2,1)S(1)} %bitcast.360), channel_id=1, source_target_pairs={{0,4},{2,6},{4,0},{6,2},{8,12},{10,14},{12,8},{14,10},{16,20},{18,... | collective-permute-start | bytes 1572872 | tf_op jit(solution)/shard_map/ppermute | solution.py:147
  176.8 11.0 %collective-permute-start.18 = (bf16[128,1024]{1,0:T(8,128)(2,1)S(1)}, bf16[128,1024]{1,0:T(8,128)(2,1)S(1)}, u32[]{:S(2)}, u32[]{:S(2)}) collective-permute-start(bf16[128,1024]{1,0:T(8,128)(2,1)S(1)} %bitcast.363), channel_id=1, source_target_pairs={{0,1},{1,0},{2,3},{3,2},{4,5},{5,4},{6,7},{7,6},{8,9},{9,8},{10,11... | collective-permute-start | bytes 786440 | tf_op jit(solution)/shard_map/ppermute | solution.py:147
  187.4 7.8 %collective-permute-start.13 = (bf16[128,1024]{1,0:T(8,128)(2,1)S(1)}, bf16[128,1024]{1,0:T(8,128)(2,1)S(1)}, u32[]{:S(2)}, u32[]{:S(2)}) collective-permute-start(bf16[128,1024]{1,0:T(8,128)(2,1)S(1)} %bitcast.364), channel_id=1, source_target_pairs={{0,1},{1,0},{2,3},{3,2},{4,5},{5,4},{6,7},{7,6},{8,9},{9,8},{10,11... | collective-permute-start | bytes 786440 | tf_op jit(solution)/shard_map/ppermute | solution.py:147
  188.5 14.6 %collective-permute-start.19 = (bf16[64,1024]{1,0:T(8,128)(2,1)}, bf16[64,1024]{1,0:T(8,128)(2,1)S(1)}, u32[]{:S(2)}, u32[]{:S(2)}) collective-permute-start(bf16[64,1024]{1,0:T(8,128)(2,1)} %bitcast.182), channel_id=1, source_target_pairs={{0,8},{2,10},{4,12},{6,14},{8,0},{10,2},{12,4},{14,6},{16,24},{18,... | collective-permute-start | bytes 393224 | tf_op jit(solution)/shard_map/ppermute | solution.py:147
  196.0 11.1 %collective-permute-start.14 = (bf16[64,1024]{1,0:T(8,128)(2,1)}, bf16[64,1024]{1,0:T(8,128)(2,1)}, u32[]{:S(2)}, u32[]{:S(2)}) collective-permute-start(bf16[64,1024]{1,0:T(8,128)(2,1)} %bitcast.167), channel_id=1, source_target_pairs={{0,8},{2,10},{4,12},{6,14},{8,0},{10,2},{12,4},{14,6},{16,24},{18,... | collective-permute-start | bytes 393224 | tf_op jit(solution)/shard_map/ppermute | solution.py:147
  199.1 31.2 %all-to-all-start.1 = ((bf16[16,8,3072]{2,1,0:T(8,128)(2,1)}), bf16[16,8,3072]{2,1,0:T(8,128)(2,1)S(1)}, u32[]{:S(2)}, u32[]{:S(2)}) async-start(bf16[16,8,3072]{2,1,0:T(8,128)(2,1)} %gather_fusion), calls=%async_computation.1 | async-start | bytes 1572864 | tf_op jit(solution)/shard_map/all_to_all | solution.py:131
  204.1 24.6 %collective-permute-start.20 = (bf16[32,1024]{1,0:T(8,128)(2,1)S(1)}, bf16[32,1024]{1,0:T(8,128)(2,1)S(1)}, u32[]{:S(2)}, u32[]{:S(2)}) collective-permute-start(bf16[32,1024]{1,0:T(8,128)(2,1)S(1)} %fusion.245), channel_id=1, source_target_pairs={{0,16},{2,18},{4,20},{6,22},{8,24},{10,26},{12,28},{14,30},{16,0},... | collective-permute-start | bytes 196616 | tf_op jit(solution)/shard_map/ppermute | solution.py:147
  208.0 21.6 %collective-permute-start.15 = (bf16[32,1024]{1,0:T(8,128)(2,1)S(1)}, bf16[32,1024]{1,0:T(8,128)(2,1)S(1)}, u32[]{:S(2)}, u32[]{:S(2)}) collective-permute-start(bf16[32,1024]{1,0:T(8,128)(2,1)S(1)} %fusion.244), channel_id=1, source_target_pairs={{0,16},{2,18},{4,20},{6,22},{8,24},{10,26},{12,28},{14,30},{16,0},... | collective-permute-start | bytes 196616 | tf_op jit(solution)/shard_map/ppermute | solution.py:147
  (75 other events, 977.7 us)

commit v3 on v1

--- a/solution.py
+++ b/solution.py
@@ -123,14 +123,87 @@
     return total
 
 
+def spread_rows(matrix):
+    return lax.all_to_all(matrix, "dp", split_axis=0, concat_axis=0, tiled=True)
+
+
+def collected(spread, plan):
+    rows, width = spread.shape
+    arranged = jnp.take(spread.reshape(plan.shape[0], -1, width), plan, axis=0, mode="clip")
+    return spread_rows(arranged.reshape(rows, width))
+
+
 def route(matrix, plan):
-    rows, width = matrix.shape
-    slots = plan.shape[0]
-    spread = lax.all_to_all(matrix, "dp", split_axis=0, concat_axis=0, tiled=True)
-    arranged = jnp.take(spread.reshape(slots, -1, width), plan, axis=0, mode="clip")
-    return lax.all_to_all(
-        arranged.reshape(rows, width), "dp", split_axis=0, concat_axis=0, tiled=True
-    )
+    return collected(spread_rows(matrix), plan)
+
+
+def exchange_order():
+    slots = (lax.axis_size("dp") - 1).bit_length()
+    seqs = (lax.axis_size("seq") - 1).bit_length()
+    return (
+        [("dp", bit, seqs + bit) for bit in range(min(1, slots))]
+        + [("seq", bit, bit) for bit in range(seqs)]
+        + [("dp", bit, seqs + bit) for bit in range(1, slots)]
+    )
+
+
+def swapped(cells, axis, bit):
+    return lax.ppermute(
+        cells, axis, [(i, i ^ (1 << bit)) for i in range(lax.axis_size(axis))]
+    )
+
+
+def half_of(cells, dim, low, which):
+    shape = cells.shape
+    split = cells.reshape(shape[:dim] + (-1, 2, low) + shape[dim + 1 :])
+    chosen = lax.dynamic_index_in_dim(split, which, dim + 1, keepdims=False)
+    return chosen.reshape(shape[:dim] + (-1,) + shape[dim + 1 :])
+
+
+def joined(axis, bit, outgoing, extra):
+    outgoing = outgoing.astype(jnp.bfloat16)
+    if extra is None:
+        return swapped(outgoing, axis, bit).astype(jnp.float32), None
+    rounded = lax.reduce_precision(extra, 8, 7)
+    arrived = swapped(
+        jnp.concatenate([outgoing, rounded.astype(jnp.bfloat16)], 0), axis, bit
+    ).astype(jnp.float32)
+    count = outgoing.shape[0]
+    return arrived[:count], rounded + arrived[count:]
+
+
+class Reduction:
+    def __init__(self, left, right, extra=None):
+        self.order = exchange_order()
+        self.rows = left.shape[1] >> len(self.order)
+        self.positions = sorted(position for _, _, position in self.order)
+        self.extra = extra
+        axis, bit, low, mine = self.next_exchange()
+        outgoing = transposed_times(half_of(left, 1, low, 1 - mine), right)
+        arrived, self.extra = joined(axis, bit, outgoing, self.extra)
+        self.total = transposed_times(half_of(left, 1, low, mine), right) + arrived
+
+    def next_exchange(self):
+        axis, bit, position = self.order.pop(0)
+        low = self.rows << self.positions.index(position)
+        self.positions.remove(position)
+        return axis, bit, low, (lax.axis_index(axis) >> bit) & 1
+
+    def step(self):
+        if self.order:
+            axis, bit, low, mine = self.next_exchange()
+            outgoing = half_of(self.total, 0, low, 1 - mine)
+            arrived, self.extra = joined(axis, bit, outgoing, self.extra)
+            self.total = half_of(self.total, 0, low, mine) + arrived
+
+    def finish(self):
+        while self.order:
+            self.step()
+        return self.total
+
+    def tie(self, other):
+        self.total, other = lax.optimization_barrier((self.total, other))
+        return other
 
 
 def per_device(
@@ -195,18 +268,15 @@
     conv_out = depthwise(padded, kernel, table)
     normed_out, hat_out, inv_out = layer_norm(conv_out, conv_gain)
     activated = (normed_out * jax.nn.sigmoid(normed_out)).astype(jnp.bfloat16)
-    out_part = lax.psum_scatter(
-        transposed_times(activated, grad_rows).astype(jnp.bfloat16),
-        ("dp", "seq"),
-        scatter_dimension=0,
-        tiled=True,
-    )
+    out_sum = Reduction(activated, grad_rows)
     act_grad = times_transposed(grad_rows, point_out)
     conv_grad = norm_backward(act_grad * swish_slope(normed_out), hat_out, inv_out, conv_gain)
     grad_padded = extended(conv_grad.astype(jnp.bfloat16), (("seq", 0),), reach).astype(
         conv_grad.dtype
     )
-    kernel_grad = lax.psum(tap_sums(conv_grad, padded, table), ("dp", "seq"))
+    tap_part = jnp.pad(tap_sums(conv_grad, padded, table), ((0, -taps % 16), (0, 0)))
+    grad_padded = out_sum.tie(grad_padded)
+    out_sum.step()
     in_grad = depthwise(grad_padded, kernel[::-1], table)
     both_grad = jnp.concatenate(
         [in_grad * logistic, in_grad * linear * logistic * (1.0 - logistic)], 1
@@ -215,19 +285,17 @@
     stream_out = (
         grad_rows.astype(jnp.float32) + norm_backward(back_in, hat_in, inv_in, norm_gain)
     ).astype(jnp.bfloat16)
-    in_part = lax.psum_scatter(
-        transposed_times(mixed, stream_out).astype(jnp.bfloat16),
-        ("dp", "seq"),
-        scatter_dimension=0,
-        tiled=True,
-    )
     mixed_grad = times_transposed(stream_out, attn_out).astype(jnp.bfloat16)
+    mixed_grad = out_sum.tie(mixed_grad)
+    out_sum.step()
     grad_heads = split_heads(mixed_grad)
     slope = jnp.einsum(
         "hqe,hke->hqk", grad_heads, value_heads, preferred_element_type=jnp.float32
     )
     delta = jnp.sum(weights * slope, -1, keepdims=True)
     score_grad = (weights * (slope - delta)).astype(jnp.bfloat16)
+    score_grad = out_sum.tie(score_grad)
+    out_sum.step()
     query_grad = merge_heads(
         (
             jnp.einsum("hqk,hke->hqe", score_grad, key_heads, preferred_element_type=jnp.float32)
@@ -245,15 +313,18 @@
     pair_grad = returned(
         [pair_part[step * frames : (step + 1) * frames] for step in range(seq_count)], "seq"
     ).astype(jnp.bfloat16)
-    stream_routed = route(stream_out, plan)
-    routed = route(jnp.concatenate([query_grad, pair_grad], 1), plan)
+    first_routed = route(jnp.concatenate([stream_out, query_grad], 1), plan)
+    in_sum = Reduction(mixed, stream_out, tap_part)
+    second_spread = in_sum.tie(spread_rows(pair_grad))
+    second_routed = collected(second_spread, plan)
+    in_part = in_sum.finish()
     return (
-        routed[None, :, :width],
-        routed[None, :, width : 2 * width],
-        routed[None, :, 2 * width :],
-        stream_routed[None],
-        kernel_grad,
-        jnp.concatenate([in_part, out_part], 1).astype(jnp.float32),
+        first_routed[None, :, width:],
+        second_routed[None, :, :width],
+        second_routed[None, :, width:],
+        first_routed[None, :, :width],
+        in_sum.extra[:taps],
+        jnp.concatenate([in_part, out_sum.finish()], 1),
     )
 
 

time: 483 us -> 216 us (0.45)
  waiting for transfers between devices: 343 us -> 65.7 us
  other arithmetic: 27 us -> 40.8 us
  starting transfers between devices: 36.5 us -> 49.5 us
  between operations: 15.6 us -> 2.92 us
    reduce_scatter x2 -> x0, waiting for transfers between devices: 156 us -> none  [the longest x1 137 us: per_device(): lax.psum_scatter(transposed_times(mixed, stream_out).astype(jnp.bfloat16)...]
    psum x1 -> x0, waiting for transfers between devices: 126 us -> none  [per_device(): kernel_grad = lax.psum(tap_sums(conv_grad, padded, table), ('dp', 'seq'))]
    ppermute x0 -> x10, waiting for transfers between devices: none -> 27.3 us  [swapped(): lax.ppermute(cells, axis, [(i, i ^ 1 << bit) for i in range(lax.axis_size...]
    ppermute x0 -> x10, starting transfers between devices: none -> 17.3 us  [swapped(): lax.ppermute(cells, axis, [(i, i ^ 1 << bit) for i in range(lax.axis_size...]
    all_to_all x4, waiting for transfers between devices: 37 us -> 19.9 us  [spread_rows(): return lax.all_to_all(matrix, 'dp', split_axis=0, concat_axis=0, tiled=True)]
    convert_element_type x2 -> x10, other arithmetic: 1.99 us -> 8.12 us  [the longest x5 5.2 us: joined(): arrived = swapped(jnp.concatenate([outgoing, rounded.astype(jnp.bfloat16)...]
    add x0 -> x9, other arithmetic: none -> 4.88 us  [the longest x8 4.2 us: step(): self.total = half_of(self.total, 0, low, mine) + arrived]
  transfers between devices with their start and end apart: 13 -> 20, of which waited for: 11 -> 11; matrix products, arithmetic and copies ran while one was open for 12% -> 22% of each run, Pallas kernels for 0% -> 0%
where the time goes in v3:
time: 216 us; the launch traced here: 214 us
  waiting for transfers between devices  65.7 us (30%)
  starting transfers between devices  49.5 us (23%)
  other arithmetic  40.8 us (19%)
  matrix products  29.9 us (14%)
  local copies, waits for them, and re-layouts  25.4 us (12%)
  between operations  2.92 us (1%)
    ppermute x10, waiting for transfers between devices, swapped(): lax.ppermute(cells, axis, [(i, i ^ 1 << bit) for i in range(lax.axis_size...  27.3 us
    all_to_all x4, waiting for transfers between devices, spread_rows(): return lax.all_to_all(matrix, 'dp', split_axis=0, concat_axis=0, tiled=True)  19.9 us
    all_to_all x4, starting transfers between devices, spread_rows(): return lax.all_to_all(matrix, 'dp', split_axis=0, concat_axis=0, tiled=True)  19.4 us
    ppermute x10, starting transfers between devices, swapped(): lax.ppermute(cells, axis, [(i, i ^ 1 << bit) for i in range(lax.axis_size...  17.3 us
    ppermute x1, waiting for transfers between devices, returned(): lax.ppermute(parts[step].astype(jnp.bfloat16), axis, [(i, (i + step) % co...  8.75 us
    reduce_sum x6, other arithmetic, tap_sums(): jnp.sum(upstream * padded[tap:tap + length].astype(jnp.float32) * table[:...  7.29 us
    dot_general x3, matrix products, times_transposed(): lax.dot_general(left, right, (((1,), (1,)), ((), ())), preferred_element_...  5.56 us
    ppermute x2, starting transfers between devices, extended(): lax.ppermute(tail, axis, [(i, (i + 1) % count) for i in range(ends)])  5.49 us
  transfers between devices with their start and end apart: 20, of which 11 were waited for; matrix products, arithmetic and copies ran while one was open for 22% of the time, Pallas kernels for 0%

profile of v3, /device:TPU:0, one launch (start us, length us, event | category | flops | bytes accessed | tf_op | source)
XLA Modules:
  0.0 214.2 jit_solution(5829816003235773299)
XLA Ops:
  1.9 3.1 %collective-permute-start = (bf16[128,2048]{1,0:T(8,128)(2,1)S(1)}, bf16[128,2048]{1,0:T(8,128)(2,1)}, u32[]{:S(2)}, u32[]{:S(2)}) collective-permute-start(bf16[128,2048]{1,0:T(8,128)(2,1)S(1)} %pad_maximum_fusion.4), channel_id=1, source_target_pairs={{1,0},{0,1},{3,2},{2,3},{5,4},{4,5},{7,6},{6,7},{9,8},{8,9},{11,10... | collective-permute-start | bytes 1572872 | tf_op jit(solution)/shard_map/ppermute | solution.py:108
  11.8 5.2 %collective-permute-done = bf16[128,2048]{1,0:T(8,128)(2,1)} collective-permute-done((bf16[128,2048]{1,0:T(8,128)(2,1)S(1)}, bf16[128,2048]{1,0:T(8,128)(2,1)}, u32[]{:S(2)}, u32[]{:S(2)}) %collective-permute-start) | collective-permute-done | bytes 524320 | tf_op jit(solution)/shard_map/ppermute | solution.py:108
  29.6 3.0 %fusion.149 = f32[128,2048]{1,0:T(8,128)S(1)} fusion(bf16[1024,2048]{1,0:T(8,128)(2,1)} %param.19, f32[128,1024]{1,0:T(8,128)S(1)} %get-tuple-element.178, f32[1024]{0:T(1024)S(1)} %copy-done.82, f32[128]{0:T(128)S(1)} %add_rsqrt_fusion.1, f32[128]{0:T(128)S(1)} %broadcast_multiply_fusion.5), kind=kOutput, calls=%fused_computation.289 | convolution fusion | flops 537395200 | bytes 5772288 | tf_op jit(solution)/shard_map/dot_general | solution.py:257
  34.4 3.6 %collective-permute-start.1 = (bf16[15,1024]{1,0:T(8,128)(2,1)}, bf16[15,1024]{1,0:T(8,128)(2,1)S(1)}, u32[]{:S(2)}, u32[]{:S(2)}) collective-permute-start(bf16[15,1024]{1,0:T(8,128)(2,1)} %get-tuple-element.80), channel_id=1, source_target_pairs={{0,1},{2,3},{4,5},{6,7},{8,9},{10,11},{12,13},{14,15},{16,17},{18,... | collective-permute-start | bytes 92168 | tf_op jit(solution)/shard_map/ppermute | solution.py:21
  39.9 4.1 %collective-permute-done.2 = bf16[15,1024]{1,0:T(8,128)(2,1)S(1)} collective-permute-done((bf16[15,1024]{1,0:T(8,128)(2,1)}, bf16[15,1024]{1,0:T(8,128)(2,1)S(1)}, u32[]{:S(2)}, u32[]{:S(2)}) %collective-permute-start.2) | collective-permute-done | bytes 30752 | tf_op jit(solution)/shard_map/ppermute | solution.py:23
  44.0 3.9 %fusion.219 = (f32[128]{0:T(128)S(1)}, f32[128,1024]{1,0:T(8,128)S(1)}) fusion(f32[128]{0:T(128)} %get-tuple-element.114, bf16[15,1024]{1,0:T(8,128)(2,1)S(1)} %collective-permute-done.2, bf16[128,1024]{1,0:T(8,128)(2,1)S(1)} %multiply_convert_fusion.5, f32[1024]{0:T(1024)S(1)} %bitcast.398, f32[128]{0:T(128)} %get-tuple-element.115, ...), kind=kLoop, calls=%fused_computation.491 | loop fusion | flops 28049280 | bytes 991232 | tf_op jit(solution)/shard_map/reduce_sum | solution.py:31
  49.1 3.1 %fusion.214 = (f32[128]{0:T(128)}, f32[128]{0:T(128)}, bf16[128,1024]{1,0:T(8,128)(2,1)}, f32[128,1024]{1,0:T(8,128)}) fusion(f32[128]{0:T(128)S(1)} %add_rsqrt_fusion, f32[128,1024]{1,0:T(8,128)S(1)} %get-tuple-element.65, f32[128]{0:T(128)S(1)} %broadcast_multiply_fusion.4, f32[1024]{0:T(1024)} %param.23, bf16[1024,1024]{1,0:T(8,128)(2,1)S(1)} %copy-done, ...), kind=kOutput, calls=%fused_computation.488 | convolution fusion | flops 270663424 | bytes 3676160 | tf_op jit(solution)/shard_map/dot_general | solution.py:86
  67.0 3.0 %multiply_convert_fusion.3 = (bf16[128,1024]{1,0:T(8,128)(2,1)S(1)}, f32[128,1024]{1,0:T(8,128)S(1)}) fusion(f32[128,2048]{1,0:T(8,128)S(1)} %copy-done.4, f32[128]{0:T(128)S(1)} %copy-done.91, f32[158,1024]{1,0:T(8,128)S(1)} %maximum_convert_fusion, f32[1024]{0:T(1024)S(1)} %bitcast.405, f32[128]{0:T(128)S(1)} %copy-done.93, f32[1024]{0:T(1024)S(1)} %bitcast.381, ...), kind=kLoop, calls=%fused_computation.274 | loop fusion | flops 12713984 | bytes 17706496 | tf_op jit(solution)/shard_map/convert.33
  75.9 10.9 %collective-permute-done.6 = bf16[256,1024]{1,0:T(8,128)(2,1)S(1)} collective-permute-done((bf16[256,1024]{1,0:T(8,128)(2,1)S(1)}, bf16[256,1024]{1,0:T(8,128)(2,1)S(1)}, u32[]{:S(2)}, u32[]{:S(2)}) %collective-permute-start.6) | collective-permute-done | bytes 524320 | tf_op jit(solution)/shard_map/ppermute | solution.py:151
  93.1 3.2 %multiply_convert_fusion = bf16[16,128,256]{1,2,0:T(8,128)(2,1)S(1)} fusion(f32[16,128,256]{1,2,0:T(8,128)} %get-tuple-element.176, f32[16,128]{1,0:T(8,128)S(1)} %copy-done.52, bf16[16,128,64]{1,2,0:T(8,128)(2,1)} %bitcast.351, bf16[16,256,64]{1,2,0:T(8,128)(2,1)S(1)} %bitcast.344), kind=kOutput, calls=%fused_computation.8 | convolution fusion | flops 137365760 | bytes 3940352 | tf_op jit(solution)/shard_map/sub | solution.py:296
  96.4 3.1 %collective-permute-done.7 = bf16[128,1024]{1,0:T(8,128)(2,1)} collective-permute-done((bf16[128,1024]{1,0:T(8,128)(2,1)}, bf16[128,1024]{1,0:T(8,128)(2,1)}, u32[]{:S(2)}, u32[]{:S(2)}) %collective-permute-start.7) | collective-permute-done | bytes 262176 | tf_op jit(solution)/shard_map/ppermute | solution.py:151
  110.5 8.8 %collective-permute-done.9 = bf16[128,2048]{1,0:T(8,128)(2,1)} collective-permute-done((bf16[128,2048]{1,0:T(8,128)(2,1)}, bf16[128,2048]{1,0:T(8,128)(2,1)}, u32[]{:S(2)}, u32[]{:S(2)}) %collective-permute-start.9) | collective-permute-done | bytes 524320 | tf_op jit(solution)/shard_map/ppermute | solution.py:117
  121.2 5.9 %all-to-all-start.2 = ((bf16[16,8,2048]{2,1,0:T(8,128)(2,1)}), bf16[16,8,2048]{2,1,0:T(8,128)(2,1)S(1)}, u32[]{:S(2)}, u32[]{:S(2)}) async-start(bf16[16,8,2048]{2,1,0:T(8,128)(2,1)} %fusion.141), calls=%async_computation.2 | async-start | bytes 1048576 | tf_op jit(solution)/shard_map/all_to_all | solution.py:127
  133.8 2.9 %convert_element_type.468 = f32[544,1024]{1,0:T(8,128)} convert(bf16[544,1024]{1,0:T(8,128)(2,1)} %collective-permute-done.8) | non-fusion elementwise | flops 557056 | bytes 3342336 | tf_op jit(solution)/shard_map/convert_element_type | solution.py:170
  136.7 5.3 %all-to-all-done.2 = bf16[16,8,2048]{2,1,0:T(8,128)(2,1)S(1)} async-done(((bf16[16,8,2048]{2,1,0:T(8,128)(2,1)}), bf16[16,8,2048]{2,1,0:T(8,128)(2,1)S(1)}, u32[]{:S(2)}, u32[]{:S(2)}) %all-to-all-start.2) | async-done | bytes 524320 | tf_op jit(solution)/shard_map/all_to_all | solution.py:127
  142.0 3.6 %all-to-all-start = ((bf16[16,8,2048]{2,1,0:T(8,128)(2,1)}), bf16[16,8,2048]{2,1,0:T(8,128)(2,1)S(1)}, u32[]{:S(2)}, u32[]{:S(2)}) async-start(bf16[16,8,2048]{2,1,0:T(8,128)(2,1)} %pad_maximum_fusion.5), calls=%async_computation | async-start | bytes 1048576 | tf_op jit(solution)/shard_map/all_to_all | solution.py:127
  151.3 2.9 %collective-permute-start.15 = (bf16[32,1024]{1,0:T(8,128)(2,1)S(1)}, bf16[32,1024]{1,0:T(8,128)(2,1)}, u32[]{:S(2)}, u32[]{:S(2)}) collective-permute-start(bf16[32,1024]{1,0:T(8,128)(2,1)S(1)} %fusion.197), channel_id=1, source_target_pairs={{0,16},{2,18},{4,20},{6,22},{8,24},{10,26},{12,28},{14,30},{16,0},... | collective-permute-start | bytes 196616 | tf_op jit(solution)/shard_map/ppermute | solution.py:151
  154.2 6.3 %all-to-all-done = bf16[16,8,2048]{2,1,0:T(8,128)(2,1)S(1)} async-done(((bf16[16,8,2048]{2,1,0:T(8,128)(2,1)}), bf16[16,8,2048]{2,1,0:T(8,128)(2,1)S(1)}, u32[]{:S(2)}, u32[]{:S(2)}) %all-to-all-start) | async-done | bytes 524320 | tf_op jit(solution)/shard_map/all_to_all | solution.py:127
  161.8 5.6 %all-to-all-start.1 = ((bf16[16,8,2048]{2,1,0:T(8,128)(2,1)}), bf16[16,8,2048]{2,1,0:T(8,128)(2,1)}, u32[]{:S(2)}, u32[]{:S(2)}) async-start(bf16[16,8,2048]{2,1,0:T(8,128)(2,1)} %gather_fusion), calls=%async_computation.1 | async-start | bytes 1048576 | tf_op jit(solution)/shard_map/all_to_all | solution.py:127
  173.9 9.3 %collective-permute-done.11 = bf16[160,1024]{1,0:T(8,128)(2,1)} collective-permute-done((bf16[160,1024]{1,0:T(8,128)(2,1)}, bf16[160,1024]{1,0:T(8,128)(2,1)}, u32[]{:S(2)}, u32[]{:S(2)}) %collective-permute-start.11) | collective-permute-done | bytes 327712 | tf_op jit(solution)/shard_map/ppermute | solution.py:151
  186.8 4.3 %all-to-all-start.3 = ((bf16[16,8,2048]{2,1,0:T(8,128)(2,1)}), bf16[16,8,2048]{2,1,0:T(8,128)(2,1)}, u32[]{:S(2)}, u32[]{:S(2)}) async-start(bf16[16,8,2048]{2,1,0:T(8,128)(2,1)} %gather_fusion.1), calls=%async_computation.3 | async-start | bytes 1048576 | tf_op jit(solution)/shard_map/all_to_all | solution.py:127
  194.9 2.8 %collective-permute-start.13 = (bf16[64,1024]{1,0:T(8,128)(2,1)S(1)}, bf16[64,1024]{1,0:T(8,128)(2,1)S(1)}, u32[]{:S(2)}, u32[]{:S(2)}) collective-permute-start(bf16[64,1024]{1,0:T(8,128)(2,1)S(1)} %pad_maximum_fusion.11), channel_id=1, source_target_pairs={{0,16},{2,18},{4,20},{6,22},{8,24},{10,26},{12,28},{14,30},{16,0},... | collective-permute-start | bytes 393224 | tf_op jit(solution)/shard_map/ppermute | solution.py:151
  197.6 8.3 %all-to-all-done.3 = bf16[16,8,2048]{2,1,0:T(8,128)(2,1)} async-done(((bf16[16,8,2048]{2,1,0:T(8,128)(2,1)}), bf16[16,8,2048]{2,1,0:T(8,128)(2,1)}, u32[]{:S(2)}, u32[]{:S(2)}) %all-to-all-start.3) | async-done | bytes 524320 | tf_op jit(solution)/shard_map/all_to_all | solution.py:127
  207.8 4.0 %collective-permute-done.13 = bf16[64,1024]{1,0:T(8,128)(2,1)S(1)} collective-permute-done((bf16[64,1024]{1,0:T(8,128)(2,1)S(1)}, bf16[64,1024]{1,0:T(8,128)(2,1)S(1)}, u32[]{:S(2)}, u32[]{:S(2)}) %collective-permute-start.13) | collective-permute-done | bytes 131104 | tf_op jit(solution)/shard_map/ppermute | solution.py:151
  (398 shorter events, 95.1 us)
Async XLA Ops:
  0.6 48.4 %copy-start = (bf16[1024,1024]{1,0:T(8,128)(2,1)S(1)}, bf16[1024,1024]{1,0:T(8,128)(2,1)}, u32[]{:S(2)}) copy-start(bf16[1024,1024]{1,0:T(8,128)(2,1)} %param.21) | copy-start | bytes 6291460
  1.9 15.1 %collective-permute-start = (bf16[128,2048]{1,0:T(8,128)(2,1)S(1)}, bf16[128,2048]{1,0:T(8,128)(2,1)}, u32[]{:S(2)}, u32[]{:S(2)}) collective-permute-start(bf16[128,2048]{1,0:T(8,128)(2,1)S(1)} %pad_maximum_fusion.4), channel_id=1, source_target_pairs={{1,0},{0,1},{3,2},{2,3},{5,4},{4,5},{7,6},{6,7},{9,8},{8,9},{11,10... | collective-permute-start | bytes 1572872 | tf_op jit(solution)/shard_map/ppermute | solution.py:108
  34.4 5.6 %collective-permute-start.1 = (bf16[15,1024]{1,0:T(8,128)(2,1)}, bf16[15,1024]{1,0:T(8,128)(2,1)S(1)}, u32[]{:S(2)}, u32[]{:S(2)}) collective-permute-start(bf16[15,1024]{1,0:T(8,128)(2,1)} %get-tuple-element.80), channel_id=1, source_target_pairs={{0,1},{2,3},{4,5},{6,7},{8,9},{10,11},{12,13},{14,15},{16,17},{18,... | collective-permute-start | bytes 92168 | tf_op jit(solution)/shard_map/ppermute | solution.py:21
  38.0 6.0 %collective-permute-start.2 = (bf16[15,1024]{1,0:T(8,128)(2,1)}, bf16[15,1024]{1,0:T(8,128)(2,1)S(1)}, u32[]{:S(2)}, u32[]{:S(2)}) collective-permute-start(bf16[15,1024]{1,0:T(8,128)(2,1)} %get-tuple-element.81), channel_id=1, source_target_pairs={{1,0},{3,2},{5,4},{7,6},{9,8},{11,10},{13,12},{15,14},{17,16},{19,... | collective-permute-start | bytes 92168 | tf_op jit(solution)/shard_map/ppermute | solution.py:23
  54.8 11.4 %collective-permute-start.3 = (bf16[512,1024]{1,0:T(8,128)(2,1)S(1)}, bf16[512,1024]{1,0:T(8,128)(2,1)S(1)}, u32[]{:S(2)}, u32[]{:S(2)}) collective-permute-start(bf16[512,1024]{1,0:T(8,128)(2,1)S(1)} %convolution_convert_fusion.1), channel_id=1, source_target_pairs={{0,2},{2,0},{4,6},{6,4},{8,10},{10,8},{12,14},{14,12},{16,18},{18,... | collective-permute-start | bytes 3145736 | tf_op jit(solution)/shard_map/ppermute | solution.py:151
  58.5 7.3 %collective-permute-start.4 = (bf16[15,1024]{1,0:T(8,128)(2,1)S(1)}, bf16[15,1024]{1,0:T(8,128)(2,1)S(1)}, u32[]{:S(2)}, u32[]{:S(2)}) collective-permute-start(bf16[15,1024]{1,0:T(8,128)(2,1)S(1)} %get-tuple-element.76), channel_id=1, source_target_pairs={{0,1},{2,3},{4,5},{6,7},{8,9},{10,11},{12,13},{14,15},{16,17},{18,... | collective-permute-start | bytes 92168 | tf_op jit(solution)/shard_map/ppermute | solution.py:21
  60.3 5.8 %collective-permute-start.5 = (bf16[15,1024]{1,0:T(8,128)(2,1)S(1)}, bf16[15,1024]{1,0:T(8,128)(2,1)S(1)}, u32[]{:S(2)}, u32[]{:S(2)}) collective-permute-start(bf16[15,1024]{1,0:T(8,128)(2,1)S(1)} %get-tuple-element.77), channel_id=1, source_target_pairs={{1,0},{3,2},{5,4},{7,6},{9,8},{11,10},{13,12},{15,14},{17,16},{19,... | collective-permute-start | bytes 92168 | tf_op jit(solution)/shard_map/ppermute | solution.py:23
  72.0 14.7 %collective-permute-start.6 = (bf16[256,1024]{1,0:T(8,128)(2,1)S(1)}, bf16[256,1024]{1,0:T(8,128)(2,1)S(1)}, u32[]{:S(2)}, u32[]{:S(2)}) collective-permute-start(bf16[256,1024]{1,0:T(8,128)(2,1)S(1)} %bitcast.376), channel_id=1, source_target_pairs={{0,1},{1,0},{2,3},{3,2},{4,5},{5,4},{6,7},{7,6},{8,9},{9,8},{10,11... | collective-permute-start | bytes 1572872 | tf_op jit(solution)/shard_map/ppermute | solution.py:151
  91.6 7.9 %collective-permute-start.7 = (bf16[128,1024]{1,0:T(8,128)(2,1)}, bf16[128,1024]{1,0:T(8,128)(2,1)}, u32[]{:S(2)}, u32[]{:S(2)}) collective-permute-start(bf16[128,1024]{1,0:T(8,128)(2,1)} %bitcast.379), channel_id=1, source_target_pairs={{0,4},{2,6},{4,0},{6,2},{8,12},{10,14},{12,8},{14,10},{16,20},{18,... | collective-permute-start | bytes 786440 | tf_op jit(solution)/shard_map/ppermute | solution.py:151
  106.6 12.6 %collective-permute-start.9 = (bf16[128,2048]{1,0:T(8,128)(2,1)}, bf16[128,2048]{1,0:T(8,128)(2,1)}, u32[]{:S(2)}, u32[]{:S(2)}) collective-permute-start(bf16[128,2048]{1,0:T(8,128)(2,1)} %fusion.13), channel_id=1, source_target_pairs={{0,1},{1,0},{2,3},{3,2},{4,5},{5,4},{6,7},{7,6},{8,9},{9,8},{10,11... | collective-permute-start | bytes 1572872 | tf_op jit(solution)/shard_map/ppermute | solution.py:117
  110.5 20.3 %copy-start.6 = (bf16[16,128,256]{1,2,0:T(8,128)(2,1)S(1)}, bf16[16,128,256]{1,2,0:T(8,128)(2,1)}, u32[]{:S(2)}) copy-start(bf16[16,128,256]{1,2,0:T(8,128)(2,1)} %copy-done.5) | copy-start | bytes 3145732
  110.5 23.3 %collective-permute-start.8 = (bf16[544,1024]{1,0:T(8,128)(2,1)}, bf16[544,1024]{1,0:T(8,128)(2,1)}, u32[]{:S(2)}, u32[]{:S(2)}) collective-permute-start(bf16[544,1024]{1,0:T(8,128)(2,1)} %pad_maximum_fusion), channel_id=1, source_target_pairs={{0,2},{2,0},{4,6},{6,4},{8,10},{10,8},{12,14},{14,12},{16,18},{18,... | collective-permute-start | bytes 3342344 | tf_op jit(solution)/shard_map/ppermute | solution.py:151
  121.2 20.8 %all-to-all-start.2 = ((bf16[16,8,2048]{2,1,0:T(8,128)(2,1)}), bf16[16,8,2048]{2,1,0:T(8,128)(2,1)S(1)}, u32[]{:S(2)}, u32[]{:S(2)}) async-start(bf16[16,8,2048]{2,1,0:T(8,128)(2,1)} %fusion.141), calls=%async_computation.2 | async-start | bytes 1048576 | tf_op jit(solution)/shard_map/all_to_all | solution.py:127
  128.9 22.3 %collective-permute-start.14 = (bf16[64,1024]{1,0:T(8,128)(2,1)}, bf16[64,1024]{1,0:T(8,128)(2,1)S(1)}, u32[]{:S(2)}, u32[]{:S(2)}) collective-permute-start(bf16[64,1024]{1,0:T(8,128)(2,1)} %bitcast.187), channel_id=1, source_target_pairs={{0,8},{2,10},{4,12},{6,14},{8,0},{10,2},{12,4},{14,6},{16,24},{18,... | collective-permute-start | bytes 393224 | tf_op jit(solution)/shard_map/ppermute | solution.py:151
  142.0 18.5 %all-to-all-start = ((bf16[16,8,2048]{2,1,0:T(8,128)(2,1)}), bf16[16,8,2048]{2,1,0:T(8,128)(2,1)S(1)}, u32[]{:S(2)}, u32[]{:S(2)}) async-start(bf16[16,8,2048]{2,1,0:T(8,128)(2,1)} %pad_maximum_fusion.5), calls=%async_computation | async-start | bytes 1048576 | tf_op jit(solution)/shard_map/all_to_all | solution.py:127
  149.1 18.3 %copy-start.12 = (f32[512,1024]{1,0:T(8,128)S(1)}, f32[512,1024]{1,0:T(8,128)}, u32[]{:S(2)}) copy-start(f32[512,1024]{1,0:T(8,128)} %copy-done.11) | copy-start | bytes 6291460
  150.0 17.6 %collective-permute-start.10 = (bf16[288,1024]{1,0:T(8,128)(2,1)}, bf16[288,1024]{1,0:T(8,128)(2,1)}, u32[]{:S(2)}, u32[]{:S(2)}) collective-permute-start(bf16[288,1024]{1,0:T(8,128)(2,1)} %pad_maximum_fusion.3), channel_id=1, source_target_pairs={{0,1},{1,0},{2,3},{3,2},{4,5},{5,4},{6,7},{7,6},{8,9},{9,8},{10,11... | collective-permute-start | bytes 1769480 | tf_op jit(solution)/shard_map/ppermute | solution.py:151
  151.3 20.4 %collective-permute-start.15 = (bf16[32,1024]{1,0:T(8,128)(2,1)S(1)}, bf16[32,1024]{1,0:T(8,128)(2,1)}, u32[]{:S(2)}, u32[]{:S(2)}) collective-permute-start(bf16[32,1024]{1,0:T(8,128)(2,1)S(1)} %fusion.197), channel_id=1, source_target_pairs={{0,16},{2,18},{4,20},{6,22},{8,24},{10,26},{12,28},{14,30},{16,0},... | collective-permute-start | bytes 196616 | tf_op jit(solution)/shard_map/ppermute | solution.py:151
  161.8 25.0 %all-to-all-start.1 = ((bf16[16,8,2048]{2,1,0:T(8,128)(2,1)}), bf16[16,8,2048]{2,1,0:T(8,128)(2,1)}, u32[]{:S(2)}, u32[]{:S(2)}) async-start(bf16[16,8,2048]{2,1,0:T(8,128)(2,1)} %gather_fusion), calls=%async_computation.1 | async-start | bytes 1048576 | tf_op jit(solution)/shard_map/all_to_all | solution.py:127
  169.8 13.5 %collective-permute-start.11 = (bf16[160,1024]{1,0:T(8,128)(2,1)}, bf16[160,1024]{1,0:T(8,128)(2,1)}, u32[]{:S(2)}, u32[]{:S(2)}) collective-permute-start(bf16[160,1024]{1,0:T(8,128)(2,1)} %pad_maximum_fusion.6), channel_id=1, source_target_pairs={{0,4},{2,6},{4,0},{6,2},{8,12},{10,14},{12,8},{14,10},{16,20},{18,... | collective-permute-start | bytes 983048 | tf_op jit(solution)/shard_map/ppermute | solution.py:151
  184.5 8.5 %collective-permute-start.12 = (bf16[96,1024]{1,0:T(8,128)(2,1)S(1)}, bf16[96,1024]{1,0:T(8,128)(2,1)S(1)}, u32[]{:S(2)}, u32[]{:S(2)}) collective-permute-start(bf16[96,1024]{1,0:T(8,128)(2,1)S(1)} %pad_maximum_fusion.10), channel_id=1, source_target_pairs={{0,8},{2,10},{4,12},{6,14},{8,0},{10,2},{12,4},{14,6},{16,24},{18,... | collective-permute-start | bytes 589832 | tf_op jit(solution)/shard_map/ppermute | solution.py:151
  186.8 19.1 %all-to-all-start.3 = ((bf16[16,8,2048]{2,1,0:T(8,128)(2,1)}), bf16[16,8,2048]{2,1,0:T(8,128)(2,1)}, u32[]{:S(2)}, u32[]{:S(2)}) async-start(bf16[16,8,2048]{2,1,0:T(8,128)(2,1)} %gather_fusion.1), calls=%async_computation.3 | async-start | bytes 1048576 | tf_op jit(solution)/shard_map/all_to_all | solution.py:127
  193.0 21.2 %copy-start.1 = (bf16[1024,1024]{1,0:T(8,128)(2,1)S(1)}, bf16[1024,1024]{1,0:T(8,128)(2,1)}, u32[]{:S(2)}) copy-start(bf16[1024,1024]{1,0:T(8,128)(2,1)} %param.21) | copy-start | bytes 6291460
  194.9 16.9 %collective-permute-start.13 = (bf16[64,1024]{1,0:T(8,128)(2,1)S(1)}, bf16[64,1024]{1,0:T(8,128)(2,1)S(1)}, u32[]{:S(2)}, u32[]{:S(2)}) collective-permute-start(bf16[64,1024]{1,0:T(8,128)(2,1)S(1)} %pad_maximum_fusion.11), channel_id=1, source_target_pairs={{0,16},{2,18},{4,20},{6,22},{8,24},{10,26},{12,28},{14,30},{16,0},... | collective-permute-start | bytes 393224 | tf_op jit(solution)/shard_map/ppermute | solution.py:151
  (129 other events, 580.5 us)

commit v4 on v3

--- a/solution.py
+++ b/solution.py
@@ -286,8 +286,6 @@
         grad_rows.astype(jnp.float32) + norm_backward(back_in, hat_in, inv_in, norm_gain)
     ).astype(jnp.bfloat16)
     mixed_grad = times_transposed(stream_out, attn_out).astype(jnp.bfloat16)
-    mixed_grad = out_sum.tie(mixed_grad)
-    out_sum.step()
     grad_heads = split_heads(mixed_grad)
     slope = jnp.einsum(
         "hqe,hke->hqk", grad_heads, value_heads, preferred_element_type=jnp.float32
@@ -310,12 +308,22 @@
         jnp.einsum("hqk,hqe->hke", weights_low, grad_heads, preferred_element_type=jnp.float32)
     )
     pair_part = jnp.concatenate([key_part, value_part], 1)
+    first_spread = spread_rows(jnp.concatenate([stream_out, query_grad], 1))
+    in_sum = Reduction(mixed, stream_out, tap_part)
     pair_grad = returned(
         [pair_part[step * frames : (step + 1) * frames] for step in range(seq_count)], "seq"
     ).astype(jnp.bfloat16)
-    first_routed = route(jnp.concatenate([stream_out, query_grad], 1), plan)
-    in_sum = Reduction(mixed, stream_out, tap_part)
-    second_spread = in_sum.tie(spread_rows(pair_grad))
+    pair_grad, first_spread, in_sum.total, in_sum.extra, out_sum.total = (
+        lax.optimization_barrier(
+            (pair_grad, first_spread, in_sum.total, in_sum.extra, out_sum.total)
+        )
+    )
+    in_sum.step()
+    out_sum.step()
+    second_spread = spread_rows(pair_grad)
+    first_routed = collected(first_spread, plan)
+    second_spread = in_sum.tie(second_spread)
+    in_sum.step()
     second_routed = collected(second_spread, plan)
     in_part = in_sum.finish()
     return (

time: 216 us -> 203 us (0.940)
  waiting for transfers between devices: 65.7 us -> 53.5 us
  local copies, waits for them, and re-layouts: 25.4 us -> 31.8 us
  other arithmetic: 40.8 us -> 35.8 us
    all_to_all x4, waiting for transfers between devices: 19.9 us -> 4.75 us  [spread_rows(): return lax.all_to_all(matrix, 'dp', split_axis=0, concat_axis=0, tiled=True)]
    ppermute x10, waiting for transfers between devices: 27.3 us -> 33.4 us  [swapped(): lax.ppermute(cells, axis, [(i, i ^ 1 << bit) for i in range(lax.axis_size...]
    ppermute x1, waiting for transfers between devices: 8.75 us -> 6.05 us  [returned(): lax.ppermute(parts[step].astype(jnp.bfloat16), axis, [(i, (i + step) % co...]
    dynamic_slice x7, local copies, waits for them, and re-layouts: 1.86 us -> 4.32 us  [half_of(): chosen = lax.dynamic_index_in_dim(split, which, dim + 1, keepdims=False)]
    convert_element_type x5, other arithmetic: 5.2 us -> 2.83 us  [joined(): arrived = swapped(jnp.concatenate([outgoing, rounded.astype(jnp.bfloat16)...]
    convert_element_type x8, local copies, waits for them, and re-layouts: 2.66 us -> 4.87 us  [joined(): outgoing = outgoing.astype(jnp.bfloat16)]
    convert_element_type x5, other arithmetic: 2.93 us -> 0.75 us  [joined(): rounded.astype(jnp.bfloat16)]
    unnamed x267 -> x249, local copies, waits for them, and re-layouts: 3.82 us -> 4.87 us
  transfers between devices with their start and end apart: 20 -> 20, of which waited for: 11 -> 10; matrix products, arithmetic and copies ran while one was open for 22% -> 30% of each run, Pallas kernels for 0% -> 0%
where the time goes in v4:
time: 203 us; the launch traced here: 201 us
  waiting for transfers between devices  53.5 us (26%)
  starting transfers between devices  47.5 us (23%)
  other arithmetic  35.8 us (18%)
  local copies, waits for them, and re-layouts  31.8 us (16%)
  matrix products  29.9 us (15%)
  between operations  2.86 us (1%)
    ppermute x10, waiting for transfers between devices, swapped(): lax.ppermute(cells, axis, [(i, i ^ 1 << bit) for i in range(lax.axis_size...  33.4 us
    all_to_all x4, starting transfers between devices, spread_rows(): return lax.all_to_all(matrix, 'dp', split_axis=0, concat_axis=0, tiled=True)  18.5 us
    ppermute x10, starting transfers between devices, swapped(): lax.ppermute(cells, axis, [(i, i ^ 1 << bit) for i in range(lax.axis_size...  17 us
    ppermute x1, waiting for transfers between devices, returned(): lax.ppermute(parts[step].astype(jnp.bfloat16), axis, [(i, (i + step) % co...  6.05 us
    ppermute x2, starting transfers between devices, extended(): lax.ppermute(tail, axis, [(i, (i + 1) % count) for i in range(ends)])  5.94 us
    dot_general x3, matrix products, times_transposed(): lax.dot_general(left, right, (((1,), (1,)), ((), ())), preferred_element_...  5.64 us
    reduce_sum x6, other arithmetic, tap_sums(): jnp.sum(upstream * padded[tap:tap + length].astype(jnp.float32) * table[:...  5.48 us
    dot_general x4, matrix products, transposed_times(): lax.dot_general(left, right, (((0,), (0,)), ((), ())), preferred_element_...  5.3 us
  transfers between devices with their start and end apart: 20, of which 10 were waited for; matrix products, arithmetic and copies ran while one was open for 30% of the time, Pallas kernels for 0%

profile of v4, /device:TPU:0, one launch (start us, length us, event | category | flops | bytes accessed | tf_op | source)
XLA Modules:
  0.0 201.4 jit_solution(15841654040323598239)
XLA Ops:
  1.9 3.1 %collective-permute-start = (bf16[128,2048]{1,0:T(8,128)(2,1)S(1)}, bf16[128,2048]{1,0:T(8,128)(2,1)}, u32[]{:S(2)}, u32[]{:S(2)}) collective-permute-start(bf16[128,2048]{1,0:T(8,128)(2,1)S(1)} %pad_maximum_fusion.4), channel_id=1, source_target_pairs={{1,0},{0,1},{3,2},{2,3},{5,4},{4,5},{7,6},{6,7},{9,8},{8,9},{11,10... | collective-permute-start | bytes 1572872 | tf_op jit(solution)/shard_map/ppermute | solution.py:108
  11.7 5.2 %collective-permute-done = bf16[128,2048]{1,0:T(8,128)(2,1)} collective-permute-done((bf16[128,2048]{1,0:T(8,128)(2,1)S(1)}, bf16[128,2048]{1,0:T(8,128)(2,1)}, u32[]{:S(2)}, u32[]{:S(2)}) %collective-permute-start) | collective-permute-done | bytes 524320 | tf_op jit(solution)/shard_map/ppermute | solution.py:108
  24.7 2.4 %convolution_convert_fusion.2 = bf16[16,128,64]{1,2,0:T(8,128)(2,1)S(1)} fusion(bf16[16,256,64]{1,2,0:T(8,128)(2,1)S(1)} %bitcast.344, f32[16,128]{1,0:T(8,128)S(1)} %broadcast_divide_fusion, f32[16,256,128]{2,1,0:T(8,128)} %fusion.222, pred[128,256]{0,1:T(8,128)(4,1)S(1)} %broadcast_compare_fusion), kind=kOutput, calls=%fused_computation.53 | convolution fusion | flops 69863680 | bytes 2924544 | tf_op jit(solution)/shard_map/hqk,hke->hqe/dot_general | solution.py:249
  29.7 3.0 %fusion.148 = f32[128,2048]{1,0:T(8,128)S(1)} fusion(bf16[1024,2048]{1,0:T(8,128)(2,1)} %param.19, f32[128,1024]{1,0:T(8,128)S(1)} %get-tuple-element.182, f32[1024]{0:T(1024)S(1)} %copy-done.79, f32[128]{0:T(128)S(1)} %add_rsqrt_fusion.1, f32[128]{0:T(128)S(1)} %broadcast_multiply_fusion.5), kind=kOutput, calls=%fused_computation.288 | convolution fusion | flops 537395200 | bytes 5772288 | tf_op jit(solution)/shard_map/dot_general | solution.py:257
  34.4 3.6 %collective-permute-start.1 = (bf16[15,1024]{1,0:T(8,128)(2,1)}, bf16[15,1024]{1,0:T(8,128)(2,1)S(1)}, u32[]{:S(2)}, u32[]{:S(2)}) collective-permute-start(bf16[15,1024]{1,0:T(8,128)(2,1)} %get-tuple-element.84), channel_id=1, source_target_pairs={{0,1},{2,3},{4,5},{6,7},{8,9},{10,11},{12,13},{14,15},{16,17},{18,... | collective-permute-start | bytes 92168 | tf_op jit(solution)/shard_map/ppermute | solution.py:21
  40.0 4.1 %collective-permute-done.2 = bf16[15,1024]{1,0:T(8,128)(2,1)S(1)} collective-permute-done((bf16[15,1024]{1,0:T(8,128)(2,1)}, bf16[15,1024]{1,0:T(8,128)(2,1)S(1)}, u32[]{:S(2)}, u32[]{:S(2)}) %collective-permute-start.2) | collective-permute-done | bytes 30752 | tf_op jit(solution)/shard_map/ppermute | solution.py:23
  44.2 4.1 %fusion.215 = (f32[128]{0:T(128)S(1)}, f32[128,1024]{1,0:T(8,128)S(1)}) fusion(f32[128]{0:T(128)} %get-tuple-element.118, bf16[15,1024]{1,0:T(8,128)(2,1)S(1)} %collective-permute-done.2, bf16[128,1024]{1,0:T(8,128)(2,1)S(1)} %multiply_convert_fusion.5, f32[1024]{0:T(1024)S(1)} %bitcast.400, f32[128]{0:T(128)} %get-tuple-element.119, ...), kind=kLoop, calls=%fused_computation.489 | loop fusion | flops 28049280 | bytes 991232 | tf_op jit(solution)/shard_map/reduce_sum | solution.py:31
  70.2 3.0 %collective-permute-start.6 = (bf16[256,1024]{1,0:T(8,128)(2,1)}, bf16[256,1024]{1,0:T(8,128)(2,1)}, u32[]{:S(2)}, u32[]{:S(2)}) collective-permute-start(bf16[256,1024]{1,0:T(8,128)(2,1)} %bitcast.113), channel_id=1, source_target_pairs={{0,1},{1,0},{2,3},{3,2},{4,5},{5,4},{6,7},{7,6},{8,9},{9,8},{10,11... | collective-permute-start | bytes 1572872 | tf_op jit(solution)/shard_map/ppermute | solution.py:151
  73.6 3.9 %multiply_convert_fusion.3 = (bf16[128,1024]{1,0:T(8,128)(2,1)S(1)}, f32[128,1024]{1,0:T(8,128)S(1)}) fusion(f32[128,2048]{1,0:T(8,128)S(1)} %copy-done.4, f32[128]{0:T(128)S(1)} %copy-done.94, f32[158,1024]{1,0:T(8,128)S(1)} %maximum_convert_fusion, f32[1024]{0:T(1024)S(1)} %bitcast.405, f32[128]{0:T(128)S(1)} %copy-done.96, f32[1024]{0:T(1024)S(1)} %bitcast.381, ...), kind=kLoop, calls=%fused_computation.273 | loop fusion | flops 12713984 | bytes 17706496 | tf_op jit(solution)/shard_map/convert.33
  77.7 2.5 %fusion.211 = (f32[128]{0:T(128)S(1)}, f32[128]{0:T(128)S(1)}, f32[128,1024]{1,0:T(8,128)S(1)}) fusion(f32[128]{0:T(128)} %copy-done.121, f32[128,1024]{1,0:T(8,128)S(1)} %get-tuple-element.182, f32[128]{0:T(128)} %copy-done.119, f32[1024]{0:T(1024)S(1)} %copy-done.80, bf16[1024,2048]{1,0:T(8,128)(2,1)S(1)} %copy-done.2, ...), kind=kOutput, calls=%fused_computation.486 | convolution fusion | flops 538705664 | bytes 5773312 | tf_op jit(solution)/shard_map/dot_general | solution.py:86
  88.4 3.2 %multiply_convert_fusion = bf16[16,128,256]{1,2,0:T(8,128)(2,1)S(1)} fusion(f32[16,128,256]{1,2,0:T(8,128)} %get-tuple-element.180, f32[16,128]{1,0:T(8,128)S(1)} %copy-done.65, bf16[16,128,64]{1,2,0:T(8,128)(2,1)S(1)} %bitcast.352, bf16[16,256,64]{1,2,0:T(8,128)(2,1)S(1)} %bitcast.345), kind=kOutput, calls=%fused_computation.8 | convolution fusion | flops 137365760 | bytes 3940352 | tf_op jit(solution)/shard_map/sub | solution.py:294
  91.6 2.6 %bitcast_add_fusion = f32[256,1024]{1,0:T(8,128)} fusion(f32[8,1,32,1024]{3,2,1,0:T(8,128)} %constant_dynamic-slice_fusion.7, bf16[256,1024]{1,0:T(8,128)(2,1)} %collective-permute-done.6), kind=kLoop, calls=%fused_computation.64 | loop fusion | flops 524288 | bytes 2621440 | tf_op jit(solution)/shard_map/add | solution.py:197
  103.6 5.0 %all-to-all-start = ((bf16[16,8,2048]{2,1,0:T(8,128)(2,1)}), bf16[16,8,2048]{2,1,0:T(8,128)(2,1)S(1)}, u32[]{:S(2)}, u32[]{:S(2)}) async-start(bf16[16,8,2048]{2,1,0:T(8,128)(2,1)} %pad_maximum_fusion.5), calls=%async_computation | async-start | bytes 1048576 | tf_op jit(solution)/shard_map/all_to_all | solution.py:127
  110.6 6.1 %collective-permute-done.7 = bf16[128,2048]{1,0:T(8,128)(2,1)} collective-permute-done((bf16[128,2048]{1,0:T(8,128)(2,1)}, bf16[128,2048]{1,0:T(8,128)(2,1)}, u32[]{:S(2)}, u32[]{:S(2)}) %collective-permute-start.7) | collective-permute-done | bytes 524320 | tf_op jit(solution)/shard_map/ppermute | solution.py:117
  127.6 4.3 %all-to-all-start.2 = ((bf16[16,8,2048]{2,1,0:T(8,128)(2,1)}), bf16[16,8,2048]{2,1,0:T(8,128)(2,1)}, u32[]{:S(2)}, u32[]{:S(2)}) async-start(bf16[16,8,2048]{2,1,0:T(8,128)(2,1)} %bitcast.170), calls=%async_computation.2 | async-start | bytes 1048576 | tf_op jit(solution)/shard_map/all_to_all | solution.py:127
  136.9 4.6 %collective-permute-done.10 = bf16[288,1024]{1,0:T(8,128)(2,1)} collective-permute-done((bf16[288,1024]{1,0:T(8,128)(2,1)}, bf16[288,1024]{1,0:T(8,128)(2,1)}, u32[]{:S(2)}, u32[]{:S(2)}) %collective-permute-start.10) | collective-permute-done | bytes 589856 | tf_op jit(solution)/shard_map/ppermute | solution.py:151
  142.9 3.8 %all-to-all-done.2 = bf16[16,8,2048]{2,1,0:T(8,128)(2,1)} async-done(((bf16[16,8,2048]{2,1,0:T(8,128)(2,1)}), bf16[16,8,2048]{2,1,0:T(8,128)(2,1)}, u32[]{:S(2)}, u32[]{:S(2)}) %all-to-all-start.2) | async-done | bytes 524320 | tf_op jit(solution)/shard_map/all_to_all | solution.py:127
  146.7 4.2 %all-to-all-start.1 = ((bf16[16,8,2048]{2,1,0:T(8,128)(2,1)}), bf16[16,8,2048]{2,1,0:T(8,128)(2,1)}, u32[]{:S(2)}, u32[]{:S(2)}) async-start(bf16[16,8,2048]{2,1,0:T(8,128)(2,1)} %gather_fusion), calls=%async_computation.1 | async-start | bytes 1048576 | tf_op jit(solution)/shard_map/all_to_all | solution.py:127
  153.8 2.5 %collective-permute-start.15 = (bf16[32,1024]{1,0:T(8,128)(2,1)S(1)}, bf16[32,1024]{1,0:T(8,128)(2,1)S(1)}, u32[]{:S(2)}, u32[]{:S(2)}) collective-permute-start(bf16[32,1024]{1,0:T(8,128)(2,1)S(1)} %fusion.195), channel_id=1, source_target_pairs={{0,16},{2,18},{4,20},{6,22},{8,24},{10,26},{12,28},{14,30},{16,0},... | collective-permute-start | bytes 196616 | tf_op jit(solution)/shard_map/ppermute | solution.py:151
  156.3 10.0 %collective-permute-done.11 = bf16[160,1024]{1,0:T(8,128)(2,1)S(1)} collective-permute-done((bf16[160,1024]{1,0:T(8,128)(2,1)S(1)}, bf16[160,1024]{1,0:T(8,128)(2,1)S(1)}, u32[]{:S(2)}, u32[]{:S(2)}) %collective-permute-start.11) | collective-permute-done | bytes 327712 | tf_op jit(solution)/shard_map/ppermute | solution.py:151
  168.9 2.4 %gather_fusion.1 = bf16[16,8,2048]{2,1,0:T(8,128)(2,1)} fusion(bf16[16,8,2048]{2,1,0:T(8,128)(2,1)} %bitcast.172, s32[1024]{0:T(1024)S(1)} %pad_clamp_fusion), kind=kCustom, calls=%fused_computation.1 | custom fusion | bytes 1048640 | tf_op jit(solution)/shard_map/jit(_take)/gather | solution.py:132
  173.2 5.0 %all-to-all-start.3 = ((bf16[16,8,2048]{2,1,0:T(8,128)(2,1)}), bf16[16,8,2048]{2,1,0:T(8,128)(2,1)S(1)}, u32[]{:S(2)}, u32[]{:S(2)}) async-start(bf16[16,8,2048]{2,1,0:T(8,128)(2,1)} %gather_fusion.1), calls=%async_computation.3 | async-start | bytes 1048576 | tf_op jit(solution)/shard_map/all_to_all | solution.py:127
  178.2 2.9 %collective-permute-start.13 = (bf16[64,1024]{1,0:T(8,128)(2,1)S(1)}, bf16[64,1024]{1,0:T(8,128)(2,1)S(1)}, u32[]{:S(2)}, u32[]{:S(2)}) collective-permute-start(bf16[64,1024]{1,0:T(8,128)(2,1)S(1)} %pad_maximum_fusion.11), channel_id=1, source_target_pairs={{0,16},{2,18},{4,20},{6,22},{8,24},{10,26},{12,28},{14,30},{16,0},... | collective-permute-start | bytes 393224 | tf_op jit(solution)/shard_map/ppermute | solution.py:151
  183.0 16.1 %collective-permute-done.13 = bf16[64,1024]{1,0:T(8,128)(2,1)S(1)} collective-permute-done((bf16[64,1024]{1,0:T(8,128)(2,1)S(1)}, bf16[64,1024]{1,0:T(8,128)(2,1)S(1)}, u32[]{:S(2)}, u32[]{:S(2)}) %collective-permute-start.13) | collective-permute-done | bytes 131104 | tf_op jit(solution)/shard_map/ppermute | solution.py:151
  (381 shorter events, 91.1 us)
Async XLA Ops:
  0.6 47.9 %copy-start = (bf16[1024,1024]{1,0:T(8,128)(2,1)S(1)}, bf16[1024,1024]{1,0:T(8,128)(2,1)}, u32[]{:S(2)}) copy-start(bf16[1024,1024]{1,0:T(8,128)(2,1)} %param.21) | copy-start | bytes 6291460
  1.9 15.1 %collective-permute-start = (bf16[128,2048]{1,0:T(8,128)(2,1)S(1)}, bf16[128,2048]{1,0:T(8,128)(2,1)}, u32[]{:S(2)}, u32[]{:S(2)}) collective-permute-start(bf16[128,2048]{1,0:T(8,128)(2,1)S(1)} %pad_maximum_fusion.4), channel_id=1, source_target_pairs={{1,0},{0,1},{3,2},{2,3},{5,4},{4,5},{7,6},{6,7},{9,8},{8,9},{11,10... | collective-permute-start | bytes 1572872 | tf_op jit(solution)/shard_map/ppermute | solution.py:108
  9.8 34.3 %copy-start.25 = (f32[1,1024]{1,0:T(1,128)}, f32[1,1024]{1,0:T(1,128)S(1)}, u32[]{:S(2)}) copy-start(f32[1,1024]{1,0:T(1,128)S(1)} %get-tuple-element.109) | copy-start | bytes 12292
  9.8 34.3 %copy-start.27 = (f32[1,1024]{1,0:T(1,128)}, f32[1,1024]{1,0:T(1,128)S(1)}, u32[]{:S(2)}) copy-start(f32[1,1024]{1,0:T(1,128)S(1)} %get-tuple-element.110) | copy-start | bytes 12292
  9.8 34.3 %copy-start.29 = (f32[1,1024]{1,0:T(1,128)}, f32[1,1024]{1,0:T(1,128)S(1)}, u32[]{:S(2)}) copy-start(f32[1,1024]{1,0:T(1,128)S(1)} %get-tuple-element.111) | copy-start | bytes 12292
  34.4 5.6 %collective-permute-start.1 = (bf16[15,1024]{1,0:T(8,128)(2,1)}, bf16[15,1024]{1,0:T(8,128)(2,1)S(1)}, u32[]{:S(2)}, u32[]{:S(2)}) collective-permute-start(bf16[15,1024]{1,0:T(8,128)(2,1)} %get-tuple-element.84), channel_id=1, source_target_pairs={{0,1},{2,3},{4,5},{6,7},{8,9},{10,11},{12,13},{14,15},{16,17},{18,... | collective-permute-start | bytes 92168 | tf_op jit(solution)/shard_map/ppermute | solution.py:21
  38.1 6.0 %collective-permute-start.2 = (bf16[15,1024]{1,0:T(8,128)(2,1)}, bf16[15,1024]{1,0:T(8,128)(2,1)S(1)}, u32[]{:S(2)}, u32[]{:S(2)}) collective-permute-start(bf16[15,1024]{1,0:T(8,128)(2,1)} %get-tuple-element.85), channel_id=1, source_target_pairs={{1,0},{3,2},{5,4},{7,6},{9,8},{11,10},{13,12},{15,14},{17,16},{19,... | collective-permute-start | bytes 92168 | tf_op jit(solution)/shard_map/ppermute | solution.py:23
  54.5 10.2 %collective-permute-start.4 = (bf16[15,1024]{1,0:T(8,128)(2,1)}, bf16[15,1024]{1,0:T(8,128)(2,1)}, u32[]{:S(2)}, u32[]{:S(2)}) collective-permute-start(bf16[15,1024]{1,0:T(8,128)(2,1)} %get-tuple-element.80), channel_id=1, source_target_pairs={{0,1},{2,3},{4,5},{6,7},{8,9},{10,11},{12,13},{14,15},{16,17},{18,... | collective-permute-start | bytes 92168 | tf_op jit(solution)/shard_map/ppermute | solution.py:21
  56.8 7.9 %collective-permute-start.5 = (bf16[15,1024]{1,0:T(8,128)(2,1)}, bf16[15,1024]{1,0:T(8,128)(2,1)}, u32[]{:S(2)}, u32[]{:S(2)}) collective-permute-start(bf16[15,1024]{1,0:T(8,128)(2,1)} %get-tuple-element.81), channel_id=1, source_target_pairs={{1,0},{3,2},{5,4},{7,6},{9,8},{11,10},{13,12},{15,14},{17,16},{19,... | collective-permute-start | bytes 92168 | tf_op jit(solution)/shard_map/ppermute | solution.py:23
  60.8 4.8 %collective-permute-start.3 = (bf16[512,1024]{1,0:T(8,128)(2,1)}, bf16[512,1024]{1,0:T(8,128)(2,1)S(1)}, u32[]{:S(2)}, u32[]{:S(2)}) collective-permute-start(bf16[512,1024]{1,0:T(8,128)(2,1)} %convolution_convert_fusion.1), channel_id=1, source_target_pairs={{0,2},{2,0},{4,6},{6,4},{8,10},{10,8},{12,14},{14,12},{16,18},{18,... | collective-permute-start | bytes 3145736 | tf_op jit(solution)/shard_map/ppermute | solution.py:151
  70.2 21.4 %collective-permute-start.6 = (bf16[256,1024]{1,0:T(8,128)(2,1)}, bf16[256,1024]{1,0:T(8,128)(2,1)}, u32[]{:S(2)}, u32[]{:S(2)}) collective-permute-start(bf16[256,1024]{1,0:T(8,128)(2,1)} %bitcast.113), channel_id=1, source_target_pairs={{0,1},{1,0},{2,3},{3,2},{4,5},{5,4},{6,7},{7,6},{8,9},{9,8},{10,11... | collective-permute-start | bytes 1572872 | tf_op jit(solution)/shard_map/ppermute | solution.py:151
  85.8 32.7 %collective-permute-start.8 = (bf16[544,1024]{1,0:T(8,128)(2,1)}, bf16[544,1024]{1,0:T(8,128)(2,1)}, u32[]{:S(2)}, u32[]{:S(2)}) collective-permute-start(bf16[544,1024]{1,0:T(8,128)(2,1)} %pad_maximum_fusion), channel_id=1, source_target_pairs={{0,2},{2,0},{4,6},{6,4},{8,10},{10,8},{12,14},{14,12},{16,18},{18,... | collective-permute-start | bytes 3342344 | tf_op jit(solution)/shard_map/ppermute | solution.py:151
  98.6 11.1 %collective-permute-start.9 = (bf16[128,1024]{1,0:T(8,128)(2,1)}, bf16[128,1024]{1,0:T(8,128)(2,1)S(1)}, u32[]{:S(2)}, u32[]{:S(2)}) collective-permute-start(bf16[128,1024]{1,0:T(8,128)(2,1)} %bitcast.163), channel_id=1, source_target_pairs={{0,4},{2,6},{4,0},{6,2},{8,12},{10,14},{12,8},{14,10},{16,20},{18,... | collective-permute-start | bytes 786440 | tf_op jit(solution)/shard_map/ppermute | solution.py:151
  102.5 14.2 %collective-permute-start.7 = (bf16[128,2048]{1,0:T(8,128)(2,1)}, bf16[128,2048]{1,0:T(8,128)(2,1)}, u32[]{:S(2)}, u32[]{:S(2)}) collective-permute-start(bf16[128,2048]{1,0:T(8,128)(2,1)} %fusion.13), channel_id=1, source_target_pairs={{0,1},{1,0},{2,3},{3,2},{4,5},{5,4},{6,7},{7,6},{8,9},{9,8},{10,11... | collective-permute-start | bytes 1572872 | tf_op jit(solution)/shard_map/ppermute | solution.py:117
  103.6 19.3 %all-to-all-start = ((bf16[16,8,2048]{2,1,0:T(8,128)(2,1)}), bf16[16,8,2048]{2,1,0:T(8,128)(2,1)S(1)}, u32[]{:S(2)}, u32[]{:S(2)}) async-start(bf16[16,8,2048]{2,1,0:T(8,128)(2,1)} %pad_maximum_fusion.5), calls=%async_computation | async-start | bytes 1048576 | tf_op jit(solution)/shard_map/all_to_all | solution.py:127
  125.8 15.7 %collective-permute-start.10 = (bf16[288,1024]{1,0:T(8,128)(2,1)}, bf16[288,1024]{1,0:T(8,128)(2,1)}, u32[]{:S(2)}, u32[]{:S(2)}) collective-permute-start(bf16[288,1024]{1,0:T(8,128)(2,1)} %pad_maximum_fusion.3), channel_id=1, source_target_pairs={{0,1},{1,0},{2,3},{3,2},{4,5},{5,4},{6,7},{7,6},{8,9},{9,8},{10,11... | collective-permute-start | bytes 1769480 | tf_op jit(solution)/shard_map/ppermute | solution.py:151
  127.6 19.1 %all-to-all-start.2 = ((bf16[16,8,2048]{2,1,0:T(8,128)(2,1)}), bf16[16,8,2048]{2,1,0:T(8,128)(2,1)}, u32[]{:S(2)}, u32[]{:S(2)}) async-start(bf16[16,8,2048]{2,1,0:T(8,128)(2,1)} %bitcast.170), calls=%async_computation.2 | async-start | bytes 1048576 | tf_op jit(solution)/shard_map/all_to_all | solution.py:127
  132.5 20.3 %collective-permute-start.14 = (bf16[64,1024]{1,0:T(8,128)(2,1)}, bf16[64,1024]{1,0:T(8,128)(2,1)}, u32[]{:S(2)}, u32[]{:S(2)}) collective-permute-start(bf16[64,1024]{1,0:T(8,128)(2,1)} %bitcast.188), channel_id=1, source_target_pairs={{0,8},{2,10},{4,12},{6,14},{8,0},{10,2},{12,4},{14,6},{16,24},{18,... | collective-permute-start | bytes 393224 | tf_op jit(solution)/shard_map/ppermute | solution.py:151
  146.7 26.5 %all-to-all-start.1 = ((bf16[16,8,2048]{2,1,0:T(8,128)(2,1)}), bf16[16,8,2048]{2,1,0:T(8,128)(2,1)}, u32[]{:S(2)}, u32[]{:S(2)}) async-start(bf16[16,8,2048]{2,1,0:T(8,128)(2,1)} %gather_fusion), calls=%async_computation.1 | async-start | bytes 1048576 | tf_op jit(solution)/shard_map/all_to_all | solution.py:127
  151.0 15.3 %collective-permute-start.11 = (bf16[160,1024]{1,0:T(8,128)(2,1)S(1)}, bf16[160,1024]{1,0:T(8,128)(2,1)S(1)}, u32[]{:S(2)}, u32[]{:S(2)}) collective-permute-start(bf16[160,1024]{1,0:T(8,128)(2,1)S(1)} %pad_maximum_fusion.6), channel_id=1, source_target_pairs={{0,4},{2,6},{4,0},{6,2},{8,12},{10,14},{12,8},{14,10},{16,20},{18,... | collective-permute-start | bytes 983048 | tf_op jit(solution)/shard_map/ppermute | solution.py:151
  153.8 15.1 %collective-permute-start.15 = (bf16[32,1024]{1,0:T(8,128)(2,1)S(1)}, bf16[32,1024]{1,0:T(8,128)(2,1)S(1)}, u32[]{:S(2)}, u32[]{:S(2)}) collective-permute-start(bf16[32,1024]{1,0:T(8,128)(2,1)S(1)} %fusion.195), channel_id=1, source_target_pairs={{0,16},{2,18},{4,20},{6,22},{8,24},{10,26},{12,28},{14,30},{16,0},... | collective-permute-start | bytes 196616 | tf_op jit(solution)/shard_map/ppermute | solution.py:151
  166.6 6.5 %collective-permute-start.12 = (bf16[96,1024]{1,0:T(8,128)(2,1)S(1)}, bf16[96,1024]{1,0:T(8,128)(2,1)S(1)}, u32[]{:S(2)}, u32[]{:S(2)}) collective-permute-start(bf16[96,1024]{1,0:T(8,128)(2,1)S(1)} %pad_maximum_fusion.10), channel_id=1, source_target_pairs={{0,8},{2,10},{4,12},{6,14},{8,0},{10,2},{12,4},{14,6},{16,24},{18,... | collective-permute-start | bytes 589832 | tf_op jit(solution)/shard_map/ppermute | solution.py:151
  173.2 27.3 %all-to-all-start.3 = ((bf16[16,8,2048]{2,1,0:T(8,128)(2,1)}), bf16[16,8,2048]{2,1,0:T(8,128)(2,1)S(1)}, u32[]{:S(2)}, u32[]{:S(2)}) async-start(bf16[16,8,2048]{2,1,0:T(8,128)(2,1)} %gather_fusion.1), calls=%async_computation.3 | async-start | bytes 1048576 | tf_op jit(solution)/shard_map/all_to_all | solution.py:127
  178.2 20.8 %collective-permute-start.13 = (bf16[64,1024]{1,0:T(8,128)(2,1)S(1)}, bf16[64,1024]{1,0:T(8,128)(2,1)S(1)}, u32[]{:S(2)}, u32[]{:S(2)}) collective-permute-start(bf16[64,1024]{1,0:T(8,128)(2,1)S(1)} %pad_maximum_fusion.11), channel_id=1, source_target_pairs={{0,16},{2,18},{4,20},{6,22},{8,24},{10,26},{12,28},{14,30},{16,0},... | collective-permute-start | bytes 393224 | tf_op jit(solution)/shard_map/ppermute | solution.py:151
  (120 other events, 908.1 us)

commit v5 on v4

--- a/solution.py
+++ b/solution.py
@@ -127,14 +127,10 @@
     return lax.all_to_all(matrix, "dp", split_axis=0, concat_axis=0, tiled=True)
 
 
-def collected(spread, plan):
+def by_slot(spread, plan):
     rows, width = spread.shape
     arranged = jnp.take(spread.reshape(plan.shape[0], -1, width), plan, axis=0, mode="clip")
-    return spread_rows(arranged.reshape(rows, width))
-
-
-def route(matrix, plan):
-    return collected(spread_rows(matrix), plan)
+    return arranged.reshape(rows, width)
 
 
 def exchange_order():
@@ -321,16 +317,16 @@
     in_sum.step()
     out_sum.step()
     second_spread = spread_rows(pair_grad)
-    first_routed = collected(first_spread, plan)
+    first_slots = by_slot(first_spread, plan)
     second_spread = in_sum.tie(second_spread)
     in_sum.step()
-    second_routed = collected(second_spread, plan)
+    routed = spread_rows(jnp.concatenate([first_slots, by_slot(second_spread, plan)], 1))
     in_part = in_sum.finish()
     return (
-        first_routed[None, :, width:],
-        second_routed[None, :, :width],
-        second_routed[None, :, width:],
-        first_routed[None, :, :width],
+        routed[None, :, width : 2 * width],
+        routed[None, :, 2 * width : 3 * width],
+        routed[None, :, 3 * width :],
+        routed[None, :, :width],
         in_sum.extra[:taps],
         jnp.concatenate([in_part, out_sum.finish()], 1),
     )

time: 203 us -> 199 us (0.980)
  waiting for transfers between devices: 53.5 us -> 49.1 us
  starting transfers between devices: 47.5 us -> 43.8 us
  other arithmetic: 35.8 us -> 39.4 us
    all_to_all x4 -> x3, starting transfers between devices: 18.5 us -> 13.9 us  [spread_rows(): return lax.all_to_all(matrix, 'dp', split_axis=0, concat_axis=0, tiled=True)]
    all_to_all x4 -> x3, waiting for transfers between devices: 4.75 us -> 0.93 us  [spread_rows(): return lax.all_to_all(matrix, 'dp', split_axis=0, concat_axis=0, tiled=True)]
    concatenate x0 -> x1, other arithmetic: none -> 2.12 us  [per_device(): jnp.concatenate([first_slots, by_slot(second_spread, plan)], 1)]
    unnamed x249 -> x261, local copies, waits for them, and re-layouts: 4.87 us -> 4.9 us
  transfers between devices with their start and end apart: 20 -> 19, of which waited for: 10 -> 9; matrix products, arithmetic and copies ran while one was open for 30% -> 32% of each run, Pallas kernels for 0% -> 0%
where the time goes in v5:
time: 199 us; the launch traced here: 197 us
  waiting for transfers between devices  49.1 us (25%)
  starting transfers between devices  43.8 us (22%)
  other arithmetic  39.4 us (20%)
  local copies, waits for them, and re-layouts  32.2 us (16%)
  matrix products  29.8 us (15%)
  between operations  2.91 us (1%)
    ppermute x10, waiting for transfers between devices, swapped(): lax.ppermute(cells, axis, [(i, i ^ 1 << bit) for i in range(lax.axis_size...  33.4 us
    ppermute x10, starting transfers between devices, swapped(): lax.ppermute(cells, axis, [(i, i ^ 1 << bit) for i in range(lax.axis_size...  17.9 us
    all_to_all x3, starting transfers between devices, spread_rows(): return lax.all_to_all(matrix, 'dp', split_axis=0, concat_axis=0, tiled=True)  13.9 us
    dynamic_slice x7, local copies, waits for them, and re-layouts, half_of(): chosen = lax.dynamic_index_in_dim(split, which, dim + 1, keepdims=False)  6.32 us
    ppermute x1, waiting for transfers between devices, returned(): lax.ppermute(parts[step].astype(jnp.bfloat16), axis, [(i, (i + step) % co...  6.03 us
    ppermute x2, starting transfers between devices, extended(): lax.ppermute(tail, axis, [(i, (i + 1) % count) for i in range(ends)])  5.95 us
    dot_general x3, matrix products, times_transposed(): lax.dot_general(left, right, (((1,), (1,)), ((), ())), preferred_element_...  5.59 us
    reduce_sum x6, other arithmetic, tap_sums(): jnp.sum(upstream * padded[tap:tap + length].astype(jnp.float32) * table[:...  5.47 us
  transfers between devices with their start and end apart: 19, of which 9 were waited for; matrix products, arithmetic and copies ran while one was open for 32% of the time, Pallas kernels for 0%

profile of v5, /device:TPU:0, one launch (start us, length us, event | category | flops | bytes accessed | tf_op | source)
XLA Modules:
  0.0 197.2 jit_solution(16918943207835655901)
XLA Ops:
  1.9 3.1 %collective-permute-start = (bf16[128,2048]{1,0:T(8,128)(2,1)S(1)}, bf16[128,2048]{1,0:T(8,128)(2,1)}, u32[]{:S(2)}, u32[]{:S(2)}) collective-permute-start(bf16[128,2048]{1,0:T(8,128)(2,1)S(1)} %pad_maximum_fusion.5), channel_id=1, source_target_pairs={{1,0},{0,1},{3,2},{2,3},{5,4},{4,5},{7,6},{6,7},{9,8},{8,9},{11,10... | collective-permute-start | bytes 1572872 | tf_op jit(solution)/shard_map/ppermute | solution.py:108
  12.4 4.6 %collective-permute-done = bf16[128,2048]{1,0:T(8,128)(2,1)} collective-permute-done((bf16[128,2048]{1,0:T(8,128)(2,1)S(1)}, bf16[128,2048]{1,0:T(8,128)(2,1)}, u32[]{:S(2)}, u32[]{:S(2)}) %collective-permute-start) | collective-permute-done | bytes 524320 | tf_op jit(solution)/shard_map/ppermute | solution.py:108
  24.7 2.4 %convolution_convert_fusion.2 = bf16[16,128,64]{1,2,0:T(8,128)(2,1)S(1)} fusion(bf16[16,256,64]{1,2,0:T(8,128)(2,1)S(1)} %bitcast.343, f32[16,128]{1,0:T(8,128)S(1)} %broadcast_divide_fusion, f32[16,256,128]{2,1,0:T(8,128)} %fusion.222, pred[128,256]{0,1:T(8,128)(4,1)S(1)} %broadcast_compare_fusion), kind=kOutput, calls=%fused_computation.53 | convolution fusion | flops 69863680 | bytes 2924544 | tf_op jit(solution)/shard_map/hqk,hke->hqe/dot_general | solution.py:245
  29.7 3.0 %fusion.148 = f32[128,2048]{1,0:T(8,128)S(1)} fusion(bf16[1024,2048]{1,0:T(8,128)(2,1)} %param.19, f32[128,1024]{1,0:T(8,128)S(1)} %get-tuple-element.182, f32[1024]{0:T(1024)S(1)} %copy-done.85, f32[128]{0:T(128)S(1)} %add_rsqrt_fusion.1, f32[128]{0:T(128)S(1)} %broadcast_multiply_fusion.5), kind=kOutput, calls=%fused_computation.289 | convolution fusion | flops 537395200 | bytes 5772288 | tf_op jit(solution)/shard_map/dot_general | solution.py:253
  34.4 3.6 %collective-permute-start.1 = (bf16[15,1024]{1,0:T(8,128)(2,1)}, bf16[15,1024]{1,0:T(8,128)(2,1)S(1)}, u32[]{:S(2)}, u32[]{:S(2)}) collective-permute-start(bf16[15,1024]{1,0:T(8,128)(2,1)} %get-tuple-element.84), channel_id=1, source_target_pairs={{0,1},{2,3},{4,5},{6,7},{8,9},{10,11},{12,13},{14,15},{16,17},{18,... | collective-permute-start | bytes 92168 | tf_op jit(solution)/shard_map/ppermute | solution.py:21
  40.0 4.1 %collective-permute-done.2 = bf16[15,1024]{1,0:T(8,128)(2,1)S(1)} collective-permute-done((bf16[15,1024]{1,0:T(8,128)(2,1)}, bf16[15,1024]{1,0:T(8,128)(2,1)S(1)}, u32[]{:S(2)}, u32[]{:S(2)}) %collective-permute-start.2) | collective-permute-done | bytes 30752 | tf_op jit(solution)/shard_map/ppermute | solution.py:23
  44.2 4.1 %fusion.215 = (f32[128]{0:T(128)S(1)}, f32[128,1024]{1,0:T(8,128)S(1)}) fusion(f32[128]{0:T(128)} %get-tuple-element.118, bf16[15,1024]{1,0:T(8,128)(2,1)S(1)} %collective-permute-done.2, bf16[128,1024]{1,0:T(8,128)(2,1)S(1)} %multiply_convert_fusion.5, f32[1024]{0:T(1024)S(1)} %bitcast.400, f32[128]{0:T(128)} %get-tuple-element.119, ...), kind=kLoop, calls=%fused_computation.490 | loop fusion | flops 28049280 | bytes 991232 | tf_op jit(solution)/shard_map/reduce_sum | solution.py:31
  70.2 3.0 %collective-permute-start.6 = (bf16[256,1024]{1,0:T(8,128)(2,1)}, bf16[256,1024]{1,0:T(8,128)(2,1)}, u32[]{:S(2)}, u32[]{:S(2)}) collective-permute-start(bf16[256,1024]{1,0:T(8,128)(2,1)} %bitcast.113), channel_id=1, source_target_pairs={{0,1},{1,0},{2,3},{3,2},{4,5},{5,4},{6,7},{7,6},{8,9},{9,8},{10,11... | collective-permute-start | bytes 1572872 | tf_op jit(solution)/shard_map/ppermute | solution.py:147
  73.7 3.9 %multiply_convert_fusion.3 = (bf16[128,1024]{1,0:T(8,128)(2,1)S(1)}, f32[128,1024]{1,0:T(8,128)S(1)}) fusion(f32[128,2048]{1,0:T(8,128)S(1)} %copy-done.4, f32[128]{0:T(128)S(1)} %copy-done.100, f32[158,1024]{1,0:T(8,128)S(1)} %maximum_convert_fusion, f32[1024]{0:T(1024)S(1)} %bitcast.405, f32[128]{0:T(128)S(1)} %copy-done.102, f32[1024]{0:T(1024)S(1)} %bitcast.381, ...), kind=kLoop, calls=%fused_computation.274 | loop fusion | flops 12713984 | bytes 17706496 | tf_op jit(solution)/shard_map/convert.33
  77.8 2.4 %fusion.211 = (f32[128]{0:T(128)S(1)}, f32[128]{0:T(128)S(1)}, f32[128,1024]{1,0:T(8,128)S(1)}) fusion(f32[128]{0:T(128)} %copy-done.127, f32[128,1024]{1,0:T(8,128)S(1)} %get-tuple-element.182, f32[128]{0:T(128)} %copy-done.125, f32[1024]{0:T(1024)S(1)} %copy-done.86, bf16[1024,2048]{1,0:T(8,128)(2,1)S(1)} %copy-done.2, ...), kind=kOutput, calls=%fused_computation.487 | convolution fusion | flops 538705664 | bytes 5773312 | tf_op jit(solution)/shard_map/dot_general | solution.py:86
  81.6 2.4 %fusion.147 = f32[16,256,64]{1,2,0:T(8,128)S(1)} fusion(bf16[16,128,64]{1,2,0:T(8,128)(2,1)S(1)} %bitcast.351, f32[16,128]{1,0:T(8,128)S(1)} %copy-done.71, f32[16,256,128]{2,1,0:T(8,128)} %fusion.222, pred[128,256]{0,1:T(8,128)(4,1)} %copy-done.72), kind=kOutput, calls=%fused_computation.286 | convolution fusion | flops 69732608 | bytes 3448832 | tf_op jit(solution)/shard_map/hqk,hqe->hke/dot_general | solution.py:304
  88.5 3.2 %multiply_convert_fusion = bf16[16,128,256]{1,2,0:T(8,128)(2,1)S(1)} fusion(f32[16,128,256]{1,2,0:T(8,128)} %get-tuple-element.180, f32[16,128]{1,0:T(8,128)S(1)} %copy-done.71, bf16[16,128,64]{1,2,0:T(8,128)(2,1)S(1)} %bitcast.352, bf16[16,256,64]{1,2,0:T(8,128)(2,1)S(1)} %bitcast.344), kind=kOutput, calls=%fused_computation.8 | convolution fusion | flops 137365760 | bytes 3940352 | tf_op jit(solution)/shard_map/sub | solution.py:290
  91.7 2.6 %bitcast_add_fusion = f32[256,1024]{1,0:T(8,128)} fusion(f32[8,1,32,1024]{3,2,1,0:T(8,128)} %constant_dynamic-slice_fusion.7, bf16[256,1024]{1,0:T(8,128)(2,1)} %collective-permute-done.6), kind=kLoop, calls=%fused_computation.65 | loop fusion | flops 524288 | bytes 2621440 | tf_op jit(solution)/shard_map/add | solution.py:193
  103.7 5.0 %all-to-all-start = ((bf16[16,8,2048]{2,1,0:T(8,128)(2,1)}), bf16[16,8,2048]{2,1,0:T(8,128)(2,1)S(1)}, u32[]{:S(2)}, u32[]{:S(2)}) async-start(bf16[16,8,2048]{2,1,0:T(8,128)(2,1)} %pad_maximum_fusion.6), calls=%async_computation | async-start | bytes 1048576 | tf_op jit(solution)/shard_map/all_to_all | solution.py:127
  110.7 6.0 %collective-permute-done.7 = bf16[128,2048]{1,0:T(8,128)(2,1)} collective-permute-done((bf16[128,2048]{1,0:T(8,128)(2,1)}, bf16[128,2048]{1,0:T(8,128)(2,1)}, u32[]{:S(2)}, u32[]{:S(2)}) %collective-permute-start.7) | collective-permute-done | bytes 524320 | tf_op jit(solution)/shard_map/ppermute | solution.py:117
  123.7 4.2 %all-to-all-start.1 = ((bf16[16,8,2048]{2,1,0:T(8,128)(2,1)}), bf16[16,8,2048]{2,1,0:T(8,128)(2,1)}, u32[]{:S(2)}, u32[]{:S(2)}) async-start(bf16[16,8,2048]{2,1,0:T(8,128)(2,1)} %bitcast.168), calls=%async_computation.1 | async-start | bytes 1048576 | tf_op jit(solution)/shard_map/all_to_all | solution.py:127
  137.5 4.6 %collective-permute-done.14 = bf16[64,1024]{1,0:T(8,128)(2,1)S(1)} collective-permute-done((bf16[64,1024]{1,0:T(8,128)(2,1)S(1)}, bf16[64,1024]{1,0:T(8,128)(2,1)S(1)}, u32[]{:S(2)}, u32[]{:S(2)}) %collective-permute-start.14) | collective-permute-done | bytes 131104 | tf_op jit(solution)/shard_map/ppermute | solution.py:147
  142.2 4.0 %collective-permute-done.10 = bf16[288,1024]{1,0:T(8,128)(2,1)} collective-permute-done((bf16[288,1024]{1,0:T(8,128)(2,1)}, bf16[288,1024]{1,0:T(8,128)(2,1)}, u32[]{:S(2)}, u32[]{:S(2)}) %collective-permute-start.10) | collective-permute-done | bytes 589856 | tf_op jit(solution)/shard_map/ppermute | solution.py:147
  147.6 2.9 %gather_fusion.1 = bf16[16,8,2048]{2,1,0:T(8,128)(2,1)} fusion(bf16[16,8,2048]{2,1,0:T(8,128)(2,1)} %bitcast.170, s32[1024]{0:T(1024)} %pad_clamp_fusion), kind=kCustom, calls=%fused_computation.1 | custom fusion | bytes 1048640 | tf_op jit(solution)/shard_map/jit(_take)/gather | solution.py:132
  155.1 4.6 %all-to-all-start.2 = ((bf16[16,8,4096]{2,1,0:T(8,128)(2,1)}), bf16[16,8,4096]{2,1,0:T(8,128)(2,1)S(1)}, u32[]{:S(2)}, u32[]{:S(2)}) async-start(bf16[16,8,4096]{2,1,0:T(8,128)(2,1)} %pad_maximum_fusion.3), calls=%async_computation.2 | async-start | bytes 2097152 | tf_op jit(solution)/shard_map/all_to_all | solution.py:127
  164.0 2.4 %collective-permute-start.15 = (bf16[32,1024]{1,0:T(8,128)(2,1)S(1)}, bf16[32,1024]{1,0:T(8,128)(2,1)S(1)}, u32[]{:S(2)}, u32[]{:S(2)}) collective-permute-start(bf16[32,1024]{1,0:T(8,128)(2,1)S(1)} %fusion.195), channel_id=1, source_target_pairs={{0,16},{2,18},{4,20},{6,22},{8,24},{10,26},{12,28},{14,30},{16,0},... | collective-permute-start | bytes 196616 | tf_op jit(solution)/shard_map/ppermute | solution.py:147
  166.5 17.3 %collective-permute-done.12 = bf16[96,1024]{1,0:T(8,128)(2,1)S(1)} collective-permute-done((bf16[96,1024]{1,0:T(8,128)(2,1)S(1)}, bf16[96,1024]{1,0:T(8,128)(2,1)S(1)}, u32[]{:S(2)}, u32[]{:S(2)}) %collective-permute-start.12) | collective-permute-done | bytes 196640 | tf_op jit(solution)/shard_map/ppermute | solution.py:147
  183.9 3.3 %collective-permute-start.13 = (bf16[64,1024]{1,0:T(8,128)(2,1)S(1)}, bf16[64,1024]{1,0:T(8,128)(2,1)S(1)}, u32[]{:S(2)}, u32[]{:S(2)}) collective-permute-start(bf16[64,1024]{1,0:T(8,128)(2,1)S(1)} %pad_maximum_fusion.12), channel_id=1, source_target_pairs={{0,16},{2,18},{4,20},{6,22},{8,24},{10,26},{12,28},{14,30},{16,0},... | collective-permute-start | bytes 393224 | tf_op jit(solution)/shard_map/ppermute | solution.py:147
  187.2 5.3 %collective-permute-done.15 = bf16[32,1024]{1,0:T(8,128)(2,1)S(1)} collective-permute-done((bf16[32,1024]{1,0:T(8,128)(2,1)S(1)}, bf16[32,1024]{1,0:T(8,128)(2,1)S(1)}, u32[]{:S(2)}, u32[]{:S(2)}) %collective-permute-start.15) | collective-permute-done | bytes 65568 | tf_op jit(solution)/shard_map/ppermute | solution.py:147
  (391 shorter events, 92.2 us)
Async XLA Ops:
  0.6 47.9 %copy-start = (bf16[1024,1024]{1,0:T(8,128)(2,1)S(1)}, bf16[1024,1024]{1,0:T(8,128)(2,1)}, u32[]{:S(2)}) copy-start(bf16[1024,1024]{1,0:T(8,128)(2,1)} %param.21) | copy-start | bytes 6291460
  1.9 15.1 %collective-permute-start = (bf16[128,2048]{1,0:T(8,128)(2,1)S(1)}, bf16[128,2048]{1,0:T(8,128)(2,1)}, u32[]{:S(2)}, u32[]{:S(2)}) collective-permute-start(bf16[128,2048]{1,0:T(8,128)(2,1)S(1)} %pad_maximum_fusion.5), channel_id=1, source_target_pairs={{1,0},{0,1},{3,2},{2,3},{5,4},{4,5},{7,6},{6,7},{9,8},{8,9},{11,10... | collective-permute-start | bytes 1572872 | tf_op jit(solution)/shard_map/ppermute | solution.py:108
  10.5 33.6 %copy-start.27 = (f32[1,1024]{1,0:T(1,128)}, f32[1,1024]{1,0:T(1,128)S(1)}, u32[]{:S(2)}) copy-start(f32[1,1024]{1,0:T(1,128)S(1)} %get-tuple-element.109) | copy-start | bytes 12292
  10.5 33.6 %copy-start.29 = (f32[1,1024]{1,0:T(1,128)}, f32[1,1024]{1,0:T(1,128)S(1)}, u32[]{:S(2)}) copy-start(f32[1,1024]{1,0:T(1,128)S(1)} %get-tuple-element.110) | copy-start | bytes 12292
  10.5 33.6 %copy-start.31 = (f32[1,1024]{1,0:T(1,128)}, f32[1,1024]{1,0:T(1,128)S(1)}, u32[]{:S(2)}) copy-start(f32[1,1024]{1,0:T(1,128)S(1)} %get-tuple-element.111) | copy-start | bytes 12292
  10.5 33.6 %copy-start.33 = (f32[1,1024]{1,0:T(1,128)}, f32[1,1024]{1,0:T(1,128)S(1)}, u32[]{:S(2)}) copy-start(f32[1,1024]{1,0:T(1,128)S(1)} %get-tuple-element.112) | copy-start | bytes 12292
  34.4 5.5 %collective-permute-start.1 = (bf16[15,1024]{1,0:T(8,128)(2,1)}, bf16[15,1024]{1,0:T(8,128)(2,1)S(1)}, u32[]{:S(2)}, u32[]{:S(2)}) collective-permute-start(bf16[15,1024]{1,0:T(8,128)(2,1)} %get-tuple-element.84), channel_id=1, source_target_pairs={{0,1},{2,3},{4,5},{6,7},{8,9},{10,11},{12,13},{14,15},{16,17},{18,... | collective-permute-start | bytes 92168 | tf_op jit(solution)/shard_map/ppermute | solution.py:21
  38.1 6.0 %collective-permute-start.2 = (bf16[15,1024]{1,0:T(8,128)(2,1)}, bf16[15,1024]{1,0:T(8,128)(2,1)S(1)}, u32[]{:S(2)}, u32[]{:S(2)}) collective-permute-start(bf16[15,1024]{1,0:T(8,128)(2,1)} %get-tuple-element.85), channel_id=1, source_target_pairs={{1,0},{3,2},{5,4},{7,6},{9,8},{11,10},{13,12},{15,14},{17,16},{19,... | collective-permute-start | bytes 92168 | tf_op jit(solution)/shard_map/ppermute | solution.py:23
  54.5 10.2 %collective-permute-start.4 = (bf16[15,1024]{1,0:T(8,128)(2,1)}, bf16[15,1024]{1,0:T(8,128)(2,1)}, u32[]{:S(2)}, u32[]{:S(2)}) collective-permute-start(bf16[15,1024]{1,0:T(8,128)(2,1)} %get-tuple-element.80), channel_id=1, source_target_pairs={{0,1},{2,3},{4,5},{6,7},{8,9},{10,11},{12,13},{14,15},{16,17},{18,... | collective-permute-start | bytes 92168 | tf_op jit(solution)/shard_map/ppermute | solution.py:21
  56.8 7.9 %collective-permute-start.5 = (bf16[15,1024]{1,0:T(8,128)(2,1)}, bf16[15,1024]{1,0:T(8,128)(2,1)}, u32[]{:S(2)}, u32[]{:S(2)}) collective-permute-start(bf16[15,1024]{1,0:T(8,128)(2,1)} %get-tuple-element.81), channel_id=1, source_target_pairs={{1,0},{3,2},{5,4},{7,6},{9,8},{11,10},{13,12},{15,14},{17,16},{19,... | collective-permute-start | bytes 92168 | tf_op jit(solution)/shard_map/ppermute | solution.py:23
  60.8 4.8 %collective-permute-start.3 = (bf16[512,1024]{1,0:T(8,128)(2,1)}, bf16[512,1024]{1,0:T(8,128)(2,1)S(1)}, u32[]{:S(2)}, u32[]{:S(2)}) collective-permute-start(bf16[512,1024]{1,0:T(8,128)(2,1)} %convolution_convert_fusion.1), channel_id=1, source_target_pairs={{0,2},{2,0},{4,6},{6,4},{8,10},{10,8},{12,14},{14,12},{16,18},{18,... | collective-permute-start | bytes 3145736 | tf_op jit(solution)/shard_map/ppermute | solution.py:147
  70.2 21.4 %collective-permute-start.6 = (bf16[256,1024]{1,0:T(8,128)(2,1)}, bf16[256,1024]{1,0:T(8,128)(2,1)}, u32[]{:S(2)}, u32[]{:S(2)}) collective-permute-start(bf16[256,1024]{1,0:T(8,128)(2,1)} %bitcast.113), channel_id=1, source_target_pairs={{0,1},{1,0},{2,3},{3,2},{4,5},{5,4},{6,7},{7,6},{8,9},{9,8},{10,11... | collective-permute-start | bytes 1572872 | tf_op jit(solution)/shard_map/ppermute | solution.py:147
  85.8 32.8 %collective-permute-start.8 = (bf16[544,1024]{1,0:T(8,128)(2,1)}, bf16[544,1024]{1,0:T(8,128)(2,1)}, u32[]{:S(2)}, u32[]{:S(2)}) collective-permute-start(bf16[544,1024]{1,0:T(8,128)(2,1)} %pad_maximum_fusion), channel_id=1, source_target_pairs={{0,2},{2,0},{4,6},{6,4},{8,10},{10,8},{12,14},{14,12},{16,18},{18,... | collective-permute-start | bytes 3342344 | tf_op jit(solution)/shard_map/ppermute | solution.py:147
  98.6 11.1 %collective-permute-start.9 = (bf16[128,1024]{1,0:T(8,128)(2,1)}, bf16[128,1024]{1,0:T(8,128)(2,1)S(1)}, u32[]{:S(2)}, u32[]{:S(2)}) collective-permute-start(bf16[128,1024]{1,0:T(8,128)(2,1)} %bitcast.163), channel_id=1, source_target_pairs={{0,4},{2,6},{4,0},{6,2},{8,12},{10,14},{12,8},{14,10},{16,20},{18,... | collective-permute-start | bytes 786440 | tf_op jit(solution)/shard_map/ppermute | solution.py:147
  102.5 14.1 %collective-permute-start.7 = (bf16[128,2048]{1,0:T(8,128)(2,1)}, bf16[128,2048]{1,0:T(8,128)(2,1)}, u32[]{:S(2)}, u32[]{:S(2)}) collective-permute-start(bf16[128,2048]{1,0:T(8,128)(2,1)} %fusion.13), channel_id=1, source_target_pairs={{0,1},{1,0},{2,3},{3,2},{4,5},{5,4},{6,7},{7,6},{8,9},{9,8},{10,11... | collective-permute-start | bytes 1572872 | tf_op jit(solution)/shard_map/ppermute | solution.py:117
  103.7 19.3 %all-to-all-start = ((bf16[16,8,2048]{2,1,0:T(8,128)(2,1)}), bf16[16,8,2048]{2,1,0:T(8,128)(2,1)S(1)}, u32[]{:S(2)}, u32[]{:S(2)}) async-start(bf16[16,8,2048]{2,1,0:T(8,128)(2,1)} %pad_maximum_fusion.6), calls=%async_computation | async-start | bytes 1048576 | tf_op jit(solution)/shard_map/all_to_all | solution.py:127
  123.7 23.9 %all-to-all-start.1 = ((bf16[16,8,2048]{2,1,0:T(8,128)(2,1)}), bf16[16,8,2048]{2,1,0:T(8,128)(2,1)}, u32[]{:S(2)}, u32[]{:S(2)}) async-start(bf16[16,8,2048]{2,1,0:T(8,128)(2,1)} %bitcast.168), calls=%async_computation.1 | async-start | bytes 1048576 | tf_op jit(solution)/shard_map/all_to_all | solution.py:127
  130.3 15.9 %collective-permute-start.10 = (bf16[288,1024]{1,0:T(8,128)(2,1)}, bf16[288,1024]{1,0:T(8,128)(2,1)}, u32[]{:S(2)}, u32[]{:S(2)}) collective-permute-start(bf16[288,1024]{1,0:T(8,128)(2,1)} %pad_maximum_fusion.4), channel_id=1, source_target_pairs={{0,1},{1,0},{2,3},{3,2},{4,5},{5,4},{6,7},{7,6},{8,9},{9,8},{10,11... | collective-permute-start | bytes 1769480 | tf_op jit(solution)/shard_map/ppermute | solution.py:147
  133.0 9.1 %collective-permute-start.14 = (bf16[64,1024]{1,0:T(8,128)(2,1)S(1)}, bf16[64,1024]{1,0:T(8,128)(2,1)S(1)}, u32[]{:S(2)}, u32[]{:S(2)}) collective-permute-start(bf16[64,1024]{1,0:T(8,128)(2,1)S(1)} %bitcast.379), channel_id=1, source_target_pairs={{0,8},{2,10},{4,12},{6,14},{8,0},{10,2},{12,4},{14,6},{16,24},{18,... | collective-permute-start | bytes 393224 | tf_op jit(solution)/shard_map/ppermute | solution.py:147
  151.3 9.5 %collective-permute-start.11 = (bf16[160,1024]{1,0:T(8,128)(2,1)}, bf16[160,1024]{1,0:T(8,128)(2,1)}, u32[]{:S(2)}, u32[]{:S(2)}) collective-permute-start(bf16[160,1024]{1,0:T(8,128)(2,1)} %pad_maximum_fusion.7), channel_id=1, source_target_pairs={{0,4},{2,6},{4,0},{6,2},{8,12},{10,14},{12,8},{14,10},{16,20},{18,... | collective-permute-start | bytes 983048 | tf_op jit(solution)/shard_map/ppermute | solution.py:147
  155.1 41.1 %all-to-all-start.2 = ((bf16[16,8,4096]{2,1,0:T(8,128)(2,1)}), bf16[16,8,4096]{2,1,0:T(8,128)(2,1)S(1)}, u32[]{:S(2)}, u32[]{:S(2)}) async-start(bf16[16,8,4096]{2,1,0:T(8,128)(2,1)} %pad_maximum_fusion.3), calls=%async_computation.2 | async-start | bytes 2097152 | tf_op jit(solution)/shard_map/all_to_all | solution.py:127
  162.1 21.7 %collective-permute-start.12 = (bf16[96,1024]{1,0:T(8,128)(2,1)S(1)}, bf16[96,1024]{1,0:T(8,128)(2,1)S(1)}, u32[]{:S(2)}, u32[]{:S(2)}) collective-permute-start(bf16[96,1024]{1,0:T(8,128)(2,1)S(1)} %pad_maximum_fusion.11), channel_id=1, source_target_pairs={{0,8},{2,10},{4,12},{6,14},{8,0},{10,2},{12,4},{14,6},{16,24},{18,... | collective-permute-start | bytes 589832 | tf_op jit(solution)/shard_map/ppermute | solution.py:147
  164.0 28.5 %collective-permute-start.15 = (bf16[32,1024]{1,0:T(8,128)(2,1)S(1)}, bf16[32,1024]{1,0:T(8,128)(2,1)S(1)}, u32[]{:S(2)}, u32[]{:S(2)}) collective-permute-start(bf16[32,1024]{1,0:T(8,128)(2,1)S(1)} %fusion.195), channel_id=1, source_target_pairs={{0,16},{2,18},{4,20},{6,22},{8,24},{10,26},{12,28},{14,30},{16,0},... | collective-permute-start | bytes 196616 | tf_op jit(solution)/shard_map/ppermute | solution.py:147
  183.9 10.8 %collective-permute-start.13 = (bf16[64,1024]{1,0:T(8,128)(2,1)S(1)}, bf16[64,1024]{1,0:T(8,128)(2,1)S(1)}, u32[]{:S(2)}, u32[]{:S(2)}) collective-permute-start(bf16[64,1024]{1,0:T(8,128)(2,1)S(1)} %pad_maximum_fusion.12), channel_id=1, source_target_pairs={{0,16},{2,18},{4,20},{6,22},{8,24},{10,26},{12,28},{14,30},{16,0},... | collective-permute-start | bytes 393224 | tf_op jit(solution)/shard_map/ppermute | solution.py:147
  (125 other events, 984.8 us)
